TPU v7x, 128 devices: a whole 4x4x4 slice. The times are simulated.
128 devices in a mesh: dp: 32 (over x, z, core), rep: 4 (over y).
Axes of the slice: x: 4, y: 4, z: 4, core: 2. Of those that a mesh axis runs over, the one named last changes fastest.
Arguments:
- cross_in: bfloat16 [65536, 3456], P(('dp', 'rep')), may hold values from -24 to 24
- cotangent: bfloat16 [65536, 3456], P(('dp', 'rep')), may hold values from -24 to 24
- weight_down: bfloat16 [3456, 512], replicated, may hold values from -0.109375 to 0.109375
- weight_up: bfloat16 [512, 3456], replicated, may hold values from -0.25 to 0.25
- cross_bias: float32 [3456], replicated, may hold values from -3 to 3
- row_place: int32 [65536, 26], P(('dp', 'rep')), may hold values from 0 to 66559, as said below
- frequent_table: float32 [1024, 128], replicated, may hold values from -0.6 to 0.6
- frequent_accum: float32 [1024], replicated, may hold values from 416 to 106496
- shard_table: float32 [65536, 128], P('dp'), may hold values from -0.6 to 0.6
- shard_accum: float32 [65536], P('dp'), may hold values from 0.01 to 1
Outputs:
- new_frequent: float32 [1024, 128], replicated
- new_frequent_accum: float32 [1024], replicated
- new_shard: float32 [65536, 128], P('dp')
- new_shard_accum: float32 [65536], P('dp')
- grad_up: float32 [512, 3456], P(('dp', 'rep'))
- grad_down: float32 [3456, 512], P(('dp', 'rep'))
- grad_bias: float32 [3456], P(('dp', 'rep'))
Inputs may be any that keep to these rules, and one draw needn't show every extreme that they name: `row_place`: within the rows of one device (aligned blocks of 512 samples), at most 208 entries name rows of any one owner, and in every block some owner is named by exactly 208 entries; every owner is named at least once in every block.
All inputs are finite; a program needn't handle non-finite values.
Results may differ from a plain program's by a relative error of at most 0.0013.
The roundings to bfloat16 on the way count: a program that leaves them out, or rounds other values in their place, can miss the bound.
Values sent between devices are 32-bit elements; how exact they have to be, the bound alone decides.
A program may use at most 192 MiB of HBM per device.

v0:
```python
import jax
import jax.numpy as jnp
from jax import lax
from jax.sharding import PartitionSpec as P

learn_rate = 0.05
eps_ada = 1e-08


def row_adagrad(table, accum, grad):
    accum_new = accum + jnp.mean(grad * grad, axis=1)
    return (table - learn_rate * grad / (jnp.sqrt(accum_new)[:, None] + eps_ada), accum_new)


def body(
    cross_in,
    cotangent,
    weight_down,
    weight_up,
    cross_bias,
    row_place,
    frequent_table,
    frequent_accum,
    shard_table,
    shard_accum,
):
    emb_width = frequent_table.shape[1]
    num_tables = row_place.shape[1]
    local_rows = cross_in.shape[0]
    f_count = frequent_table.shape[0]
    owned_rows = shard_table.shape[0]
    hidden = jnp.dot(cross_in, weight_down, preferred_element_type=jnp.float32).astype(jnp.bfloat16)
    scaled = jnp.dot(hidden, weight_up, preferred_element_type=jnp.float32) + cross_bias
    cot_wide = cotangent.astype(jnp.float32)
    inner = cot_wide * cross_in.astype(jnp.float32)
    inner_half = inner.astype(jnp.bfloat16)
    back_low = lax.dot_general(
        inner_half, weight_up, (((1,), (1,)), ((), ())), preferred_element_type=jnp.float32
    ).astype(jnp.bfloat16)
    back_in = cot_wide * (scaled + 1.0) + lax.dot_general(
        back_low, weight_down, (((1,), (1,)), ((), ())), preferred_element_type=jnp.float32
    )
    local_up = lax.dot_general(
        hidden, inner_half, (((0,), (0,)), ((), ())), preferred_element_type=jnp.float32
    )
    local_down = lax.dot_general(
        cross_in, back_low, (((0,), (0,)), ((), ())), preferred_element_type=jnp.float32
    )
    local_bias = jnp.sum(inner, axis=0)
    grad_up, grad_down, grad_bias = (
        lax.psum_scatter(local_up, ("dp", "rep"), scatter_dimension=0, tiled=True),
        lax.psum_scatter(local_down, ("dp", "rep"), scatter_dimension=0, tiled=True),
        lax.psum_scatter(local_bias, ("dp", "rep"), scatter_dimension=0, tiled=True),
    )
    values = back_in[:, emb_width:].reshape(local_rows * num_tables, emb_width)
    places = row_place.reshape(-1)
    is_frequent = places < f_count
    freq_grad = jax.ops.segment_sum(values, jnp.where(is_frequent, places, f_count), f_count + 1)[
        :f_count
    ]
    shards = lax.axis_size("dp")
    capacity = local_rows * num_tables // (2 * shards)
    owners = jnp.where(is_frequent, shards, (places - f_count) // owned_rows)
    owner_row = jnp.where(is_frequent, 0, (places - f_count) % owned_rows)
    sorted_order = jnp.argsort(owners, stable=True)
    sorted_owner = owners[sorted_order]
    counts = jnp.sum((owners[:, None] == jnp.arange(shards + 1)[None, :]).astype(jnp.int32), axis=0)
    starts = jnp.cumsum(counts) - counts
    slot_pos = jnp.arange(owners.shape[0]) - starts[sorted_owner]
    target = jnp.where(sorted_owner < shards, sorted_owner * capacity + slot_pos, shards * capacity)
    bucket = (
        jnp.zeros((shards * capacity + 1, emb_width), jnp.float32)
        .at[target]
        .set(values[sorted_order])
    )
    bucket = bucket[: shards * capacity].reshape(shards, capacity, emb_width)
    bucket_rows = (
        jnp.zeros((shards * capacity + 1,), jnp.int32).at[target].set(owner_row[sorted_order])
    )
    bucket_rows = bucket_rows[: shards * capacity].reshape(shards, capacity)
    arrived, arrived_rows = (
        lax.all_to_all(bucket, "dp", split_axis=0, concat_axis=0, tiled=True),
        lax.all_to_all(bucket_rows, "dp", split_axis=0, concat_axis=0, tiled=True),
    )
    shard_grad = jax.ops.segment_sum(
        arrived.reshape(-1, emb_width), arrived_rows.reshape(-1), owned_rows
    )
    shard_grad = lax.psum(shard_grad, "rep")
    new_shard, new_shard_accum = row_adagrad(shard_table, shard_accum, shard_grad)
    freq_total = lax.psum(freq_grad, ("dp", "rep"))
    new_frequent, new_frequent_accum = row_adagrad(frequent_table, frequent_accum, freq_total)
    return (
        new_frequent,
        new_frequent_accum,
        new_shard,
        new_shard_accum,
        grad_up,
        grad_down,
        grad_bias,
    )


def solution(mesh):
    in_specs = (
        P(("dp", "rep"), None),
        P(("dp", "rep"), None),
        P(),
        P(),
        P(),
        P(("dp", "rep"), None),
        P(),
        P(),
        P("dp", None),
        P("dp"),
    )
    out_specs = (
        P(),
        P(),
        P("dp", None),
        P("dp"),
        P(("dp", "rep"), None),
        P(("dp", "rep"), None),
        P(("dp", "rep")),
    )
    return jax.shard_map(body, mesh=mesh, in_specs=in_specs, out_specs=out_specs, check_vma=False)
```

profile of v0, /device:TPU:1, one launch (start us, length us, event | category | flops | bytes accessed | tf_op | source)
XLA Modules:
  0.0 876.6 jit_solution(13880018079292635862)
XLA Ops:
  22.4 9.1 %sort.17 = (s32[13312]{0:T(1024)}, s32[13312]{0:T(1024)}) sort(s32[13312]{0:T(1024)} %copy-done.2, s32[13312]{0:T(1024)} %iota.12), dimensions={0}, to_apply=%region_3.0 | sort | flops 186368 | bytes 212992 | tf_op jit(solution)/shard_map/jit(argsort)/sort | solution.py:65
  32.9 121.2 %gather_fusion = s32[13312]{0:T(1024)} fusion(s32[13312]{0:T(1024)} %copy-done.2, s32[13312]{0:T(1024)} %fusion.19), kind=kCustom, calls=%fused_computation | custom fusion | bytes 159744 | tf_op jit(solution)/shard_map/gather | solution.py:66
  154.1 5.3 compare_select_fusion.3
  159.4 4.2 compare_reduce_fusion.25
  163.7 16.6 %select_select_fusion = s32[13312]{0:T(1024)S(1)} fusion(pred[13312]{0:T(1024)(128)(4,1)S(1)} %get-tuple-element.62, pred[13312]{0:T(1024)(128)(4,1)S(1)} %get-tuple-element.61, pred[13312]{0:T(1024)(128)(4,1)S(1)} %get-tuple-element.60, pred[13312]{0:T(1024)(128)(4,1)S(1)} %get-tuple-element.59, pred[13312]{0:T(1024)(128)(4,1)S(1)} %get-tuple-element.58, ...), kind=kLoop, calls=%fused_computation.77 | loop fusion | flops 346112 | bytes 452712 | tf_op jit(solution)/shard_map/gather | solution.py:69
  181.8 120.7 %gather_fusion.1 = s32[13312]{0:T(1024)} fusion(s32[13312]{0:T(1024)} %get-tuple-element.72, s32[13312]{0:T(1024)} %fusion.19), kind=kCustom, calls=%fused_computation.1 | custom fusion | bytes 159744 | tf_op jit(solution)/shard_map/gather | solution.py:78
  302.6 49.8 %scatter_custom_fusion.1 = s32[6657]{0:T(1024)} fusion(s32[13312]{0:T(1024)} %bitcast.62, s32[13312]{0:T(1024)} %gather_fusion.1, s32[]{:T(128)} %constant.29.clone.1), kind=kCustom, calls=%fused_computation.83 | custom fusion | bytes 27140 | tf_op jit(solution)/shard_map/scatter | solution.py:78
  353.9 9.8 %all-to-all-start = ((s32[32,1,208]{2,1,0:T(1,128)}), s32[32,1,208]{2,1,0:T(1,128)}, u32[]{:S(2)}, u32[]{:S(2)}) async-start(s32[32,1,208]{2,1,0:T(1,128)} %all_to_all.9), calls=%async_computation | async-start | bytes 65536 | tf_op jit(solution)/shard_map/all_to_all | solution.py:83
  363.7 2.6 convert_element_type.18
  370.0 2.1 fusion.10
  374.3 2.1 fusion.27
  376.4 3.3 slice_add_fusion
  379.8 7.8 reshape.231
  387.5 108.8 %scatter_custom_fusion.2 = f32[6657,128]{1,0:T(8,128)S(1)} fusion(s32[13312]{0:T(1024)} %bitcast.63, f32[13312,128]{1,0:T(8,128)} %reshape.231, s32[13312]{0:T(1024)} %fusion.19, f32[]{:T(128)} %constant.21.clone.1), kind=kCustom, calls=%fused_computation.12 | custom fusion | bytes 3408896 | tf_op jit(solution)/shard_map/scatter | solution.py:74
  498.3 7.7 all-to-all-start.1
  511.0 72.4 %scatter_custom_fusion = f32[1025,128]{1,0:T(8,128)} fusion(s32[13312]{0:T(1024)} %bitcast.64, f32[13312,128]{1,0:T(8,128)} %reshape.231, f32[]{:T(128)} %constant.21.clone.1), kind=kCustom, calls=%fused_computation.33 | custom fusion | flops 1703936 | bytes 525312 | tf_op jit(solution)/shard_map/scatter-add | solution.py:58
  588.2 42.0 %scatter_custom_fusion.3 = f32[2048,128]{1,0:T(8,128)} fusion(s32[6656]{0:T(1024)} %reshape.253, f32[6656,128]{1,0:T(8,128)} %bitcast.40, f32[]{:T(128)} %constant.21.clone.1), kind=kCustom, calls=%fused_computation.26 | custom fusion | flops 851968 | bytes 1049088 | tf_op jit(solution)/shard_map/scatter-add | solution.py:85
  630.3 6.2 convolution_bitcast_fusion
  636.5 5.1 fusion.6
  641.6 4.2 fusion.3
  645.8 66.7 %all-reduce.2 = f32[3456]{0:T(1024)} all-reduce(f32[3456]{0:T(1024)S(1)} %fusion.3), channel_id=4, replica_groups=mesh['dp'=32,'rep'=4] {'dp','rep'}, use_global_device_ids=true, to_apply=%region_14.15.clone | all-reduce | flops 3456 | bytes 27648
  716.6 3.0 divide_subtract_fusion
  719.6 140.1 %all-reduce.9.cloned.1.call-done = (f32[1024,128]{1,0:T(8,128)}, f32[512,3456]{1,0:T(8,128)}, f32[3456,512]{0,1:T(8,128)}) async-done(((f32[1024,128]{1,0:T(8,128)}, f32[512,3456]{1,0:T(8,128)}, f32[3456,512]{0,1:T(8,128)}), (f32[1024,128]{1,0:T(8,128)}, f32[512,3456]{1,0:T(8,128)}, f32[3456,512]{0,1:T(8,128)})) %all-reduce.9.cloned.1.call-update) | async-done | bytes 14680080 | tf_op jit(solution)/shard_map/psum | solution.py:90
  865.8 2.2 divide_subtract_fusion.1
  (69 shorter events, 49.2 us)
Async XLA Ops:
  7.2 362.8 %copy-start = (bf16[512,3456]{1,0:T(8,128)(2,1)S(1)}, bf16[512,3456]{1,0:T(8,128)(2,1)}, u32[]{:S(2)}) copy-start(bf16[512,3456]{1,0:T(8,128)(2,1)} %param.13) | copy-start | bytes 10616836
  16.4 0.6 copy-start.2
  353.9 144.5 %all-to-all-start = ((s32[32,1,208]{2,1,0:T(1,128)}), s32[32,1,208]{2,1,0:T(1,128)}, u32[]{:S(2)}, u32[]{:S(2)}) async-start(s32[32,1,208]{2,1,0:T(1,128)} %all_to_all.9), calls=%async_computation | async-start | bytes 65536 | tf_op jit(solution)/shard_map/all_to_all | solution.py:83
  363.7 3.1 copy-start.3
  363.7 4.1 copy-start.7
  367.9 2.1 copy-start.5
  369.9 2.1 copy-start.9
  372.1 4.3 copy-start.11
  372.1 2.2 copy-start.8
  374.3 2.1 copy-start.12
  498.3 131.9 %copy-start.4 = (bf16[512,3456]{1,0:T(8,128)(2,1)S(1)}, bf16[512,3456]{1,0:T(8,128)(2,1)}, u32[]{:S(2)}) copy-start(bf16[512,3456]{1,0:T(8,128)(2,1)} %param.10) | copy-start | bytes 10616836
  498.3 89.8 %all-to-all-start.1 = ((f32[32,208,128]{2,1,0:T(8,128)}), f32[32,208,128]{2,1,0:T(8,128)}, u32[]{:S(2)}, u32[]{:S(2)}) async-start(f32[32,208,128]{2,1,0:T(8,128)} %bitcast.56), calls=%async_computation.1 | async-start | bytes 6815744 | tf_op jit(solution)/shard_map/all_to_all | solution.py:82
  506.0 207.7 %all-reduce.7.cloned.1.call-start = ((), (), s32[]{:S(2)}) async-start(), calls=%async_computation.2 | async-start | bytes 2097152 | tf_op jit(solution)/shard_map/psum | solution.py:88
  630.2 229.5 %all-reduce.9.cloned.1.call-start = ((), (), s32[]{:S(2)}) async-start(), calls=%async_computation.3 | async-start | bytes 29360128 | tf_op jit(solution)/shard_map/psum | solution.py:90
  630.3 6.2 copy-start.6
  630.3 6.2 copy-start.10
  641.6 227.9 %copy-start.1 = (bf16[512,3456]{1,0:T(8,128)(2,1)S(1)}, bf16[512,3456]{1,0:T(8,128)(2,1)}, u32[]{:S(2)}) copy-start(bf16[512,3456]{1,0:T(8,128)(2,1)} %param.13) | copy-start | bytes 10616836
Sparse Core Ops, SparseCore 0:
  630.3 45.7 all-reduce.6
  683.2 176.4 all-reduce.8
where the time goes:
time: 885 us; the launch traced here: 877 us
  local copies, waits for them, and re-layouts  435 us (49%)
  other arithmetic  183 us (21%)
  waiting for transfers between devices  140 us (16%)
  blocking collectives  66.7 us (8%)
  matrix products  19.6 us (2%)
  starting transfers between devices  17.6 us (2%)
  between operations  14.5 us (2%)
    psum x1, waiting for transfers between devices, body(): freq_total = lax.psum(freq_grad, ('dp', 'rep'))  140 us
    gather x1, local copies, waits for them, and re-layouts, body(): sorted_owner = owners[sorted_order]  121 us
    gather x1, local copies, waits for them, and re-layouts, body(): owner_row[sorted_order]  121 us
    scatter x1, local copies, waits for them, and re-layouts, body(): bucket = jnp.zeros((shards * capacity + 1, emb_width), jnp.float32).at[ta...  109 us
    scatter-add x1, other arithmetic, body(): jax.ops.segment_sum(values, jnp.where(is_frequent, places, f_count), f_co...  72.4 us
    unnamed x1, blocking collectives  66.7 us
    scatter x1, local copies, waits for them, and re-layouts, body(): jnp.zeros((shards * capacity + 1,), jnp.int32).at[target]  49.8 us
    scatter-add x1, other arithmetic, body(): jax.ops.segment_sum(arrived.reshape(-1, emb_width), arrived_rows.reshape(...  42 us
  transfers between devices with their start and end apart: 4, of which 1 were waited for; matrix products, arithmetic and copies ran while one was open for 27% of the time, Pallas kernels for 0%

commit v1 on v0

v1 whole, which is shorter than its diff:
```python
import functools
import jax
import jax.numpy as jnp
from jax import lax
from jax.experimental import pallas as pl
from jax.experimental.pallas import tpu as pltpu
from jax.sharding import PartitionSpec as P

learn_rate = 0.05
eps_ada = 1e-08
f32, bf16, i32 = jnp.float32, jnp.bfloat16, jnp.int32
VLIM = 60 * 1024 * 1024


def row_adagrad(table, accum, grad):
    accum_new = accum + jnp.mean(grad * grad, axis=1)
    return (table - learn_rate * grad / (jnp.sqrt(accum_new)[:, None] + eps_ada), accum_new)


def dot_nt(a, b):
    return lax.dot_general(a, b, (((1,), (1,)), ((), ())), preferred_element_type=f32)


def dot_tn(a, b):
    return lax.dot_general(a, b, (((0,), (0,)), ((), ())), preferred_element_type=f32)


def hi_lo(v):
    hi = v.astype(bf16)
    lo = (v - hi.astype(f32)).astype(bf16)
    return jnp.concatenate([hi, lo], axis=1)


def one_hot(flags):
    return jnp.where(flags, 1.0, 0.0).astype(bf16)


def index_kernel(frequent, owned, place, idx, row, hot, cum):
    tables, samples = place.shape
    owners, slots = idx.shape
    at = lax.broadcasted_iota(i32, (1, samples), 1)
    owner_iota = lax.broadcasted_iota(i32, (owners, samples), 0)
    tri = one_hot(
        lax.broadcasted_iota(i32, (samples, samples), 0)
        < lax.broadcasted_iota(i32, (samples, samples), 1)
    )
    shift = owned.bit_length() - 1
    for t in range(tables):
        owner = lax.shift_right_arithmetic(place[t : t + 1, :] - frequent, shift)
        hot[t * owners : (t + 1) * owners, :] = one_hot(owner_iota == owner)
    cum[...] = jnp.dot(hot[...], tri, preferred_element_type=f32)
    base = jnp.zeros((owners, 1), f32)
    total = jnp.zeros((4 * owners, slots), f32)
    slot_iota = lax.broadcasted_iota(i32, (slots, samples), 0)
    at_hi = lax.shift_right_logical(at, 7).astype(f32)
    at_lo = (at & 127).astype(f32)
    blocks = samples // 128
    for t in range(tables):
        mine = hot[t * owners : (t + 1) * owners, :].astype(f32)
        before = cum[t * owners : (t + 1) * owners, :] + base
        rank = jnp.sum(mine * before, axis=0, keepdims=True).astype(i32)
        base = before[:, samples - 1 :] + mine[:, samples - 1 :]
        local = (place[t : t + 1, :] - frequent) & (owned - 1)
        parts = [
            mine * (at_hi + float((t + 1) * blocks)),
            mine * at_lo,
            mine * (lax.shift_right_logical(local, 7) + 1).astype(f32),
            mine * (local & 127).astype(f32),
        ]
        left = jnp.concatenate(parts, axis=0).astype(bf16)
        total = total + dot_nt(left, one_hot(slot_iota == rank))
    idx[...] = (total[:owners] * 128.0 + total[owners : 2 * owners]).astype(i32)
    row[...] = (total[2 * owners : 3 * owners] - 1.0) * 128.0 + total[3 * owners :]


def values_kernel(hidden, back_low, cot, up, down, bias, out):
    scaled = jnp.dot(hidden[...], up[...], preferred_element_type=f32) + bias[...]
    back = dot_nt(back_low[...], down[...])
    v = cot[...].astype(f32) * (scaled + 1.0) + back
    for k in range(out.shape[0]):
        out[k] = v[:, k * 128 : (k + 1) * 128]


def gather_kernel(idx, values, row, out):
    o = pl.program_id(0)
    slots = out.shape[1] - 8

    def step(i, _):
        at = pl.multiple_of(i * 16, 16)
        for k in range(16):
            src = idx[o, at + k]
            out[0, pl.ds(at + k, 1), :] = values[pl.ds(src, 1), :]
        return 0

    lax.fori_loop(0, slots // 16, step, 0)
    out[0, slots : slots + 8, :] = jnp.zeros((8, 128), f32)
    out[0, slots : slots + 1, :] = row[0, :, 0:128]
    out[0, slots + 1 : slots + 2, :] = row[0, :, 128:256]


def weights_kernel(count, steps, hidden, back_low, cross, cot, values, place, both, freq, hidden_t, down, up):
    g = pl.program_id(0)
    rank = hidden.shape[1]
    wide = cross.shape[1]
    per = wide // 128
    frequent = freq.shape[0]
    block = both.shape[0] // count
    up_rows = rank // count
    width = wide * steps
    down_rows = width // count

    @pl.when(g == 0)
    def _():
        hidden_t[...] = hidden[...].T
        freq[...] = jnp.zeros_like(freq)

    inner = cot[...].astype(f32) * cross[...].astype(f32)
    u = jnp.dot(hidden_t[...], inner.astype(bf16), preferred_element_type=f32)
    for k in range(per):
        up[k * rank : (k + 1) * rank, :] = u[:, k * 128 : (k + 1) * 128]
    d = dot_tn(cross[...], back_low[...])
    for k in range(rank // 128):
        down[pl.ds(pl.multiple_of(k * width + g * wide, 128), wide), :] = d[:, k * 128 : (k + 1) * 128]
    row_iota = lax.broadcasted_iota(i32, (frequent, 512), 0)
    for k in range(per):
        hot = one_hot(row_iota == place[0, k : k + 1, :])
        s = jnp.dot(hot, hi_lo(values[k]), preferred_element_type=f32)
        freq[...] += s[:, :128] + s[:, 128:]

    cols = per * steps

    def put_up(i, _):
        for k in range(per):
            both[pl.ds(i * block + g * per + k, up_rows, stride=cols), :] = up[
                pl.ds(k * rank + i * up_rows, up_rows), :
            ]
        return 0

    lax.fori_loop(0, count, put_up, 0)

    @pl.when(g == steps - 1)
    def _():
        def put_down(i, _):
            for k in range(rank // 128):
                both[pl.ds(i * block + up_rows * cols + k, down_rows, stride=rank // 128), :] = down[
                    pl.ds(k * width + i * down_rows, down_rows), :
                ]
            return 0

        lax.fori_loop(0, count, put_down, 0)


def segment_kernel(arrived, out, acc):
    g = pl.program_id(0)
    owned = out.shape[0]
    slots = arrived.shape[1] - 8

    @pl.when(g == 0)
    def _():
        acc[...] = jnp.zeros_like(acc)

    hots, parts = [], []
    for b in range(arrived.shape[0]):
        r0 = arrived[b, slots : slots + 1, :]
        r1 = arrived[b, slots + 1 : slots + 2, : slots - 128]
        hots.append(jnp.concatenate([r0, r1], axis=1).astype(i32))
        parts.append(hi_lo(arrived[b, :slots, :]))
    rows = jnp.concatenate(hots, axis=1)
    right = jnp.concatenate(parts, axis=0)
    step = 512
    for m in range(0, owned, step):
        hot = one_hot(lax.broadcasted_iota(i32, (step, rows.shape[1]), 0) + m == rows)
        acc[m : m + step, :] += jnp.dot(hot, right, preferred_element_type=f32)

    @pl.when(g == pl.num_programs(0) - 1)
    def _():
        out[...] = acc[:, :128] + acc[:, 128:]


def params(**kw):
    return pltpu.CompilerParams(vmem_limit_bytes=VLIM, **kw)


def body(cross_in, cotangent, weight_down, weight_up, cross_bias, row_place, frequent_table, frequent_accum, shard_table, shard_accum):
    samples, width = cross_in.shape
    rank = weight_down.shape[1]
    tables = row_place.shape[1]
    emb = frequent_table.shape[1]
    f_count = frequent_table.shape[0]
    owned = shard_table.shape[0]
    shards = lax.axis_size("dp")
    count = shards * lax.axis_size("rep")
    capacity = samples * tables // (2 * shards)
    blocks = width // emb
    per = 3
    steps = blocks // per
    wide = per * emb
    vmem = pl.BlockSpec(memory_space=pltpu.VMEM)

    place_t = row_place.T
    idx, row = pl.pallas_call(
        functools.partial(index_kernel, f_count, owned),
        out_shape=(jax.ShapeDtypeStruct((shards, 256), i32), jax.ShapeDtypeStruct((shards, 256), f32)),
        in_specs=[vmem],
        out_specs=(vmem, vmem),
        scratch_shapes=[pltpu.VMEM((tables * shards, samples), bf16), pltpu.VMEM((tables * shards, samples), f32)],
        compiler_params=params(),
        name="index_kernel",
    )(place_t)

    hidden = jnp.dot(cross_in, weight_down, preferred_element_type=f32).astype(bf16)
    inner = cotangent.astype(f32) * cross_in.astype(f32)
    back_low = lax.dot_general(
        inner.astype(bf16), weight_up, (((1,), (1,)), ((), ())), preferred_element_type=f32
    ).astype(bf16)

    values = pl.pallas_call(
        values_kernel,
        grid=(steps,),
        out_shape=jax.ShapeDtypeStruct((blocks, samples, emb), f32),
        in_specs=[
            pl.BlockSpec((samples, rank), lambda g: (0, 0)),
            pl.BlockSpec((samples, rank), lambda g: (0, 0)),
            pl.BlockSpec((samples, wide), lambda g: (0, g)),
            pl.BlockSpec((rank, wide), lambda g: (0, g)),
            pl.BlockSpec((wide, rank), lambda g: (g, 0)),
            pl.BlockSpec((1, wide), lambda g: (0, g)),
        ],
        out_specs=pl.BlockSpec((per, samples, emb), lambda g: (g, 0, 0)),
        compiler_params=params(),
        name="values_kernel",
    )(hidden, back_low, cotangent, weight_up, weight_down, cross_bias.reshape(1, -1))

    bucket = pl.pallas_call(
        gather_kernel,
        grid=(shards,),
        out_shape=jax.ShapeDtypeStruct((shards, capacity + 8, emb), f32),
        in_specs=[
            pl.BlockSpec(memory_space=pltpu.SMEM),
            pl.BlockSpec((blocks * samples, emb), lambda g: (0, 0)),
            pl.BlockSpec((1, 1, 256), lambda g: (g, 0, 0)),
        ],
        out_specs=pl.BlockSpec((1, capacity + 8, emb), lambda g: (g, 0, 0)),
        compiler_params=params(),
        name="gather_kernel",
    )(idx, values.reshape(blocks * samples, emb), row.reshape(shards, 1, 256))

    arrived = lax.all_to_all(bucket, "dp", split_axis=0, concat_axis=0, tiled=True)

    place3 = jnp.concatenate([jnp.full((1, samples), -1, i32), place_t], axis=0).reshape(steps, per, samples)
    block = rank * width // count // 128 * 2
    both, freq = pl.pallas_call(
        functools.partial(weights_kernel, count, steps),
        grid=(steps,),
        out_shape=(
            jax.ShapeDtypeStruct((count * block, 128), f32),
            jax.ShapeDtypeStruct((f_count, emb), f32),
        ),
        in_specs=[
            pl.BlockSpec((samples, rank), lambda g: (0, 0)),
            pl.BlockSpec((samples, rank), lambda g: (0, 0)),
            pl.BlockSpec((samples, wide), lambda g: (0, g)),
            pl.BlockSpec((samples, wide), lambda g: (0, g)),
            pl.BlockSpec((per, samples, emb), lambda g: (g, 0, 0)),
            pl.BlockSpec((1, per, samples), lambda g: (g, 0, 0)),
        ],
        out_specs=(
            pl.BlockSpec((count * block, 128), lambda g: (0, 0)),
            pl.BlockSpec((f_count, emb), lambda g: (0, 0)),
        ),
        scratch_shapes=[
            pltpu.VMEM((rank, samples), bf16),
            pltpu.VMEM((rank // 128 * width, 128), f32),
            pltpu.VMEM((per * rank, 128), f32),
        ],
        compiler_params=params(),
        name="weights_kernel",
    )(hidden, back_low, cross_in, cotangent, values, place3)
    local_bias = jnp.sum(inner, axis=0)

    mine = lax.psum_scatter(both, ("dp", "rep"), scatter_dimension=0, tiled=True)
    mine = lax.optimization_barrier(mine)
    small = jnp.concatenate([freq, local_bias.reshape(blocks, emb)], axis=0)
    small = lax.psum(jnp.pad(small, ((0, -small.shape[0] % 8), (0, 0))), ("dp", "rep"))
    me = lax.axis_index("dp") * lax.axis_size("rep") + lax.axis_index("rep")
    bias_all = small[f_count : f_count + blocks].reshape(-1)
    grad_bias = lax.dynamic_slice(bias_all, (me * (width // count),), (width // count,))
    grad_up = mine[: block // 2].reshape(rank // count, width)
    grad_down = mine[block // 2 :].reshape(width // count, rank)

    shard_grad = pl.pallas_call(
        segment_kernel,
        grid=(shards // 4,),
        out_shape=jax.ShapeDtypeStruct((owned, emb), f32),
        in_specs=[pl.BlockSpec((4, capacity + 8, emb), lambda g: (g, 0, 0))],
        out_specs=pl.BlockSpec((owned, emb), lambda g: (0, 0)),
        scratch_shapes=[pltpu.VMEM((owned, 256), f32)],
        compiler_params=params(),
        name="segment_kernel",
    )(arrived)
    shard_grad = lax.psum(shard_grad, "rep")
    new_shard, new_shard_accum = row_adagrad(shard_table, shard_accum, shard_grad)
    new_frequent, new_frequent_accum = row_adagrad(frequent_table, frequent_accum, small[:f_count])
    return (new_frequent, new_frequent_accum, new_shard, new_shard_accum, grad_up, grad_down, grad_bias)


def solution(mesh):
    both = ("dp", "rep")
    in_specs = (P(both, None), P(both, None), P(), P(), P(), P(both, None), P(), P(), P("dp", None), P("dp"))
    out_specs = (P(), P(), P("dp", None), P("dp"), P(both, None), P(both, None), P(both))
    return jax.shard_map(body, mesh=mesh, in_specs=in_specs, out_specs=out_specs, check_vma=False)
```

time: 885 us -> 540 us (0.61)
  local copies, waits for them, and re-layouts: 435 us -> 6.99 us
  waiting for transfers between devices: 140 us -> 401 us
  other arithmetic: 183 us -> 12.5 us
  Pallas kernels: 0 us -> 85 us
  blocking collectives: 66.7 us -> 0 us
  matrix products: 19.6 us -> 8.95 us
    gather x4 -> x0, local copies, waits for them, and re-layouts: 243 us -> none  [the longest x1 121 us: body(): sorted_owner = owners[sorted_order]]
    unnamed x2 -> x4, waiting for transfers between devices: 0.03 us -> 227 us
    scatter x2 -> x0, local copies, waits for them, and re-layouts: 159 us -> none  [the longest x1 109 us: body(): bucket = jnp.zeros((shards * capacity + 1, emb_width), jnp.float32).at[ta...]
    scatter-add x2 -> x0, other arithmetic: 114 us -> none  [the longest x1 72.4 us: body(): jax.ops.segment_sum(values, jnp.where(is_frequent, places, f_count), f_co...]
    pallas_call x0 -> x5, Pallas kernels: none -> 85 us  [the longest x1 30.2 us: body(): pl.pallas_call(functools.partial(weights_kernel, count, steps), grid=(ste...]
    unnamed x1 -> x0, blocking collectives: 66.7 us -> none
    psum x1, waiting for transfers between devices: 0.01 us -> 40.5 us  [body(): shard_grad = lax.psum(shard_grad, 'rep')]
    gather x4 -> x0, other arithmetic: 27.6 us -> none  [the longest x3 26.2 us: body(): slot_pos = jnp.arange(owners.shape[0]) - starts[sorted_owner]]
  transfers between devices with their start and end apart: 4 -> 4, of which waited for: 1 -> 4; matrix products, arithmetic and copies ran while one was open for 27% -> 3% of each run, Pallas kernels for 0% -> 8%
where the time goes in v1:
time: 540 us; the launch traced here: 538 us
  waiting for transfers between devices  401 us (74%)
  Pallas kernels  85 us (16%)
  between operations  13.9 us (3%)
  other arithmetic  12.5 us (2%)
  starting transfers between devices  9.74 us (2%)
  matrix products  8.95 us (2%)
  local copies, waits for them, and re-layouts  6.99 us (1%)
    unnamed x4, waiting for transfers between devices  227 us
    psum x1, waiting for transfers between devices, body(): lax.psum(jnp.pad(small, ((0, -small.shape[0] % 8), (0, 0))), ('dp', 'rep'))  124 us
    psum x1, waiting for transfers between devices, body(): shard_grad = lax.psum(shard_grad, 'rep')  40.5 us
    pallas_call x1, Pallas kernels, body(): pl.pallas_call(functools.partial(weights_kernel, count, steps), grid=(ste...  30.2 us
    pallas_call x1, Pallas kernels, body(): pl.pallas_call(gather_kernel, grid=(shards,), out_shape=jax.ShapeDtypeStr...  24.3 us
    pallas_call x1, Pallas kernels, body(): pl.pallas_call(segment_kernel, grid=(shards // 4,), out_shape=jax.ShapeDt...  12.7 us
    pallas_call x1, Pallas kernels, body(): pl.pallas_call(values_kernel, grid=(steps,), out_shape=jax.ShapeDtypeStru...  12.4 us
  transfers between devices with their start and end apart: 4, of which 4 were waited for; matrix products, arithmetic and copies ran while one was open for 3% of the time, Pallas kernels for 8%

profile of v1, /device:TPU:1, one launch (start us, length us, event | category | flops | bytes accessed | tf_op | source)
XLA Modules:
  0.0 537.6 jit_solution(12522468238906519066)
XLA Ops:
  7.2 1.3 reshape.42.bias
  8.5 5.4 %index_kernel.1 = (s32[32,256]{1,0:T(8,128)}, f32[32,256]{1,0:T(8,128)}) custom-call(s32[26,512]{1,0:T(8,128)} %bitcast.9), custom_call_target="tpu_custom_call" | custom-call | tf_op jit(solution)/shard_map/index_kernel/pallas_call | solution.py:201
  13.9 1.4 reshape.46.row
  15.3 6.1 %convolution_convert_fusion.hidden = bf16[512,512]{1,0:T(8,128)(2,1)} fusion(bf16[512,3456]{1,0:T(8,128)(2,1)} %cross.1, bf16[3456,512]{1,0:T(8,128)(2,1)} %down.1), kind=kOutput, calls=%fused_computation.5 | convolution fusion | flops 1812201472 | bytes 7602176 | tf_op jit(solution)/shard_map/dot_general | solution.py:211
  21.5 2.9 fusion.4.back_low
  24.3 12.4 %values_kernel.1.values = f32[27,512,128]{2,1,0:T(8,128)} custom-call(bf16[512,512]{1,0:T(8,128)(2,1)} %convolution_convert_fusion.hidden, bf16[512,512]{1,0:T(8,128)(2,1)} %fusion.4.back_low, bf16[512,3456]{1,0:T(8,128)(2,1)} %cot.3, bf16[512,3456]{1,0:T(8,128)(2,1)} %up.1, bf16[3456,512]{1,0:T(8,128)(2,1)} %down.1, f32[1,3456]{1,0:T(1,128)} %reshape.42.bias), custom_call_target="tpu_custom_call" | custom-call | tf_op jit(solution)/shard_map/values_kernel/pallas_call | solution.py:217
  36.8 24.3 %gather_kernel.1 = f32[32,216,128]{2,1,0:T(8,128)} custom-call(s32[32,256]{1,0:T(8,128)} %get-tuple-element.12.idx, f32[13824,128]{1,0:T(8,128)} %bitcast.8, f32[32,1,256]{2,1,0:T(1,128)} %reshape.46.row), custom_call_target="tpu_custom_call" | custom-call | tf_op jit(solution)/shard_map/gather_kernel/pallas_call | solution.py:234
  61.0 9.6 %all-to-all-start = ((f32[32,216,128]{2,1,0:T(8,128)}), f32[32,216,128]{2,1,0:T(8,128)}, u32[]{:S(2)}, u32[]{:S(2)}) async-start(f32[32,216,128]{2,1,0:T(8,128)} %gather_kernel.1), calls=%async_computation | async-start | bytes 7077888 | tf_op jit(solution)/shard_map/all_to_all | solution.py:248
  70.7 0.6 reshape.43.place
  71.4 30.2 %weights_kernel.1 = (f32[27648,128]{1,0:T(8,128)}, f32[1024,128]{1,0:T(8,128)}) custom-call(bf16[512,512]{1,0:T(8,128)(2,1)} %convolution_convert_fusion.hidden, bf16[512,512]{1,0:T(8,128)(2,1)} %fusion.4.back_low, bf16[512,3456]{1,0:T(8,128)(2,1)} %cross.1, bf16[512,3456]{1,0:T(8,128)(2,1)} %cot.3, f32[27,512,128]{2,1,0:T(8,128)} %values_kernel.1.values, ...), custom_call_target="tpu_custom_call" | custom-call | tf_op jit(solution)/shard_map/weights_kernel/pallas_call | solution.py:252
  101.6 3.0 fusion
  104.6 0.9 select_maximum_fusion
  105.5 9.5 %all-to-all-done.arrived = f32[32,216,128]{2,1,0:T(8,128)} async-done(((f32[32,216,128]{2,1,0:T(8,128)}), f32[32,216,128]{2,1,0:T(8,128)}, u32[]{:S(2)}, u32[]{:S(2)}) %all-to-all-start) | async-done | bytes 3538976 | tf_op jit(solution)/shard_map/all_to_all | solution.py:248
  115.0 12.7 %segment_kernel.1 = f32[2048,128]{1,0:T(8,128)} custom-call(f32[32,216,128]{2,1,0:T(8,128)} %all-to-all-done.arrived), custom_call_target="tpu_custom_call" | custom-call | tf_op jit(solution)/shard_map/segment_kernel/pallas_call | solution.py:291
  127.9 0.6 reduce-scatter.4.cloned.1.call-update
  128.6 123.8 %all-reduce.6.cloned.1.call-done = f32[1056,128]{1,0:T(8,128)} async-done(((f32[1056,128]{1,0:T(8,128)}), f32[1056,128]{1,0:T(8,128)}) %all-reduce.6.cloned.1.call-update) | async-done | bytes 540688 | tf_op jit(solution)/shard_map/psum | solution.py:284
  252.4 0.7 slice_bitcast_fusion
  253.7 1.2 multiply_reduce_fusion.1
  255.6 2.0 divide_subtract_fusion.1
  257.6 40.5 %all-reduce.8.cloned.1.call-done = f32[2048,128]{1,0:T(8,128)} async-done(((f32[2048,128]{1,0:T(8,128)}), f32[2048,128]{1,0:T(8,128)}) %all-reduce.8.cloned.1.call-update) | async-done | bytes 1048592 | tf_op jit(solution)/shard_map/psum | solution.py:301
  298.1 1.6 multiply_reduce_fusion
  300.3 2.5 divide_subtract_fusion
  302.8 226.1 %reduce-scatter.4.cloned.1.call-done = f32[216,128]{1,0:T(8,128)} async-done(((f32[27648,128]{1,0:T(8,128)}), f32[216,128]{1,0:T(8,128)}) %reduce-scatter.4.cloned.1.call-update) | async-done | bytes 110608
  528.9 0.9 fusion.7
  (31 shorter events, 3.4 us)
Async XLA Ops:
  15.3 6.1 %copy-start = (bf16[512,3456]{1,0:T(8,128)(2,1)S(1)}, bf16[512,3456]{1,0:T(8,128)(2,1)}, u32[]{:S(2)}) copy-start(bf16[512,3456]{1,0:T(8,128)(2,1)} %cot.3) | copy-start | bytes 10616836
  15.3 6.1 %copy-start.2 = (bf16[512,3456]{1,0:T(8,128)(2,1)S(1)}, bf16[512,3456]{1,0:T(8,128)(2,1)}, u32[]{:S(2)}) copy-start(bf16[512,3456]{1,0:T(8,128)(2,1)} %cross.1) | copy-start | bytes 10616836
  15.3 6.2 %copy-start.3 = (bf16[512,3456]{1,0:T(8,128)(2,1)S(1)}, bf16[512,3456]{1,0:T(8,128)(2,1)}, u32[]{:S(2)}) copy-start(bf16[512,3456]{1,0:T(8,128)(2,1)} %up.1) | copy-start | bytes 10616836
  61.0 9.7 %copy-start.7 = (s32[512,26]{0,1:T(8,128)S(1)}, s32[512,26]{0,1:T(8,128)}, u32[]{:S(2)}) copy-start(s32[512,26]{0,1:T(8,128)} %param.15) | copy-start | bytes 159748
  61.0 54.0 %all-to-all-start = ((f32[32,216,128]{2,1,0:T(8,128)}), f32[32,216,128]{2,1,0:T(8,128)}, u32[]{:S(2)}, u32[]{:S(2)}) async-start(f32[32,216,128]{2,1,0:T(8,128)} %gather_kernel.1), calls=%async_computation | async-start | bytes 7077888 | tf_op jit(solution)/shard_map/all_to_all | solution.py:248
  70.7 181.7 %all-reduce.6.cloned.1.call-start = ((), (), s32[]{:S(2)}) async-start(), calls=%async_computation.2 | async-start | bytes 1081344 | tf_op jit(solution)/shard_map/psum | solution.py:284
  71.4 30.2 %copy-start.1 = (bf16[512,3456]{1,0:T(8,128)(2,1)S(1)}, bf16[512,3456]{1,0:T(8,128)(2,1)}, u32[]{:S(2)}) copy-start(bf16[512,3456]{1,0:T(8,128)(2,1)} %cot.3) | copy-start | bytes 10616836
  101.6 3.0 copy-start.6
  105.5 192.6 %all-reduce.8.cloned.1.call-start = ((), (), s32[]{:S(2)}) async-start(), calls=%async_computation.3 | async-start | bytes 2097152 | tf_op jit(solution)/shard_map/psum | solution.py:301
  127.8 401.0 %reduce-scatter.4.cloned.1.call-start = ((), (), s32[]{:S(2)}) async-start(), calls=%async_computation.4 | async-start | bytes 14266368
  127.9 127.1 %copy-start.9 = (f32[1024]{0:T(1024)S(1)}, f32[1024]{0:T(1024)}, u32[]{:S(2)}) copy-start(f32[1024]{0:T(1024)} %param.17) | copy-start | bytes 12292
  127.9 127.7 %copy-start.5 = (f32[1024,128]{1,0:T(8,128)S(1)}, f32[1024,128]{1,0:T(8,128)}, u32[]{:S(2)}) copy-start(f32[1024,128]{1,0:T(8,128)} %param.16) | copy-start | bytes 1572868
  127.9 171.8 %copy-start.8 = (f32[2048]{0:T(1024)S(1)}, f32[2048]{0:T(1024)}, u32[]{:S(2)}) copy-start(f32[2048]{0:T(1024)} %param.19) | copy-start | bytes 24580
  128.6 171.7 %copy-start.4 = (f32[2048,128]{1,0:T(8,128)S(1)}, f32[2048,128]{1,0:T(8,128)}, u32[]{:S(2)}) copy-start(f32[2048,128]{1,0:T(8,128)} %param.18) | copy-start | bytes 3145732
Sparse Core Ops, SparseCore 0:
  105.6 146.7 all-reduce.5
  255.5 42.5 all-reduce.7
  303.1 225.6 reduce-scatter.3

commit v2 on v1

--- a/solution.py
+++ b/solution.py
@@ -98,7 +98,7 @@
     out[0, slots + 1 : slots + 2, :] = row[0, :, 128:256]
 
 
-def weights_kernel(count, steps, hidden, back_low, cross, cot, values, place, both, freq, hidden_t, down, up):
+def weights_kernel(count, steps, hidden, back_low, cross, cot, values, place, both, bias, freq, hidden_t, down, up):
     g = pl.program_id(0)
     rank = hidden.shape[1]
     wide = cross.shape[1]
@@ -115,6 +115,7 @@
         freq[...] = jnp.zeros_like(freq)
 
     inner = cot[...].astype(f32) * cross[...].astype(f32)
+    bias[...] = jnp.sum(inner, axis=0, keepdims=True)
     u = jnp.dot(hidden_t[...], inner.astype(bf16), preferred_element_type=f32)
     for k in range(per):
         up[k * rank : (k + 1) * rank, :] = u[:, k * 128 : (k + 1) * 128]
@@ -145,6 +146,7 @@
                 both[pl.ds(i * block + up_rows * cols + k, down_rows, stride=rank // 128), :] = down[
                     pl.ds(k * width + i * down_rows, down_rows), :
                 ]
+            both[pl.ds(i * block + block - 8, 8), :] = freq[pl.ds(pl.multiple_of(i * 8, 8), 8), :]
             return 0
 
         lax.fori_loop(0, count, put_down, 0)
@@ -177,8 +179,303 @@
         out[...] = acc[:, :128] + acc[:, 128:]
 
 
+PORT = ((0, 96, 48, "xzy"), (96, 96, 48, "zxy"), (192, 40, 24, "yxz"))
+
+
 def params(**kw):
     return pltpu.CompilerParams(vmem_limit_bytes=VLIM, **kw)
+
+
+def reduce_kernel(both, bias, seg, mine, freq_out, seg_out, *scratch):
+    n_port = len(PORT)
+    it = iter(scratch)
+    work = [next(it) for _ in PORT]
+    pair = [next(it) for _ in PORT]
+    land = [[[next(it) for _ in range(4)] for _ in range(3)] for _ in PORT]
+    swork = next(it)
+    sland = [next(it) for _ in range(4)]
+    sgath = next(it)
+    gath = next(it)
+    send_sems, recv_sems, local_sems = next(it), next(it), next(it)
+
+    dp, y = lax.axis_index("dp"), lax.axis_index("rep")
+    me = {"x": dp // 8, "z": (dp // 2) % 4, "y": y}
+    core = dp % 2
+
+    def device(axis, to):
+        at = dict(me, **{axis: to})
+        return ((at["x"] * 4 + at["z"]) * 2 + core, at["y"])
+
+    partner = (dp + 1 - 2 * core, y)
+    up = {a: (me[a] + 1) % 4 for a in "xzy"}
+    down = {a: (me[a] + 3) % 4 for a in "xzy"}
+    far = {a: (me[a] + 2) % 4 for a in "xzy"}
+    peers = [partner] + [device(a, s[a]) for a in "xzy" for s in (up, down)]
+    barrier = pltpu.get_barrier_semaphore()
+    for peer in peers:
+        pl.semaphore_signal(barrier, inc=1, device_id=peer, device_id_type=pl.DeviceIdType.MESH)
+    pl.semaphore_wait(barrier, len(peers))
+
+    sent, used = [], [0]
+
+    def send(src, dst, to):
+        k = used[0]
+        used[0] += 1
+        copy = pltpu.make_async_remote_copy(
+            src_ref=src, dst_ref=dst, send_sem=send_sems.at[k], recv_sem=recv_sems.at[k],
+            device_id=to, device_id_type=pl.DeviceIdType.MESH,
+        )
+        copy.start()
+        sent.append(copy)
+        return copy
+
+    def place(done, axis, t, rem=None):
+        rem = iter(rem) if rem is not None else None
+        out = []
+        for a in "xzy":
+            if a in done:
+                out.append(me[a])
+            elif a == axis:
+                out.append(t)
+            else:
+                out.append(slice(None) if rem is None else next(rem))
+        return tuple(out)
+
+    def each(n_rem, fn):
+        if n_rem == 0:
+            fn(())
+        elif n_rem == 1:
+            lax.fori_loop(0, 4, lambda i, _: (fn((i,)), 0)[1], 0)
+        else:
+            lax.fori_loop(0, 16, lambda i, _: (fn((i // 4, i % 4)), 0)[1], 0)
+
+    class Reduce:
+        def __init__(self, ref, done, axis, rows, half, lands, free=2):
+            self.ref, self.done, self.axis, self.rows, self.half, self.lands = ref, done, axis, rows, half, lands
+            self.n = free
+
+        def at(self, t, lo, hi):
+            if self.done is None:
+                return self.ref.at[t, pl.ds(lo, hi - lo), :]
+            return self.ref.at[place(self.done, self.axis, t) + (pl.ds(lo, hi - lo), slice(None))]
+
+        def add(self, t, lo, hi, *refs):
+            def one(rem):
+                if self.done is None:
+                    step = 128
+                    for r in range(lo, hi, step):
+                        v = self.ref[t, r : r + step, :]
+                        for ref in refs:
+                            v = v + ref[r - lo : r - lo + step, :]
+                        self.ref[t, r : r + step, :] = v
+                    return
+                where = place(self.done, self.axis, t, rem)
+                v = self.ref[where + (slice(lo, hi), slice(None))]
+                for ref in refs:
+                    v = v + ref[rem + (slice(None), slice(None))]
+                self.ref[where + (slice(lo, hi), slice(None))] = v
+
+            each(self.n, one)
+
+        def start(self):
+            a = self.axis
+            self.c0 = send(self.at(far[a], 0, self.half), self.lands[0], device(a, up[a]))
+            self.c1 = send(self.at(far[a], self.half, self.rows), self.lands[1], device(a, down[a]))
+
+        def middle(self):
+            a = self.axis
+            self.c0.wait_recv()
+            self.add(up[a], 0, self.half, self.lands[0])
+            self.c2 = send(self.at(up[a], 0, self.rows), self.lands[2], device(a, up[a]))
+            self.c1.wait_recv()
+            self.add(down[a], self.half, self.rows, self.lands[1])
+            self.c3 = send(self.at(down[a], 0, self.rows), self.lands[3], device(a, down[a]))
+
+        def finish(self):
+            self.c2.wait_recv()
+            self.c3.wait_recv()
+            self.add(me[self.axis], 0, self.rows, self.lands[2], self.lands[3])
+
+    class Gather:
+        def __init__(self, axis, at):
+            self.axis, self.at = axis, at
+
+        def start(self):
+            a = self.axis
+            src = self.at(me[a], None)
+            self.c0 = send(src, src, device(a, up[a]))
+            self.c1 = send(src, src, device(a, down[a]))
+
+        def middle(self):
+            a = self.axis
+            self.c0.wait_recv()
+            src = self.at(down[a], 0)
+            self.c2 = send(src, src, device(a, up[a]))
+            self.c1.wait_recv()
+            src = self.at(up[a], 1)
+            self.c3 = None
+            if src is not None:
+                self.c3 = send(src, src, device(a, down[a]))
+
+        def finish(self):
+            self.c2.wait_recv()
+            if self.c3 is not None:
+                self.c3.wait_recv()
+
+    firsts, locals_ = [], []
+    for p, (first, rows, half, order) in enumerate(PORT):
+        whole = rows if p < n_port - 1 else rows - 8
+        got = [
+            send(
+                both.at[:, :, 1 - core, :, pl.ds(first, whole), :],
+                pair[p].at[:, :, :, pl.ds(0, whole), :],
+                partner,
+            )
+        ]
+        loc = [pltpu.make_async_copy(
+            both.at[:, :, core, :, pl.ds(first, whole), :], work[p].at[:, :, :, pl.ds(0, whole), :], local_sems.at[p])]
+        if p == n_port - 1:
+            got.append(send(bias.at[:, :, 1 - core], pair[p].at[:, :, :, pl.ds(whole, 8), :], partner))
+            loc.append(pltpu.make_async_copy(
+                bias.at[:, :, core], work[p].at[:, :, :, pl.ds(whole, 8), :], local_sems.at[n_port]))
+        for c in loc:
+            c.start()
+        firsts.append(got)
+        locals_.append(loc)
+    load = pltpu.make_async_copy(seg, swork, local_sems.at[n_port + 1])
+    load.start()
+    load.wait()
+    owned = swork.shape[1]
+    s_red = Reduce(swork, None, "y", owned, owned // 2, sland, 0)
+    s_red.start()
+
+    reds = []
+    for p, (first, rows, half, order) in enumerate(PORT):
+        phases = []
+        for k in range(3):
+            phases.append(Reduce(work[p], order[:k], order[k], rows, half, land[p][k], 2 - k))
+        reds.append(phases)
+
+    def begin(p):
+        for c in locals_[p]:
+            c.wait()
+        for c in firsts[p]:
+            c.wait_recv()
+
+        def one(i, _):
+            w = (i // 16, (i // 4) % 4, i % 4)
+            work[p][w] = work[p][w] + pair[p][w]
+            return 0
+
+        lax.fori_loop(0, 64, one, 0)
+        reds[p][0].start()
+
+    def s_half(t, h):
+        if h is None:
+            return sgath.at[t]
+        return sgath.at[t, pl.ds(h * (owned // 2), owned // 2), :]
+
+    s_gat = Gather("y", s_half)
+
+    def y_at(t, h):
+        return None if h == 1 else gath.at[me["x"], me["z"], core, t]
+
+    def z_at(t, h):
+        return gath.at[me["x"], t, core] if h is None else gath.at[me["x"], t, core, pl.ds(2 * h, 2)]
+
+    def x_at(t, h):
+        return gath.at[t, :, core] if h is None else gath.at[t, pl.ds(2 * h, 2), core]
+
+    g_y, g_z, g_x = Gather("y", y_at), Gather("z", z_at), Gather("x", x_at)
+    here = (me["x"], me["z"], me["y"])
+
+    begin(2)
+    begin(0)
+    begin(1)
+    s_red.middle()
+    reds[2][0].middle()
+    reds[0][0].middle()
+    reds[1][0].middle()
+    reds[2][0].finish()
+    reds[2][1].start()
+    s_red.finish()
+    sgath[me["y"]] = swork[me["y"]]
+    s_gat.start()
+    reds[2][1].middle()
+    reds[2][1].finish()
+    reds[2][2].start()
+    reds[2][2].middle()
+    reds[2][2].finish()
+    last = n_port - 1
+    rows_last = PORT[last][1]
+    gath[me["x"], me["z"], core, me["y"]] = work[last][here + (slice(rows_last - 16, rows_last - 8), slice(None))]
+    g_y.start()
+    s_gat.middle()
+    g_y.middle()
+    reds[0][0].finish()
+    reds[0][1].start()
+    reds[1][0].finish()
+    reds[1][1].start()
+    g_y.finish()
+    g_z.start()
+    s_gat.finish()
+    reds[0][1].middle()
+    reds[1][1].middle()
+    g_z.middle()
+    reds[0][1].finish()
+    reds[0][2].start()
+    reds[1][1].finish()
+    reds[1][2].start()
+    g_z.finish()
+    g_x.start()
+    reds[0][2].middle()
+    reds[1][2].middle()
+    g_x.middle()
+    reds[0][2].finish()
+    reds[1][2].finish()
+    g_x.finish()
+    g_c = send(gath.at[:, :, core], gath.at[:, :, core], partner)
+    for p, (first, rows, half, order) in enumerate(PORT):
+        mine[first : first + rows, :] = work[p][here]
+    seg_out[...] = sgath[...]
+    g_c.wait_recv()
+    freq_out[...] = gath[...]
+    for c in sent:
+        c.wait_send()
+
+
+def reduce_scratch(owned):
+    v = lambda *s: pltpu.VMEM(s, f32)
+    out = [v(4, 4, 4, r, 128) for _, r, _, _ in PORT] * 2
+    for _, r, h, _ in PORT:
+        for k in range(3):
+            lead = (4,) * (2 - k)
+            out += [v(*lead, h, 128), v(*lead, r - h, 128), v(*lead, r, 128), v(*lead, r, 128)]
+    out += [v(4, owned // 4, 128), v(owned // 8, 128), v(owned // 8, 128), v(owned // 4, 128), v(owned // 4, 128), v(4, owned // 4, 128)]
+    out += [v(4, 4, 2, 4, 8, 128)]
+    out += [pltpu.SemaphoreType.DMA((80,)), pltpu.SemaphoreType.DMA((80,)), pltpu.SemaphoreType.DMA((8,))]
+    return out
+
+
+def reduce_all(both, bias, seg):
+    owned = seg.shape[0]
+    per = both.shape[0] // 128
+    vmem = pl.BlockSpec(memory_space=pltpu.VMEM)
+    anyw = pl.BlockSpec(memory_space=pl.ANY)
+    mine, freq, seg = pl.pallas_call(
+        reduce_kernel,
+        out_shape=(
+            jax.ShapeDtypeStruct((per + 8, 128), f32),
+            jax.ShapeDtypeStruct((4, 4, 2, 4, 8, 128), f32),
+            jax.ShapeDtypeStruct((4, owned // 4, 128), f32),
+        ),
+        in_specs=[anyw, anyw, anyw],
+        out_specs=(vmem, vmem, vmem),
+        scratch_shapes=reduce_scratch(owned),
+        compiler_params=params(collective_id=0, has_side_effects=True),
+        name="reduce_kernel",
+    )(both.reshape(4, 4, 2, 4, per, 128), bias.reshape(4, 4, 2, 4, 8, 128), seg.reshape(4, owned // 4, 128))
+    return mine, freq.reshape(1024, 128), seg.reshape(owned, 128)
 
 
 def body(cross_in, cotangent, weight_down, weight_up, cross_bias, row_place, frequent_table, frequent_accum, shard_table, shard_accum):
@@ -248,13 +545,13 @@
     arrived = lax.all_to_all(bucket, "dp", split_axis=0, concat_axis=0, tiled=True)
 
     place3 = jnp.concatenate([jnp.full((1, samples), -1, i32), place_t], axis=0).reshape(steps, per, samples)
-    block = rank * width // count // 128 * 2
-    both, freq = pl.pallas_call(
+    block = rank * width // count // 128 * 2 + f_count // count
+    both, bias = pl.pallas_call(
         functools.partial(weights_kernel, count, steps),
         grid=(steps,),
         out_shape=(
             jax.ShapeDtypeStruct((count * block, 128), f32),
-            jax.ShapeDtypeStruct((f_count, emb), f32),
+            jax.ShapeDtypeStruct((1, width), f32),
         ),
         in_specs=[
             pl.BlockSpec((samples, rank), lambda g: (0, 0)),
@@ -266,9 +563,10 @@
         ],
         out_specs=(
             pl.BlockSpec((count * block, 128), lambda g: (0, 0)),
-            pl.BlockSpec((f_count, emb), lambda g: (0, 0)),
+            pl.BlockSpec((1, wide), lambda g: (0, g)),
         ),
         scratch_shapes=[
+            pltpu.VMEM((f_count, emb), f32),
             pltpu.VMEM((rank, samples), bf16),
             pltpu.VMEM((rank // 128 * width, 128), f32),
             pltpu.VMEM((per * rank, 128), f32),
@@ -276,17 +574,7 @@
         compiler_params=params(),
         name="weights_kernel",
     )(hidden, back_low, cross_in, cotangent, values, place3)
-    local_bias = jnp.sum(inner, axis=0)
-
-    mine = lax.psum_scatter(both, ("dp", "rep"), scatter_dimension=0, tiled=True)
-    mine = lax.optimization_barrier(mine)
-    small = jnp.concatenate([freq, local_bias.reshape(blocks, emb)], axis=0)
-    small = lax.psum(jnp.pad(small, ((0, -small.shape[0] % 8), (0, 0))), ("dp", "rep"))
-    me = lax.axis_index("dp") * lax.axis_size("rep") + lax.axis_index("rep")
-    bias_all = small[f_count : f_count + blocks].reshape(-1)
-    grad_bias = lax.dynamic_slice(bias_all, (me * (width // count),), (width // count,))
-    grad_up = mine[: block // 2].reshape(rank // count, width)
-    grad_down = mine[block // 2 :].reshape(width // count, rank)
+    bias = jnp.pad(bias.reshape(count, 1, width // count), ((0, 0), (0, 7), (0, 128 - width // count)))
 
     shard_grad = pl.pallas_call(
         segment_kernel,
@@ -298,9 +586,13 @@
         compiler_params=params(),
         name="segment_kernel",
     )(arrived)
-    shard_grad = lax.psum(shard_grad, "rep")
+    mine, freq, shard_grad = reduce_all(both, bias, shard_grad)
+    n = rank * width // count // 128
+    grad_up = mine[:n].reshape(rank // count, width)
+    grad_down = mine[n : 2 * n].reshape(width // count, rank)
+    grad_bias = mine[block, : width // count]
     new_shard, new_shard_accum = row_adagrad(shard_table, shard_accum, shard_grad)
-    new_frequent, new_frequent_accum = row_adagrad(frequent_table, frequent_accum, small[:f_count])
+    new_frequent, new_frequent_accum = row_adagrad(frequent_table, frequent_accum, freq)
     return (new_frequent, new_frequent_accum, new_shard, new_shard_accum, grad_up, grad_down, grad_bias)
 
 

time: 540 us -> 219 us (0.41)
  waiting for transfers between devices: 401 us -> 7.74 us
  Pallas kernels: 85 us -> 170 us
  between operations: 13.9 us -> 0.75 us
  local copies, waits for them, and re-layouts: 6.99 us -> 13.7 us
    unnamed x4 -> x0, waiting for transfers between devices: 227 us -> none
    psum x2 -> x0, waiting for transfers between devices: 164 us -> none  [the longest x1 124 us: body(): lax.psum(jnp.pad(small, ((0, -small.shape[0] % 8), (0, 0))), ('dp', 'rep'))]
    pallas_call x0 -> x1, Pallas kernels: none -> 84.9 us  [reduce_all(): pl.pallas_call(reduce_kernel, out_shape=(jax.ShapeDtypeStruct((per + 8, 1...]
  transfers between devices with their start and end apart: 4 -> 1, of which waited for: 4 -> 1; matrix products, arithmetic and copies ran while one was open for 3% -> 3% of each run, Pallas kernels for 8% -> 14%
where the time goes in v2:
time: 219 us; the launch traced here: 218 us
  Pallas kernels  170 us (78%)
  local copies, waits for them, and re-layouts  13.7 us (6%)
  starting transfers between devices  9.44 us (4%)
  matrix products  8.95 us (4%)
  waiting for transfers between devices  7.74 us (4%)
  other arithmetic  7.13 us (3%)
    pallas_call x1, Pallas kernels, reduce_all(): pl.pallas_call(reduce_kernel, out_shape=(jax.ShapeDtypeStruct((per + 8, 1...  84.9 us
    pallas_call x1, Pallas kernels, body(): pl.pallas_call(functools.partial(weights_kernel, count, steps), grid=(ste...  30.3 us
    pallas_call x1, Pallas kernels, body(): pl.pallas_call(gather_kernel, grid=(shards,), out_shape=jax.ShapeDtypeStr...  24.3 us
    pallas_call x1, Pallas kernels, body(): pl.pallas_call(segment_kernel, grid=(shards // 4,), out_shape=jax.ShapeDt...  12.7 us
    pallas_call x1, Pallas kernels, body(): pl.pallas_call(values_kernel, grid=(steps,), out_shape=jax.ShapeDtypeStru...  12.4 us
    all_to_all x1, starting transfers between devices, body(): lax.all_to_all(bucket, 'dp', split_axis=0, concat_axis=0, tiled=True)  9.44 us
    all_to_all x1, waiting for transfers between devices, body(): lax.all_to_all(bucket, 'dp', split_axis=0, concat_axis=0, tiled=True)  7.74 us
    dot_general x1, matrix products, body(): jnp.dot(cross_in, weight_down, preferred_element_type=f32).astype(bf16)  6.06 us
  transfers between devices with their start and end apart: 1, of which 1 were waited for; matrix products, arithmetic and copies ran while one was open for 3% of the time, Pallas kernels for 14%

profile of v2, /device:TPU:1, one launch (start us, length us, event | category | flops | bytes accessed | tf_op | source)
XLA Modules:
  0.0 217.8 jit_solution(3003796102508565048)
XLA Ops:
  0.6 1.3 reshape.60.bias
  2.0 5.4 %index_kernel.1 = (s32[32,256]{1,0:T(8,128)}, f32[32,256]{1,0:T(8,128)}) custom-call(s32[26,512]{1,0:T(8,128)} %bitcast.26), custom_call_target="tpu_custom_call" | custom-call | tf_op jit(solution)/shard_map/index_kernel/pallas_call | solution.py:498
  7.4 1.4 reshape.66.row
  8.8 6.1 %convolution_convert_fusion.hidden = bf16[512,512]{1,0:T(8,128)(2,1)} fusion(bf16[512,3456]{1,0:T(8,128)(2,1)} %cross.1, bf16[3456,512]{1,0:T(8,128)(2,1)} %down.1), kind=kOutput, calls=%fused_computation.3 | convolution fusion | flops 1812201472 | bytes 7602176 | tf_op jit(solution)/shard_map/dot_general | solution.py:508
  14.9 2.9 %fusion.1.back_low = bf16[512,512]{1,0:T(8,128)(2,1)} fusion(bf16[512,3456]{1,0:T(8,128)(2,1)S(1)} %copy-done.3, bf16[512,3456]{1,0:T(8,128)(2,1)S(1)} %copy-done.2, bf16[512,3456]{1,0:T(8,128)(2,1)S(1)} %copy-done.1), kind=kOutput, calls=%fused_computation.2 | convolution fusion | flops 1819279360 | bytes 11141120 | tf_op jit(solution)/shard_map/dot_general | solution.py:510
  17.8 12.4 %values_kernel.1.values = f32[27,512,128]{2,1,0:T(8,128)} custom-call(bf16[512,512]{1,0:T(8,128)(2,1)} %convolution_convert_fusion.hidden, bf16[512,512]{1,0:T(8,128)(2,1)} %fusion.1.back_low, bf16[512,3456]{1,0:T(8,128)(2,1)} %cot.3, bf16[512,3456]{1,0:T(8,128)(2,1)} %up.1, bf16[3456,512]{1,0:T(8,128)(2,1)} %down.1, f32[1,3456]{1,0:T(1,128)} %reshape.60.bias), custom_call_target="tpu_custom_call" | custom-call | tf_op jit(solution)/shard_map/values_kernel/pallas_call | solution.py:514
  30.2 24.3 %gather_kernel.1 = f32[32,216,128]{2,1,0:T(8,128)} custom-call(s32[32,256]{1,0:T(8,128)} %get-tuple-element.16.idx, f32[13824,128]{1,0:T(8,128)} %bitcast.22, f32[32,1,256]{2,1,0:T(1,128)} %reshape.66.row), custom_call_target="tpu_custom_call" | custom-call | tf_op jit(solution)/shard_map/gather_kernel/pallas_call | solution.py:531
  54.5 9.4 %all-to-all-start = ((f32[32,216,128]{2,1,0:T(8,128)}), f32[32,216,128]{2,1,0:T(8,128)S(1)}, u32[]{:S(2)}, u32[]{:S(2)}) async-start(f32[32,216,128]{2,1,0:T(8,128)} %gather_kernel.1), calls=%async_computation | async-start | bytes 7077888 | tf_op jit(solution)/shard_map/all_to_all | solution.py:545
  64.0 1.5 concatenate.3
  65.5 1.5 reshape.61.place
  66.9 30.3 %weights_kernel.1 = (f32[28672,128]{1,0:T(8,128)}, f32[1,3456]{1,0:T(1,128)}) custom-call(bf16[512,512]{1,0:T(8,128)(2,1)} %convolution_convert_fusion.hidden, bf16[512,512]{1,0:T(8,128)(2,1)} %fusion.1.back_low, bf16[512,3456]{1,0:T(8,128)(2,1)} %cross.1, bf16[512,3456]{1,0:T(8,128)(2,1)} %cot.3, f32[27,512,128]{2,1,0:T(8,128)} %values_kernel.1.values, ...), custom_call_target="tpu_custom_call" | custom-call | tf_op jit(solution)/shard_map/weights_kernel/pallas_call | solution.py:549
  97.3 0.7 reduce.2
  98.0 0.8 reshape.63
  98.9 1.7 pad.5.clone
  100.5 7.7 %all-to-all-done.arrived = f32[32,216,128]{2,1,0:T(8,128)S(1)} async-done(((f32[32,216,128]{2,1,0:T(8,128)}), f32[32,216,128]{2,1,0:T(8,128)S(1)}, u32[]{:S(2)}, u32[]{:S(2)}) %all-to-all-start) | async-done | bytes 3538976 | tf_op jit(solution)/shard_map/all_to_all | solution.py:545
  108.3 1.8 copy-done
  110.0 12.7 %segment_kernel.1 = f32[2048,128]{1,0:T(8,128)} custom-call(f32[32,216,128]{2,1,0:T(8,128)} %copy-done), custom_call_target="tpu_custom_call" | custom-call | tf_op jit(solution)/shard_map/segment_kernel/pallas_call | solution.py:579
  122.8 84.9 %reduce_kernel.1 = (f32[232,128]{1,0:T(8,128)}, f32[4,4,2,4,8,128]{5,4,3,2,1,0:T(8,128)}, f32[4,512,128]{2,1,0:T(8,128)}) custom-call(f32[4,4,2,4,224,128]{5,4,3,2,1,0:T(8,128)} %bitcast.23, f32[4,4,2,4,8,128]{5,4,3,2,1,0:T(8,128)} %bitcast.25, f32[4,512,128]{2,1,0:T(8,128)} %bitcast.24), custom_call_target="tpu_custom_call" | custom-call | tf_op jit(solution)/shard_map/reduce_kernel/pallas_call | solution.py:465
  207.8 1.3 slice_bitcast_fusion
  209.1 0.9 fusion.4
  211.3 1.3 multiply_reduce_fusion.1
  212.7 1.6 multiply_reduce_fusion
  215.5 1.0 fusion.3
  216.5 1.3 fusion.2
  (23 shorter events, 2.7 us)
Async XLA Ops:
  8.8 6.1 %copy-start.1 = (bf16[512,3456]{1,0:T(8,128)(2,1)S(1)}, bf16[512,3456]{1,0:T(8,128)(2,1)}, u32[]{:S(2)}) copy-start(bf16[512,3456]{1,0:T(8,128)(2,1)} %cot.3) | copy-start | bytes 10616836
  8.8 6.1 %copy-start.2 = (bf16[512,3456]{1,0:T(8,128)(2,1)S(1)}, bf16[512,3456]{1,0:T(8,128)(2,1)}, u32[]{:S(2)}) copy-start(bf16[512,3456]{1,0:T(8,128)(2,1)} %cross.1) | copy-start | bytes 10616836
  8.8 6.2 %copy-start.3 = (bf16[512,3456]{1,0:T(8,128)(2,1)S(1)}, bf16[512,3456]{1,0:T(8,128)(2,1)}, u32[]{:S(2)}) copy-start(bf16[512,3456]{1,0:T(8,128)(2,1)} %up.1) | copy-start | bytes 10616836
  54.5 53.7 %all-to-all-start = ((f32[32,216,128]{2,1,0:T(8,128)}), f32[32,216,128]{2,1,0:T(8,128)S(1)}, u32[]{:S(2)}, u32[]{:S(2)}) async-start(f32[32,216,128]{2,1,0:T(8,128)} %gather_kernel.1), calls=%async_computation | async-start | bytes 7077888 | tf_op jit(solution)/shard_map/all_to_all | solution.py:545
  108.3 1.8 copy-start
  207.7 6.6 %copy-start.7 = (f32[1024]{0:T(1024)S(1)}, f32[1024]{0:T(1024)}, u32[]{:S(2)}) copy-start(f32[1024]{0:T(1024)} %param.17) | copy-start | bytes 12292
  207.7 7.2 %copy-start.6 = (f32[2048]{0:T(1024)S(1)}, f32[2048]{0:T(1024)}, u32[]{:S(2)}) copy-start(f32[2048]{0:T(1024)} %param.19) | copy-start | bytes 24580
  207.8 7.7 %copy-start.5 = (f32[1024,128]{1,0:T(8,128)S(1)}, f32[1024,128]{1,0:T(8,128)}, u32[]{:S(2)}) copy-start(f32[1024,128]{1,0:T(8,128)} %param.16) | copy-start | bytes 1572868
  207.8 8.7 %copy-start.4 = (f32[2048,128]{1,0:T(8,128)S(1)}, f32[2048,128]{1,0:T(8,128)}, u32[]{:S(2)}) copy-start(f32[2048,128]{1,0:T(8,128)} %param.18) | copy-start | bytes 3145732

commit v3 on v2

--- a/solution.py
+++ b/solution.py
@@ -35,7 +35,7 @@
     return jnp.where(flags, 1.0, 0.0).astype(bf16)
 
 
-def index_kernel(frequent, owned, place, idx, row, hot, cum):
+def index_work(frequent, owned, place, idx, row_a, row_b, hot, cum):
     tables, samples = place.shape
     owners, slots = idx.shape
     at = lax.broadcasted_iota(i32, (1, samples), 1)
@@ -70,32 +70,88 @@
         left = jnp.concatenate(parts, axis=0).astype(bf16)
         total = total + dot_nt(left, one_hot(slot_iota == rank))
     idx[...] = (total[:owners] * 128.0 + total[owners : 2 * owners]).astype(i32)
-    row[...] = (total[2 * owners : 3 * owners] - 1.0) * 128.0 + total[3 * owners :]
-
-
-def values_kernel(hidden, back_low, cot, up, down, bias, out):
-    scaled = jnp.dot(hidden[...], up[...], preferred_element_type=f32) + bias[...]
-    back = dot_nt(back_low[...], down[...])
-    v = cot[...].astype(f32) * (scaled + 1.0) + back
-    for k in range(out.shape[0]):
-        out[k] = v[:, k * 128 : (k + 1) * 128]
-
-
-def gather_kernel(idx, values, row, out):
-    o = pl.program_id(0)
-    slots = out.shape[1] - 8
-
-    def step(i, _):
-        at = pl.multiple_of(i * 16, 16)
-        for k in range(16):
-            src = idx[o, at + k]
-            out[0, pl.ds(at + k, 1), :] = values[pl.ds(src, 1), :]
+    row = (total[2 * owners : 3 * owners] - 1.0) * 128.0 + total[3 * owners :]
+    row_a[...] = row[:, :128]
+    row_b[...] = row[:, 128:]
+
+
+def front_kernel(
+    frequent, owned, place, bias, cross_hbm, cot_hbm, down_hbm, up_hbm,
+    hidden, back_low, values_hbm, bucket_hbm,
+    cross, cot, down, up, values, bucket, hot, cum, idx_v, row_a, row_b, idx, h_acc, b_acc, in_sems, v_sems, b_sems, i_sem,
+):
+    samples = hidden.shape[0]
+    emb = values.shape[1]
+    steps = in_sems.shape[0]
+    wide = cross.shape[1] // steps
+    per = wide // emb
+    owners = bucket.shape[0]
+    slots = bucket.shape[1] - 8
+
+    def loads(g):
+        cols = pl.ds(pl.multiple_of(g * wide, wide), wide)
+        return [
+            pltpu.make_async_copy(cross_hbm.at[:, cols], cross.at[:, cols], in_sems.at[g, 0]),
+            pltpu.make_async_copy(cot_hbm.at[:, cols], cot.at[:, cols], in_sems.at[g, 1]),
+            pltpu.make_async_copy(down_hbm.at[cols, :], down.at[cols, :], in_sems.at[g, 2]),
+            pltpu.make_async_copy(up_hbm.at[:, cols], up.at[:, cols], in_sems.at[g, 3]),
+        ]
+
+    for g in range(steps):
+        for c in loads(g):
+            c.start()
+    index_work(frequent, owned, place, idx_v, row_a, row_b, hot, cum)
+    to_scalar = pltpu.make_async_copy(idx_v, idx, i_sem)
+    to_scalar.start()
+    h_acc[...] = jnp.zeros_like(h_acc)
+    b_acc[...] = jnp.zeros_like(b_acc)
+
+    def low(g, _):
+        for c in loads(g):
+            c.wait()
+        cols = pl.ds(pl.multiple_of(g * wide, wide), wide)
+        x = cross[:, cols]
+        inner = (cot[:, cols].astype(f32) * x.astype(f32)).astype(bf16)
+        h_acc[...] += jnp.dot(x, down[cols, :], preferred_element_type=f32)
+        b_acc[...] += dot_nt(inner, up[:, cols])
         return 0
 
-    lax.fori_loop(0, slots // 16, step, 0)
-    out[0, slots : slots + 8, :] = jnp.zeros((8, 128), f32)
-    out[0, slots : slots + 1, :] = row[0, :, 0:128]
-    out[0, slots + 1 : slots + 2, :] = row[0, :, 128:256]
+    lax.fori_loop(0, steps, low, 0)
+    hidden[...] = h_acc[...].astype(bf16)
+    back_low[...] = b_acc[...].astype(bf16)
+
+    def store(g):
+        part = pl.ds(pl.multiple_of(g * per * samples, 128), per * samples)
+        return pltpu.make_async_copy(values.at[part], values_hbm.at[part], v_sems.at[g])
+
+    def high(g, _):
+        cols = pl.ds(pl.multiple_of(g * wide, wide), wide)
+        scaled = jnp.dot(hidden[...], up[:, cols], preferred_element_type=f32) + bias[:, cols]
+        v = cot[:, cols].astype(f32) * (scaled + 1.0) + dot_nt(back_low[...], down[cols, :])
+        for k in range(per):
+            values[pl.ds(pl.multiple_of((g * per + k) * samples, 128), samples), :] = v[:, k * emb : (k + 1) * emb]
+        store(g).start()
+        return 0
+
+    lax.fori_loop(0, steps, high, 0)
+    to_scalar.wait()
+
+    def ship(o):
+        return pltpu.make_async_copy(bucket.at[o], bucket_hbm.at[o], b_sems.at[o])
+
+    def pick(o, _):
+        for k in range(slots):
+            src = idx[o, k]
+            bucket[o, k : k + 1, :] = values[pl.ds(src, 1), :]
+        bucket[o, slots : slots + 8, :] = jnp.zeros((8, emb), f32)
+        bucket[o, slots : slots + 1, :] = row_a[pl.ds(o, 1), :]
+        bucket[o, slots + 1 : slots + 2, :] = row_b[pl.ds(o, 1), :]
+        ship(o).start()
+        return 0
+
+    lax.fori_loop(0, owners, pick, 0)
+    lax.fori_loop(0, steps, lambda g, _: (store(g).wait(), 0)[1], 0)
+    lax.fori_loop(0, owners, lambda o, _: (ship(o).wait(), 0)[1], 0)
 
 
 def weights_kernel(count, steps, hidden, back_low, cross, cot, values, place, both, bias, freq, hidden_t, down, up):
@@ -495,53 +551,42 @@
     vmem = pl.BlockSpec(memory_space=pltpu.VMEM)
 
     place_t = row_place.T
-    idx, row = pl.pallas_call(
-        functools.partial(index_kernel, f_count, owned),
-        out_shape=(jax.ShapeDtypeStruct((shards, 256), i32), jax.ShapeDtypeStruct((shards, 256), f32)),
-        in_specs=[vmem],
-        out_specs=(vmem, vmem),
-        scratch_shapes=[pltpu.VMEM((tables * shards, samples), bf16), pltpu.VMEM((tables * shards, samples), f32)],
+    anyw = pl.BlockSpec(memory_space=pl.ANY)
+    hidden, back_low, values, bucket = pl.pallas_call(
+        functools.partial(front_kernel, f_count, owned),
+        out_shape=(
+            jax.ShapeDtypeStruct((samples, rank), bf16),
+            jax.ShapeDtypeStruct((samples, rank), bf16),
+            jax.ShapeDtypeStruct((blocks * samples, emb), f32),
+            jax.ShapeDtypeStruct((shards, capacity + 8, emb), f32),
+        ),
+        in_specs=[vmem, vmem, anyw, anyw, anyw, anyw],
+        out_specs=(vmem, vmem, anyw, anyw),
+        scratch_shapes=[
+            pltpu.VMEM((samples, width), bf16),
+            pltpu.VMEM((samples, width), bf16),
+            pltpu.VMEM((width, rank), bf16),
+            pltpu.VMEM((rank, width), bf16),
+            pltpu.VMEM((blocks * samples, emb), f32),
+            pltpu.VMEM((shards, capacity + 8, emb), f32),
+            pltpu.VMEM((tables * shards, samples), bf16),
+            pltpu.VMEM((tables * shards, samples), f32),
+            pltpu.VMEM((shards, 256), i32),
+            pltpu.VMEM((shards, 128), f32),
+            pltpu.VMEM((shards, 128), f32),
+            pltpu.SMEM((shards, 256), i32),
+            pltpu.VMEM((samples, rank), f32),
+            pltpu.VMEM((samples, rank), f32),
+            pltpu.SemaphoreType.DMA((steps, 4)),
+            pltpu.SemaphoreType.DMA((steps,)),
+            pltpu.SemaphoreType.DMA((shards,)),
+            pltpu.SemaphoreType.DMA,
+        ],
         compiler_params=params(),
-        name="index_kernel",
-    )(place_t)
-
-    hidden = jnp.dot(cross_in, weight_down, preferred_element_type=f32).astype(bf16)
-    inner = cotangent.astype(f32) * cross_in.astype(f32)
-    back_low = lax.dot_general(
-        inner.astype(bf16), weight_up, (((1,), (1,)), ((), ())), preferred_element_type=f32
-    ).astype(bf16)
-
-    values = pl.pallas_call(
-        values_kernel,
-        grid=(steps,),
-        out_shape=jax.ShapeDtypeStruct((blocks, samples, emb), f32),
-        in_specs=[
-            pl.BlockSpec((samples, rank), lambda g: (0, 0)),
-            pl.BlockSpec((samples, rank), lambda g: (0, 0)),
-            pl.BlockSpec((samples, wide), lambda g: (0, g)),
-            pl.BlockSpec((rank, wide), lambda g: (0, g)),
-            pl.BlockSpec((wide, rank), lambda g: (g, 0)),
-            pl.BlockSpec((1, wide), lambda g: (0, g)),
-        ],
-        out_specs=pl.BlockSpec((per, samples, emb), lambda g: (g, 0, 0)),
-        compiler_params=params(),
-        name="values_kernel",
-    )(hidden, back_low, cotangent, weight_up, weight_down, cross_bias.reshape(1, -1))
-
-    bucket = pl.pallas_call(
-        gather_kernel,
-        grid=(shards,),
-        out_shape=jax.ShapeDtypeStruct((shards, capacity + 8, emb), f32),
-        in_specs=[
-            pl.BlockSpec(memory_space=pltpu.SMEM),
-            pl.BlockSpec((blocks * samples, emb), lambda g: (0, 0)),
-            pl.BlockSpec((1, 1, 256), lambda g: (g, 0, 0)),
-        ],
-        out_specs=pl.BlockSpec((1, capacity + 8, emb), lambda g: (g, 0, 0)),
-        compiler_params=params(),
-        name="gather_kernel",
-    )(idx, values.reshape(blocks * samples, emb), row.reshape(shards, 1, 256))
-
+        name="front_kernel",
+    )(place_t, cross_bias.reshape(1, -1), cross_in, cotangent, weight_down, weight_up)
+
+    values = values.reshape(blocks, samples, emb)
     arrived = lax.all_to_all(bucket, "dp", split_axis=0, concat_axis=0, tiled=True)
 
     place3 = jnp.concatenate([jnp.full((1, samples), -1, i32), place_t], axis=0).reshape(steps, per, samples)

time: 219 us -> 194 us (0.89)
  Pallas kernels: 170 us -> 156 us
  matrix products: 8.95 us -> 0 us
    pallas_call x3 -> x1, Pallas kernels: 42.1 us -> 27.6 us  [body(): pl.pallas_call(functools.partial(front_kernel, f_count, owned), out_shape...]
    dot_general x2 -> x0, matrix products: 8.95 us -> none  [the longest x1 6.06 us: body(): jnp.dot(cross_in, weight_down, preferred_element_type=f32).astype(bf16)]
  transfers between devices with their start and end apart: 1 -> 1, of which waited for: 1 -> 1; matrix products, arithmetic and copies ran while one was open for 3% -> 3% of each run, Pallas kernels for 14% -> 16%
where the time goes in v3:
time: 194 us; the launch traced here: 193 us
  Pallas kernels  156 us (80%)
  local copies, waits for them, and re-layouts  12.2 us (6%)
  starting transfers between devices  9.45 us (5%)
  waiting for transfers between devices  7.76 us (4%)
  other arithmetic  7.13 us (4%)
    pallas_call x1, Pallas kernels, reduce_all(): pl.pallas_call(reduce_kernel, out_shape=(jax.ShapeDtypeStruct((per + 8, 1...  84.9 us
    pallas_call x1, Pallas kernels, body(): pl.pallas_call(functools.partial(weights_kernel, count, steps), grid=(ste...  30.3 us
    pallas_call x1, Pallas kernels, body(): pl.pallas_call(functools.partial(front_kernel, f_count, owned), out_shape...  27.6 us
    pallas_call x1, Pallas kernels, body(): pl.pallas_call(segment_kernel, grid=(shards // 4,), out_shape=jax.ShapeDt...  12.7 us
    all_to_all x1, starting transfers between devices, body(): lax.all_to_all(bucket, 'dp', split_axis=0, concat_axis=0, tiled=True)  9.45 us
    all_to_all x1, waiting for transfers between devices, body(): lax.all_to_all(bucket, 'dp', split_axis=0, concat_axis=0, tiled=True)  7.76 us
  transfers between devices with their start and end apart: 1, of which 1 were waited for; matrix products, arithmetic and copies ran while one was open for 3% of the time, Pallas kernels for 16%

profile of v3, /device:TPU:1, one launch (start us, length us, event | category | flops | bytes accessed | tf_op | source)
XLA Modules:
  0.0 192.9 jit_solution(7770596288597275203)
XLA Ops:
  0.6 1.3 reshape.57.bias
  2.0 27.6 %front_kernel.1 = (bf16[512,512]{1,0:T(8,128)(2,1)}, bf16[512,512]{1,0:T(8,128)(2,1)}, f32[13824,128]{1,0:T(8,128)}, f32[32,216,128]{2,1,0:T(8,128)}) custom-call(s32[26,512]{1,0:T(8,128)} %bitcast.23, f32[1,3456]{1,0:T(1,128)} %reshape.57.bias, bf16[512,3456]{1,0:T(8,128)(2,1)} %cross.1, bf16[512,3456]{1,0:T(8,128)(2,1)} %cot.1, ...), custom_call_target="tpu_custom_call" | custom-call | tf_op jit(solution)/shard_map/front_kernel/pallas_call | solution.py:555
  29.5 9.4 %all-to-all-start = ((f32[32,216,128]{2,1,0:T(8,128)}), f32[32,216,128]{2,1,0:T(8,128)S(1)}, u32[]{:S(2)}, u32[]{:S(2)}) async-start(f32[32,216,128]{2,1,0:T(8,128)} %get-tuple-element.21), calls=%async_computation | async-start | bytes 7077888 | tf_op jit(solution)/shard_map/all_to_all | solution.py:590
  39.0 1.5 concatenate.3
  40.5 1.5 reshape.59.place
  42.0 30.3 %weights_kernel.1 = (f32[28672,128]{1,0:T(8,128)}, f32[1,3456]{1,0:T(1,128)}) custom-call(bf16[512,512]{1,0:T(8,128)(2,1)} %get-tuple-element.16.hidden, bf16[512,512]{1,0:T(8,128)(2,1)} %get-tuple-element.17.back_low, bf16[512,3456]{1,0:T(8,128)(2,1)} %cross.1, bf16[512,3456]{1,0:T(8,128)(2,1)} %cot.1, f32[27,512,128]{2,1,0:T(8,128)} %bitcast.20, ...), custom_call_target="tpu_custom_call" | custom-call | tf_op jit(solution)/shard_map/weights_kernel/pallas_call | solution.py:594
  72.3 0.7 reduce.2
  73.1 0.8 reshape.61
  73.9 1.7 pad.5.clone
  75.6 7.8 %all-to-all-done.arrived = f32[32,216,128]{2,1,0:T(8,128)S(1)} async-done(((f32[32,216,128]{2,1,0:T(8,128)}), f32[32,216,128]{2,1,0:T(8,128)S(1)}, u32[]{:S(2)}, u32[]{:S(2)}) %all-to-all-start) | async-done | bytes 3538976 | tf_op jit(solution)/shard_map/all_to_all | solution.py:590
  83.3 1.8 copy-done
  85.1 12.7 %segment_kernel.1 = f32[2048,128]{1,0:T(8,128)} custom-call(f32[32,216,128]{2,1,0:T(8,128)} %copy-done), custom_call_target="tpu_custom_call" | custom-call | tf_op jit(solution)/shard_map/segment_kernel/pallas_call | solution.py:624
  97.8 84.9 %reduce_kernel.1 = (f32[232,128]{1,0:T(8,128)}, f32[4,4,2,4,8,128]{5,4,3,2,1,0:T(8,128)}, f32[4,512,128]{2,1,0:T(8,128)}) custom-call(f32[4,4,2,4,224,128]{5,4,3,2,1,0:T(8,128)} %bitcast.19, f32[4,4,2,4,8,128]{5,4,3,2,1,0:T(8,128)} %bitcast.22, f32[4,512,128]{2,1,0:T(8,128)} %bitcast.21), custom_call_target="tpu_custom_call" | custom-call | tf_op jit(solution)/shard_map/reduce_kernel/pallas_call | solution.py:521
  182.8 1.3 slice_bitcast_fusion
  184.1 0.9 fusion.2
  185.0 0.6 reshape.65
  185.7 0.6 reshape.64
  186.3 1.3 multiply_reduce_fusion.1
  187.6 0.1 div.34
  187.7 1.6 multiply_reduce_fusion
  189.3 0.6 sqrt_add_fusion.1
  189.9 0.6 sqrt_add_fusion
  190.5 1.0 fusion.1
  191.6 1.3 fusion
  (12 shorter events, 0.1 us)
Async XLA Ops:
  29.5 53.8 %all-to-all-start = ((f32[32,216,128]{2,1,0:T(8,128)}), f32[32,216,128]{2,1,0:T(8,128)S(1)}, u32[]{:S(2)}, u32[]{:S(2)}) async-start(f32[32,216,128]{2,1,0:T(8,128)} %get-tuple-element.21), calls=%async_computation | async-start | bytes 7077888 | tf_op jit(solution)/shard_map/all_to_all | solution.py:590
  83.3 1.8 copy-start
  182.8 6.6 %copy-start.4 = (f32[1024]{0:T(1024)S(1)}, f32[1024]{0:T(1024)}, u32[]{:S(2)}) copy-start(f32[1024]{0:T(1024)} %param.17) | copy-start | bytes 12292
  182.8 7.2 %copy-start.3 = (f32[2048]{0:T(1024)S(1)}, f32[2048]{0:T(1024)}, u32[]{:S(2)}) copy-start(f32[2048]{0:T(1024)} %param.19) | copy-start | bytes 24580
  182.8 7.7 %copy-start.2 = (f32[1024,128]{1,0:T(8,128)S(1)}, f32[1024,128]{1,0:T(8,128)}, u32[]{:S(2)}) copy-start(f32[1024,128]{1,0:T(8,128)} %param.16) | copy-start | bytes 1572868
  182.8 8.7 %copy-start.1 = (f32[2048,128]{1,0:T(8,128)S(1)}, f32[2048,128]{1,0:T(8,128)}, u32[]{:S(2)}) copy-start(f32[2048,128]{1,0:T(8,128)} %param.18) | copy-start | bytes 3145732

commit v4 on v3

--- a/solution.py
+++ b/solution.py
@@ -154,125 +154,17 @@
     lax.fori_loop(0, owners, lambda o, _: (ship(o).wait(), 0)[1], 0)
 
 
-def weights_kernel(count, steps, hidden, back_low, cross, cot, values, place, both, bias, freq, hidden_t, down, up):
-    g = pl.program_id(0)
-    rank = hidden.shape[1]
-    wide = cross.shape[1]
-    per = wide // 128
-    frequent = freq.shape[0]
-    block = both.shape[0] // count
-    up_rows = rank // count
-    width = wide * steps
-    down_rows = width // count
-
-    @pl.when(g == 0)
-    def _():
-        hidden_t[...] = hidden[...].T
-        freq[...] = jnp.zeros_like(freq)
-
-    inner = cot[...].astype(f32) * cross[...].astype(f32)
-    bias[...] = jnp.sum(inner, axis=0, keepdims=True)
-    u = jnp.dot(hidden_t[...], inner.astype(bf16), preferred_element_type=f32)
-    for k in range(per):
-        up[k * rank : (k + 1) * rank, :] = u[:, k * 128 : (k + 1) * 128]
-    d = dot_tn(cross[...], back_low[...])
-    for k in range(rank // 128):
-        down[pl.ds(pl.multiple_of(k * width + g * wide, 128), wide), :] = d[:, k * 128 : (k + 1) * 128]
-    row_iota = lax.broadcasted_iota(i32, (frequent, 512), 0)
-    for k in range(per):
-        hot = one_hot(row_iota == place[0, k : k + 1, :])
-        s = jnp.dot(hot, hi_lo(values[k]), preferred_element_type=f32)
-        freq[...] += s[:, :128] + s[:, 128:]
-
-    cols = per * steps
-
-    def put_up(i, _):
-        for k in range(per):
-            both[pl.ds(i * block + g * per + k, up_rows, stride=cols), :] = up[
-                pl.ds(k * rank + i * up_rows, up_rows), :
-            ]
-        return 0
-
-    lax.fori_loop(0, count, put_up, 0)
-
-    @pl.when(g == steps - 1)
-    def _():
-        def put_down(i, _):
-            for k in range(rank // 128):
-                both[pl.ds(i * block + up_rows * cols + k, down_rows, stride=rank // 128), :] = down[
-                    pl.ds(k * width + i * down_rows, down_rows), :
-                ]
-            both[pl.ds(i * block + block - 8, 8), :] = freq[pl.ds(pl.multiple_of(i * 8, 8), 8), :]
-            return 0
-
-        lax.fori_loop(0, count, put_down, 0)
-
-
-def segment_kernel(arrived, out, acc):
-    g = pl.program_id(0)
-    owned = out.shape[0]
-    slots = arrived.shape[1] - 8
-
-    @pl.when(g == 0)
-    def _():
-        acc[...] = jnp.zeros_like(acc)
-
-    hots, parts = [], []
-    for b in range(arrived.shape[0]):
-        r0 = arrived[b, slots : slots + 1, :]
-        r1 = arrived[b, slots + 1 : slots + 2, : slots - 128]
-        hots.append(jnp.concatenate([r0, r1], axis=1).astype(i32))
-        parts.append(hi_lo(arrived[b, :slots, :]))
-    rows = jnp.concatenate(hots, axis=1)
-    right = jnp.concatenate(parts, axis=0)
-    step = 512
-    for m in range(0, owned, step):
-        hot = one_hot(lax.broadcasted_iota(i32, (step, rows.shape[1]), 0) + m == rows)
-        acc[m : m + step, :] += jnp.dot(hot, right, preferred_element_type=f32)
-
-    @pl.when(g == pl.num_programs(0) - 1)
-    def _():
-        out[...] = acc[:, :128] + acc[:, 128:]
-
-
 PORT = ((0, 96, 48, "xzy"), (96, 96, 48, "zxy"), (192, 40, 24, "yxz"))
 
 
-def params(**kw):
-    return pltpu.CompilerParams(vmem_limit_bytes=VLIM, **kw)
-
-
-def reduce_kernel(both, bias, seg, mine, freq_out, seg_out, *scratch):
-    n_port = len(PORT)
-    it = iter(scratch)
-    work = [next(it) for _ in PORT]
-    pair = [next(it) for _ in PORT]
-    land = [[[next(it) for _ in range(4)] for _ in range(3)] for _ in PORT]
-    swork = next(it)
-    sland = [next(it) for _ in range(4)]
-    sgath = next(it)
-    gath = next(it)
-    send_sems, recv_sems, local_sems = next(it), next(it), next(it)
-
+def mesh_place():
     dp, y = lax.axis_index("dp"), lax.axis_index("rep")
-    me = {"x": dp // 8, "z": (dp // 2) % 4, "y": y}
     core = dp % 2
-
-    def device(axis, to):
-        at = dict(me, **{axis: to})
-        return ((at["x"] * 4 + at["z"]) * 2 + core, at["y"])
-
-    partner = (dp + 1 - 2 * core, y)
-    up = {a: (me[a] + 1) % 4 for a in "xzy"}
-    down = {a: (me[a] + 3) % 4 for a in "xzy"}
-    far = {a: (me[a] + 2) % 4 for a in "xzy"}
-    peers = [partner] + [device(a, s[a]) for a in "xzy" for s in (up, down)]
-    barrier = pltpu.get_barrier_semaphore()
-    for peer in peers:
-        pl.semaphore_signal(barrier, inc=1, device_id=peer, device_id_type=pl.DeviceIdType.MESH)
-    pl.semaphore_wait(barrier, len(peers))
-
-    sent, used = [], [0]
+    return {"x": dp // 8, "z": (dp // 2) % 4, "y": y}, core, (dp + 1 - 2 * core, y)
+
+
+def sender(send_sems, recv_sems, sent):
+    used = [0]
 
     def send(src, dst, to):
         k = used[0]
@@ -284,6 +176,166 @@
         copy.start()
         sent.append(copy)
         return copy
+
+    return send
+
+
+def weights_kernel(steps, hidden, back_low, cross, cot, values_hbm, place, *rest):
+    outs, rest = rest[: len(PORT)], rest[len(PORT) :]
+    pair, rest = rest[: len(PORT)], rest[len(PORT) :]
+    both, freq, hidden_t, down, up, bias, values, send_sems, recv_sems, local_sems = rest
+    g = pl.program_id(0)
+    rank = hidden.shape[1]
+    wide = cross.shape[1]
+    per = wide // 128
+    frequent = freq.shape[0]
+    samples = hidden.shape[0]
+    count = frequent // 8
+    width = wide * steps
+    cols = per * steps
+    up_rows = rank // count
+    down_rows = width // count
+    base = up_rows * cols
+    freq_at = base + down_rows * rank // 128
+    _, core, partner = mesh_place()
+    load = pltpu.make_async_copy(values_hbm, values, local_sems.at[0])
+
+    @pl.when(g == 0)
+    def _():
+        barrier = pltpu.get_barrier_semaphore()
+        pl.semaphore_signal(barrier, inc=1, device_id=partner, device_id_type=pl.DeviceIdType.MESH)
+        pl.semaphore_wait(barrier, 1)
+        load.start()
+        hidden_t[...] = hidden[...].T
+        freq[...] = jnp.zeros_like(freq)
+
+    inner = cot[...].astype(f32) * cross[...].astype(f32)
+    bias[:, pl.ds(pl.multiple_of(g * wide, wide), wide)] = jnp.sum(inner, axis=0, keepdims=True)
+    u = jnp.dot(hidden_t[...], inner.astype(bf16), preferred_element_type=f32)
+    for k in range(per):
+        up[k * rank : (k + 1) * rank, :] = u[:, k * 128 : (k + 1) * 128]
+    d = dot_tn(cross[...], back_low[...])
+    for k in range(rank // 128):
+        down[pl.ds(pl.multiple_of(k * width + g * wide, 128), wide), :] = d[:, k * 128 : (k + 1) * 128]
+
+    def put_up(n, _):
+        for c in range(2):
+            for y in range(4):
+                i = n * 8 + c * 4 + y
+                for k in range(per):
+                    both[n, c, y, pl.ds(g * per + k, up_rows, stride=cols), :] = up[
+                        pl.ds(k * rank + i * up_rows, up_rows), :
+                    ]
+        return 0
+
+    lax.fori_loop(0, count // 8, put_up, 0)
+
+    @pl.when(g == steps - 1)
+    def _():
+        sent = []
+        send = sender(send_sems, recv_sems, sent)
+
+        def part(p, c):
+            first, rows = PORT[p][0], PORT[p][1]
+            return both.at[:, c, :, pl.ds(first, rows), :]
+
+        got = [send(part(0, 1 - core), pair[0], partner)]
+
+        def put_down(n, _):
+            for c in range(2):
+                for y in range(4):
+                    i = n * 8 + c * 4 + y
+                    for k in range(rank // 128):
+                        both[n, c, y, pl.ds(base + k, down_rows, stride=rank // 128), :] = down[
+                            pl.ds(k * width + i * down_rows, down_rows), :
+                        ]
+                    both[n, c, y, freq_at + 8 : freq_at + 16, :] = jnp.zeros((8, 128), f32)
+            return 0
+
+        lax.fori_loop(0, count // 8, put_down, 0)
+        got.append(send(part(1, 1 - core), pair[1], partner))
+        for i in range(count):
+            both[i // 8, (i // 4) % 2, i % 4, freq_at + 8 : freq_at + 9, 0:down_rows] = bias[
+                :, i * down_rows : (i + 1) * down_rows
+            ]
+        load.wait()
+        row_iota = lax.broadcasted_iota(i32, (frequent, samples), 0)
+
+        def tables(t, _):
+            hots, parts = [], []
+            for k in range(2):
+                hots.append(one_hot(row_iota == place[2 * t + k]))
+                parts.append(hi_lo(values[pl.ds(pl.multiple_of((2 * t + k + 1) * samples, 128), samples), :]))
+            s = jnp.dot(jnp.concatenate(hots, axis=1), jnp.concatenate(parts, axis=0), preferred_element_type=f32)
+            freq[...] += s[:, :128] + s[:, 128:]
+            return 0
+
+        lax.fori_loop(0, place.shape[0] // 2, tables, 0)
+
+        def put_freq(n, _):
+            for c in range(2):
+                for y in range(4):
+                    both[n, c, y, freq_at : freq_at + 8, :] = freq[
+                        pl.ds(pl.multiple_of((n * 8 + c * 4 + y) * 8, 8), 8), :
+                    ]
+            return 0
+
+        lax.fori_loop(0, count // 8, put_freq, 0)
+        got.append(send(part(2, 1 - core), pair[2], partner))
+        stores = []
+        for p, (first, rows, half, order) in enumerate(PORT):
+            got[p].wait_recv()
+
+            def add(n, _):
+                for y in range(4):
+                    both[n, core, y, first : first + rows, :] = (
+                        both[n, core, y, first : first + rows, :] + pair[p][n, y]
+                    )
+                return 0
+
+            lax.fori_loop(0, count // 8, add, 0)
+            stores.append(pltpu.make_async_copy(part(p, core), outs[p], local_sems.at[1 + p]))
+            stores[-1].start()
+        for c in stores:
+            c.wait()
+        for c in sent:
+            c.wait_send()
+
+
+def params(**kw):
+    return pltpu.CompilerParams(vmem_limit_bytes=VLIM, **kw)
+
+
+def reduce_kernel(*refs):
+    n_port = len(PORT)
+    it = iter(refs)
+    loads = [next(it) for _ in PORT]
+    arrived, mine, freq_out, seg_out = next(it), next(it), next(it), next(it)
+    work = [next(it) for _ in PORT]
+    land = [[[next(it) for _ in range(4)] for _ in range(3)] for _ in PORT]
+    swork = next(it)
+    sland = [next(it) for _ in range(4)]
+    sgath = next(it)
+    gath = next(it)
+    ids, right, acc = next(it), next(it), next(it)
+    send_sems, recv_sems, local_sems = next(it), next(it), next(it)
+    me, core, partner = mesh_place()
+
+    def device(axis, to):
+        at = dict(me, **{axis: to})
+        return ((at["x"] * 4 + at["z"]) * 2 + core, at["y"])
+
+    up = {a: (me[a] + 1) % 4 for a in "xzy"}
+    down = {a: (me[a] + 3) % 4 for a in "xzy"}
+    far = {a: (me[a] + 2) % 4 for a in "xzy"}
+    peers = [partner] + [device(a, s[a]) for a in "xzy" for s in (up, down)]
+    barrier = pltpu.get_barrier_semaphore()
+    for peer in peers:
+        pl.semaphore_signal(barrier, inc=1, device_id=peer, device_id_type=pl.DeviceIdType.MESH)
+    pl.semaphore_wait(barrier, len(peers))
+
+    sent = []
+    send = sender(send_sems, recv_sems, sent)
 
     def place(done, axis, t, rem=None):
         rem = iter(rem) if rem is not None else None
@@ -378,32 +430,40 @@
             if self.c3 is not None:
                 self.c3.wait_recv()
 
-    firsts, locals_ = [], []
-    for p, (first, rows, half, order) in enumerate(PORT):
-        whole = rows if p < n_port - 1 else rows - 8
-        got = [
-            send(
-                both.at[:, :, 1 - core, :, pl.ds(first, whole), :],
-                pair[p].at[:, :, :, pl.ds(0, whole), :],
-                partner,
+    copies = [pltpu.make_async_copy(loads[p], work[p], local_sems.at[p]) for p in range(n_port)]
+    for c in copies:
+        c.start()
+    owned = swork.shape[1]
+    slots = arrived.shape[1] - 8
+    some = ids.shape[0]
+    each_of = arrived.shape[0] // some
+    chunk = each_of * slots
+
+    def prepare(g, _):
+        rows = []
+        for b in range(each_of):
+            n = g * each_of + b
+            rows.append(arrived[n, slots : slots + 1, :])
+            rows.append(arrived[n, slots + 1 : slots + 2, : slots - 128])
+            right[pl.ds(pl.multiple_of(n * slots, 16), slots), :] = hi_lo(arrived[n, :slots, :])
+        ids[g] = jnp.concatenate(rows, axis=1).astype(i32)
+        return 0
+
+    def seg_block(t):
+        acc[...] = jnp.zeros_like(acc)
+        first = t * owned
+
+        def one(g, _):
+            hot = one_hot(lax.broadcasted_iota(i32, (owned, chunk), 0) + first == ids[g])
+            acc[...] += jnp.dot(
+                hot, right[pl.ds(pl.multiple_of(g * chunk, 16), chunk), :], preferred_element_type=f32
             )
-        ]
-        loc = [pltpu.make_async_copy(
-            both.at[:, :, core, :, pl.ds(first, whole), :], work[p].at[:, :, :, pl.ds(0, whole), :], local_sems.at[p])]
-        if p == n_port - 1:
-            got.append(send(bias.at[:, :, 1 - core], pair[p].at[:, :, :, pl.ds(whole, 8), :], partner))
-            loc.append(pltpu.make_async_copy(
-                bias.at[:, :, core], work[p].at[:, :, :, pl.ds(whole, 8), :], local_sems.at[n_port]))
-        for c in loc:
-            c.start()
-        firsts.append(got)
-        locals_.append(loc)
-    load = pltpu.make_async_copy(seg, swork, local_sems.at[n_port + 1])
-    load.start()
-    load.wait()
-    owned = swork.shape[1]
+            return 0
+
+        lax.fori_loop(0, some, one, 0)
+        swork[t] = acc[:, :128] + acc[:, 128:]
+
     s_red = Reduce(swork, None, "y", owned, owned // 2, sland, 0)
-    s_red.start()
 
     reds = []
     for p, (first, rows, half, order) in enumerate(PORT):
@@ -412,20 +472,6 @@
             phases.append(Reduce(work[p], order[:k], order[k], rows, half, land[p][k], 2 - k))
         reds.append(phases)
 
-    def begin(p):
-        for c in locals_[p]:
-            c.wait()
-        for c in firsts[p]:
-            c.wait_recv()
-
-        def one(i, _):
-            w = (i // 16, (i // 4) % 4, i % 4)
-            work[p][w] = work[p][w] + pair[p][w]
-            return 0
-
-        lax.fori_loop(0, 64, one, 0)
-        reds[p][0].start()
-
     def s_half(t, h):
         if h is None:
             return sgath.at[t]
@@ -445,13 +491,19 @@
     g_y, g_z, g_x = Gather("y", y_at), Gather("z", z_at), Gather("x", x_at)
     here = (me["x"], me["z"], me["y"])
 
-    begin(2)
-    begin(0)
-    begin(1)
-    s_red.middle()
+    lax.fori_loop(0, some, prepare, 0)
+    for p in (2, 0, 1):
+        copies[p].wait()
+        reds[p][0].start()
+    seg_block(far["y"])
+    s_red.start()
     reds[2][0].middle()
+    seg_block(up["y"])
     reds[0][0].middle()
     reds[1][0].middle()
+    seg_block(down["y"])
+    s_red.middle()
+    seg_block(me["y"])
     reds[2][0].finish()
     reds[2][1].start()
     s_red.finish()
@@ -500,37 +552,39 @@
         c.wait_send()
 
 
-def reduce_scratch(owned):
+def reduce_scratch(owned, arrived):
     v = lambda *s: pltpu.VMEM(s, f32)
-    out = [v(4, 4, 4, r, 128) for _, r, _, _ in PORT] * 2
+    out = [v(4, 4, 4, r, 128) for _, r, _, _ in PORT]
     for _, r, h, _ in PORT:
         for k in range(3):
             lead = (4,) * (2 - k)
             out += [v(*lead, h, 128), v(*lead, r - h, 128), v(*lead, r, 128), v(*lead, r, 128)]
     out += [v(4, owned // 4, 128), v(owned // 8, 128), v(owned // 8, 128), v(owned // 4, 128), v(owned // 4, 128), v(4, owned // 4, 128)]
     out += [v(4, 4, 2, 4, 8, 128)]
+    n = arrived.shape[0] // 4
+    flat = arrived.shape[0] * (arrived.shape[1] - 8)
+    out += [pltpu.VMEM((n, 1, flat // n), i32), pltpu.VMEM((flat, 256), bf16), v(owned // 4, 256)]
     out += [pltpu.SemaphoreType.DMA((80,)), pltpu.SemaphoreType.DMA((80,)), pltpu.SemaphoreType.DMA((8,))]
     return out
 
 
-def reduce_all(both, bias, seg):
-    owned = seg.shape[0]
-    per = both.shape[0] // 128
+def reduce_all(parts, arrived, owned):
     vmem = pl.BlockSpec(memory_space=pltpu.VMEM)
     anyw = pl.BlockSpec(memory_space=pl.ANY)
+    total = PORT[-1][0] + PORT[-1][1]
     mine, freq, seg = pl.pallas_call(
         reduce_kernel,
         out_shape=(
-            jax.ShapeDtypeStruct((per + 8, 128), f32),
+            jax.ShapeDtypeStruct((total, 128), f32),
             jax.ShapeDtypeStruct((4, 4, 2, 4, 8, 128), f32),
             jax.ShapeDtypeStruct((4, owned // 4, 128), f32),
         ),
-        in_specs=[anyw, anyw, anyw],
+        in_specs=[anyw] * len(PORT) + [vmem],
         out_specs=(vmem, vmem, vmem),
-        scratch_shapes=reduce_scratch(owned),
+        scratch_shapes=reduce_scratch(owned, arrived),
         compiler_params=params(collective_id=0, has_side_effects=True),
         name="reduce_kernel",
-    )(both.reshape(4, 4, 2, 4, per, 128), bias.reshape(4, 4, 2, 4, 8, 128), seg.reshape(4, owned // 4, 128))
+    )(*[w.reshape(4, 4, 4, w.shape[2], 128) for w in parts], arrived)
     return mine, freq.reshape(1024, 128), seg.reshape(owned, 128)
 
 
@@ -586,56 +640,43 @@
         name="front_kernel",
     )(place_t, cross_bias.reshape(1, -1), cross_in, cotangent, weight_down, weight_up)
 
-    values = values.reshape(blocks, samples, emb)
     arrived = lax.all_to_all(bucket, "dp", split_axis=0, concat_axis=0, tiled=True)
 
-    place3 = jnp.concatenate([jnp.full((1, samples), -1, i32), place_t], axis=0).reshape(steps, per, samples)
-    block = rank * width // count // 128 * 2 + f_count // count
-    both, bias = pl.pallas_call(
-        functools.partial(weights_kernel, count, steps),
+    parts = pl.pallas_call(
+        functools.partial(weights_kernel, steps),
         grid=(steps,),
-        out_shape=(
-            jax.ShapeDtypeStruct((count * block, 128), f32),
-            jax.ShapeDtypeStruct((1, width), f32),
-        ),
+        out_shape=tuple(jax.ShapeDtypeStruct((16, 4, r, 128), f32) for _, r, _, _ in PORT),
         in_specs=[
             pl.BlockSpec((samples, rank), lambda g: (0, 0)),
             pl.BlockSpec((samples, rank), lambda g: (0, 0)),
             pl.BlockSpec((samples, wide), lambda g: (0, g)),
             pl.BlockSpec((samples, wide), lambda g: (0, g)),
-            pl.BlockSpec((per, samples, emb), lambda g: (g, 0, 0)),
-            pl.BlockSpec((1, per, samples), lambda g: (g, 0, 0)),
+            anyw,
+            pl.BlockSpec((tables, 1, samples), lambda g: (0, 0, 0)),
         ],
-        out_specs=(
-            pl.BlockSpec((count * block, 128), lambda g: (0, 0)),
-            pl.BlockSpec((1, wide), lambda g: (0, g)),
-        ),
-        scratch_shapes=[
+        out_specs=(anyw,) * len(PORT),
+        scratch_shapes=[pltpu.VMEM((16, 4, r, 128), f32) for _, r, _, _ in PORT]
+        + [
+            pltpu.VMEM((16, 2, 4, PORT[-1][0] + PORT[-1][1], 128), f32),
             pltpu.VMEM((f_count, emb), f32),
             pltpu.VMEM((rank, samples), bf16),
             pltpu.VMEM((rank // 128 * width, 128), f32),
             pltpu.VMEM((per * rank, 128), f32),
+            pltpu.VMEM((1, width), f32),
+            pltpu.VMEM((blocks * samples, emb), f32),
+            pltpu.SemaphoreType.DMA((len(PORT),)),
+            pltpu.SemaphoreType.DMA((len(PORT),)),
+            pltpu.SemaphoreType.DMA((1 + len(PORT),)),
         ],
-        compiler_params=params(),
+        compiler_params=params(collective_id=1, has_side_effects=True),
         name="weights_kernel",
-    )(hidden, back_low, cross_in, cotangent, values, place3)
-    bias = jnp.pad(bias.reshape(count, 1, width // count), ((0, 0), (0, 7), (0, 128 - width // count)))
-
-    shard_grad = pl.pallas_call(
-        segment_kernel,
-        grid=(shards // 4,),
-        out_shape=jax.ShapeDtypeStruct((owned, emb), f32),
-        in_specs=[pl.BlockSpec((4, capacity + 8, emb), lambda g: (g, 0, 0))],
-        out_specs=pl.BlockSpec((owned, emb), lambda g: (0, 0)),
-        scratch_shapes=[pltpu.VMEM((owned, 256), f32)],
-        compiler_params=params(),
-        name="segment_kernel",
-    )(arrived)
-    mine, freq, shard_grad = reduce_all(both, bias, shard_grad)
+    )(hidden, back_low, cross_in, cotangent, values, place_t.reshape(tables, 1, samples))
+
+    mine, freq, shard_grad = reduce_all(parts, arrived, owned)
     n = rank * width // count // 128
     grad_up = mine[:n].reshape(rank // count, width)
     grad_down = mine[n : 2 * n].reshape(width // count, rank)
-    grad_bias = mine[block, : width // count]
+    grad_bias = mine[2 * n + f_count // count, : width // count]
     new_shard, new_shard_accum = row_adagrad(shard_table, shard_accum, shard_grad)
     new_frequent, new_frequent_accum = row_adagrad(frequent_table, frequent_accum, freq)
     return (new_frequent, new_frequent_accum, new_shard, new_shard_accum, grad_up, grad_down, grad_bias)

time: 194 us -> 171 us (0.88)
  Pallas kernels: 156 us -> 129 us
  waiting for transfers between devices: 7.76 us -> 16.3 us
  local copies, waits for them, and re-layouts: 12.2 us -> 8.21 us
    pallas_call x3 -> x2, Pallas kernels: 128 us -> 102 us  [the longest x1 75.3 us: reduce_all(): pl.pallas_call(reduce_kernel, out_shape=(jax.ShapeDtypeStruct((total, 128...]
    all_to_all x1, waiting for transfers between devices: 7.76 us -> 16.3 us  [body(): lax.all_to_all(bucket, 'dp', split_axis=0, concat_axis=0, tiled=True)]
  transfers between devices with their start and end apart: 1 -> 1, of which waited for: 1 -> 1; matrix products, arithmetic and copies ran while one was open for 3% -> 1% of each run, Pallas kernels for 16% -> 16%
where the time goes in v4:
time: 171 us
  Pallas kernels  129 us (75%)
  waiting for transfers between devices  16.3 us (10%)
  starting transfers between devices  9.45 us (6%)
  local copies, waits for them, and re-layouts  8.21 us (5%)
  other arithmetic  6.38 us (4%)
    pallas_call x1, Pallas kernels, reduce_all(): pl.pallas_call(reduce_kernel, out_shape=(jax.ShapeDtypeStruct((total, 128...  75.3 us
    pallas_call x1, Pallas kernels, body(): pl.pallas_call(functools.partial(front_kernel, f_count, owned), out_shape...  27.6 us
    pallas_call x1, Pallas kernels, body(): pl.pallas_call(functools.partial(weights_kernel, steps), grid=(steps,), o...  26.5 us
    all_to_all x1, waiting for transfers between devices, body(): lax.all_to_all(bucket, 'dp', split_axis=0, concat_axis=0, tiled=True)  16.3 us
    all_to_all x1, starting transfers between devices, body(): lax.all_to_all(bucket, 'dp', split_axis=0, concat_axis=0, tiled=True)  9.45 us
  transfers between devices with their start and end apart: 1, of which 1 were waited for; matrix products, arithmetic and copies ran while one was open for 1% of the time, Pallas kernels for 16%

profile of v4, /device:TPU:1, one launch (start us, length us, event | category | flops | bytes accessed | tf_op | source)
XLA Modules:
  0.0 170.5 jit_solution(15237628364268596378)
XLA Ops:
  0.6 1.3 reshape.51.bias
  2.0 27.6 %front_kernel.1 = (bf16[512,512]{1,0:T(8,128)(2,1)}, bf16[512,512]{1,0:T(8,128)(2,1)}, f32[13824,128]{1,0:T(8,128)}, f32[32,216,128]{2,1,0:T(8,128)}) custom-call(s32[26,512]{1,0:T(8,128)} %bitcast.20, f32[1,3456]{1,0:T(1,128)} %reshape.51.bias, bf16[512,3456]{1,0:T(8,128)(2,1)} %cross.1, bf16[512,3456]{1,0:T(8,128)(2,1)} %cot.1, ...), custom_call_target="tpu_custom_call" | custom-call | tf_op jit(solution)/shard_map/front_kernel/pallas_call | solution.py:609
  29.6 9.4 %all-to-all-start = ((f32[32,216,128]{2,1,0:T(8,128)}), f32[32,216,128]{2,1,0:T(8,128)S(1)}, u32[]{:S(2)}, u32[]{:S(2)}) async-start(f32[32,216,128]{2,1,0:T(8,128)} %get-tuple-element.23), calls=%async_computation | async-start | bytes 7077888 | tf_op jit(solution)/shard_map/all_to_all | solution.py:643
  39.0 1.5 reshape.52.place
  40.5 26.5 %weights_kernel.1 = (f32[16,4,96,128]{3,2,1,0:T(8,128)}, f32[16,4,96,128]{3,2,1,0:T(8,128)}, f32[16,4,40,128]{3,2,1,0:T(8,128)}) custom-call(bf16[512,512]{1,0:T(8,128)(2,1)} %get-tuple-element.17.hidden, bf16[512,512]{1,0:T(8,128)(2,1)} %get-tuple-element.18.back_low, bf16[512,3456]{1,0:T(8,128)(2,1)} %cross.1, bf16[512,3456]{1,0:T(8,128)(2,1)} %cot.1, ...), custom_call_target="tpu_custom_call" | custom-call | tf_op jit(solution)/shard_map/weights_kernel/pallas_call | solution.py:645
  67.1 16.3 %all-to-all-done.refs_3_ = f32[32,216,128]{2,1,0:T(8,128)S(1)} async-done(((f32[32,216,128]{2,1,0:T(8,128)}), f32[32,216,128]{2,1,0:T(8,128)S(1)}, u32[]{:S(2)}, u32[]{:S(2)}) %all-to-all-start) | async-done | bytes 3538976 | tf_op jit(solution)/shard_map/all_to_all | solution.py:643
  83.3 1.7 %copy-done = f32[32,216,128]{2,1,0:T(8,128)} copy-done((f32[32,216,128]{2,1,0:T(8,128)}, f32[32,216,128]{2,1,0:T(8,128)S(1)}, u32[]{:S(2)}) %copy-start) | copy-done | bytes 3538968
  85.1 75.3 %reduce_kernel.1 = (f32[232,128]{1,0:T(8,128)}, f32[4,4,2,4,8,128]{5,4,3,2,1,0:T(8,128)}, f32[4,512,128]{2,1,0:T(8,128)}) custom-call(f32[4,4,4,96,128]{4,3,2,1,0:T(8,128)} %bitcast.17, f32[4,4,4,96,128]{4,3,2,1,0:T(8,128)} %bitcast.18, f32[4,4,4,40,128]{4,3,2,1,0:T(8,128)} %bitcast.19, f32[32,216,128]{2,1,0:T(8,128)} %copy-done), custom_call_target="tpu_custom_call" | custom-call | tf_op jit(solution)/shard_map/reduce_kernel/pallas_call | solution.py:575
  160.4 0.0 copy-start.4
  160.4 0.0 copy-start.3
  160.4 0.0 copy-start.2
  160.4 0.0 copy-start.1
  160.5 1.3 slice_bitcast_fusion
  161.8 0.9 fusion.2
  162.7 0.6 reshape.57
  163.3 0.6 reshape.56
  164.0 1.3 multiply_reduce_fusion.1
  165.3 0.1 div.34
  165.4 1.6 multiply_reduce_fusion
  167.0 0.0 copy-done.4
  167.0 0.6 sqrt_add_fusion.1
  167.6 0.6 sqrt_add_fusion
  168.2 1.0 fusion.1
  169.2 1.3 fusion
  (7 shorter events, 0.0 us)
Async XLA Ops:
  29.6 53.8 %all-to-all-start = ((f32[32,216,128]{2,1,0:T(8,128)}), f32[32,216,128]{2,1,0:T(8,128)S(1)}, u32[]{:S(2)}, u32[]{:S(2)}) async-start(f32[32,216,128]{2,1,0:T(8,128)} %get-tuple-element.23), calls=%async_computation | async-start | bytes 7077888 | tf_op jit(solution)/shard_map/all_to_all | solution.py:643
  83.3 1.7 %copy-start = (f32[32,216,128]{2,1,0:T(8,128)}, f32[32,216,128]{2,1,0:T(8,128)S(1)}, u32[]{:S(2)}) copy-start(f32[32,216,128]{2,1,0:T(8,128)S(1)} %all-to-all-done.refs_3_) | copy-start | bytes 10616836
  160.4 6.6 %copy-start.4 = (f32[1024]{0:T(1024)S(1)}, f32[1024]{0:T(1024)}, u32[]{:S(2)}) copy-start(f32[1024]{0:T(1024)} %param.17) | copy-start | bytes 12292
  160.4 7.2 %copy-start.3 = (f32[2048]{0:T(1024)S(1)}, f32[2048]{0:T(1024)}, u32[]{:S(2)}) copy-start(f32[2048]{0:T(1024)} %param.19) | copy-start | bytes 24580
  160.4 7.8 %copy-start.2 = (f32[1024,128]{1,0:T(8,128)S(1)}, f32[1024,128]{1,0:T(8,128)}, u32[]{:S(2)}) copy-start(f32[1024,128]{1,0:T(8,128)} %param.16) | copy-start | bytes 1572868
  160.4 8.7 %copy-start.1 = (f32[2048,128]{1,0:T(8,128)S(1)}, f32[2048,128]{1,0:T(8,128)}, u32[]{:S(2)}) copy-start(f32[2048,128]{1,0:T(8,128)} %param.18) | copy-start | bytes 3145732

commit v5 on v4

--- a/solution.py
+++ b/solution.py
@@ -154,7 +154,7 @@
     lax.fori_loop(0, owners, lambda o, _: (ship(o).wait(), 0)[1], 0)
 
 
-PORT = ((0, 96, 48, "xzy"), (96, 96, 48, "zxy"), (192, 40, 24, "yxz"))
+PORT = ((72, 72, 40, "xzy"), (144, 80, 40, "zxy"), (0, 72, 40, "yxz"))
 
 
 def mesh_place():
@@ -180,9 +180,88 @@
     return send
 
 
+class Reduce:
+    def __init__(self, send, near, at, add, rows, half, lands):
+        self.send, self.near, self.at, self.add = send, near, at, add
+        self.rows, self.half, self.lands = rows, half, lands
+
+    def start(self):
+        (_, up, far, down), to = self.near
+        self.c0 = self.send(self.at(far, 0, self.half), self.lands[0], to[up])
+        self.c1 = self.send(self.at(far, self.half, self.rows), self.lands[1], to[down])
+
+    def middle(self):
+        (_, up, far, down), to = self.near
+        self.c0.wait_recv()
+        self.add(up, 0, self.half, self.lands[:1])
+        self.c2 = self.send(self.at(up, 0, self.rows), self.lands[2], to[up])
+        self.c1.wait_recv()
+        self.add(down, self.half, self.rows, self.lands[1:2])
+        self.c3 = self.send(self.at(down, 0, self.rows), self.lands[3], to[down])
+
+    def finish(self):
+        self.c2.wait_recv()
+        self.c3.wait_recv()
+        self.add(self.near[0][0], 0, self.rows, self.lands[2:4])
+
+
+class Direct:
+    def __init__(self, send, near, at, add, lands):
+        self.send, self.near, self.at, self.add, self.lands = send, near, at, add, lands
+
+    def start(self):
+        places, to = self.near
+        self.got = [self.send(self.at(places[d]), self.lands[d - 1], to[places[d]]) for d in (1, 3, 2)]
+
+    def finish(self):
+        for c in self.got:
+            c.wait_recv()
+        self.add(self.near[0][0], self.lands)
+
+
+class Spread:
+    def __init__(self, send, near, at):
+        self.send, self.near, self.at = send, near, at
+
+    def start(self):
+        places, to = self.near
+        src = self.at(places[0])
+        self.got = [self.send(src, src, to[places[d]]) for d in (1, 3, 2)]
+
+    def finish(self):
+        for c in self.got:
+            c.wait_recv()
+
+
+class Ids:
+    def __init__(self, make):
+        self.make = make
+
+    def __getitem__(self, t):
+        return self.make(t)
+
+
+def neighbours(me, core, axis):
+    def device(to):
+        at = dict(me, **{axis: to})
+        return ((at["x"] * 4 + at["z"]) * 2 + core, at["y"])
+
+    return [(me[axis] + d) % 4 for d in range(4)], Ids(device)
+
+
+def greet(peers):
+    barrier = pltpu.get_barrier_semaphore()
+    for peer in peers:
+        pl.semaphore_signal(barrier, inc=1, device_id=peer, device_id_type=pl.DeviceIdType.MESH)
+    pl.semaphore_wait(barrier, len(peers))
+
+
 def weights_kernel(steps, hidden, back_low, cross, cot, values_hbm, place, *rest):
     outs, rest = rest[: len(PORT)], rest[len(PORT) :]
+    freq_out, rest = rest[0], rest[1:]
     pair, rest = rest[: len(PORT)], rest[len(PORT) :]
+    y_land, rest = rest[:4], rest[4:]
+    f_both, f_pair, f_land, rest = rest[0], rest[1], rest[2:5], rest[5:]
     both, freq, hidden_t, down, up, bias, values, send_sems, recv_sems, local_sems = rest
     g = pl.program_id(0)
     rank = hidden.shape[1]
@@ -196,15 +275,14 @@
     up_rows = rank // count
     down_rows = width // count
     base = up_rows * cols
-    freq_at = base + down_rows * rank // 128
-    _, core, partner = mesh_place()
+    bias_at = base + down_rows * rank // 128
+    me, core, partner = mesh_place()
+    near = neighbours(me, core, "y")
     load = pltpu.make_async_copy(values_hbm, values, local_sems.at[0])
 
     @pl.when(g == 0)
     def _():
-        barrier = pltpu.get_barrier_semaphore()
-        pl.semaphore_signal(barrier, inc=1, device_id=partner, device_id_type=pl.DeviceIdType.MESH)
-        pl.semaphore_wait(barrier, 1)
+        greet([partner] + [near[1][t] for t in near[0][1:]])
         load.start()
         hidden_t[...] = hidden[...].T
         freq[...] = jnp.zeros_like(freq)
@@ -239,7 +317,7 @@
             first, rows = PORT[p][0], PORT[p][1]
             return both.at[:, c, :, pl.ds(first, rows), :]
 
-        got = [send(part(0, 1 - core), pair[0], partner)]
+        got = {2: send(part(2, 1 - core), pair[2], partner)}
 
         def put_down(n, _):
             for c in range(2):
@@ -249,15 +327,16 @@
                         both[n, c, y, pl.ds(base + k, down_rows, stride=rank // 128), :] = down[
                             pl.ds(k * width + i * down_rows, down_rows), :
                         ]
-                    both[n, c, y, freq_at + 8 : freq_at + 16, :] = jnp.zeros((8, 128), f32)
+                    both[n, c, y, bias_at : bias_at + 8, :] = jnp.zeros((8, 128), f32)
             return 0
 
         lax.fori_loop(0, count // 8, put_down, 0)
-        got.append(send(part(1, 1 - core), pair[1], partner))
         for i in range(count):
-            both[i // 8, (i // 4) % 2, i % 4, freq_at + 8 : freq_at + 9, 0:down_rows] = bias[
+            both[i // 8, (i // 4) % 2, i % 4, bias_at : bias_at + 1, 0:down_rows] = bias[
                 :, i * down_rows : (i + 1) * down_rows
             ]
+        for p in (0, 1):
+            got[p] = send(part(p, 1 - core), pair[p], partner)
         load.wait()
         row_iota = lax.broadcasted_iota(i32, (frequent, samples), 0)
 
@@ -270,20 +349,8 @@
             freq[...] += s[:, :128] + s[:, 128:]
             return 0
 
-        lax.fori_loop(0, place.shape[0] // 2, tables, 0)
-
-        def put_freq(n, _):
-            for c in range(2):
-                for y in range(4):
-                    both[n, c, y, freq_at : freq_at + 8, :] = freq[
-                        pl.ds(pl.multiple_of((n * 8 + c * 4 + y) * 8, 8), 8), :
-                    ]
-            return 0
-
-        lax.fori_loop(0, count // 8, put_freq, 0)
-        got.append(send(part(2, 1 - core), pair[2], partner))
-        stores = []
-        for p, (first, rows, half, order) in enumerate(PORT):
+        def add_pair(p):
+            first, rows = PORT[p][0], PORT[p][1]
             got[p].wait_recv()
 
             def add(n, _):
@@ -294,8 +361,60 @@
                 return 0
 
             lax.fori_loop(0, count // 8, add, 0)
+
+        first, rows, half, _ = PORT[2]
+
+        def y_at(t, lo, hi):
+            return both.at[:, core, t, pl.ds(first + lo, hi - lo), :]
+
+        def y_add(t, lo, hi, lands):
+            def add(n, _):
+                v = both[n, core, t, first + lo : first + hi, :]
+                for ref in lands:
+                    v = v + ref[n]
+                both[n, core, t, first + lo : first + hi, :] = v
+                return 0
+
+            lax.fori_loop(0, count // 8, add, 0)
+
+        def f_add(t, lands):
+            v = f_both[:, core, t]
+            for ref in lands:
+                v = v + ref[...]
+            f_both[:, core, t] = v
+
+        y_sum = Reduce(send, near, y_at, y_add, rows, half, y_land)
+        f_sum = Direct(send, near, lambda t: f_both.at[:, core, t], f_add, f_land)
+        pairs = place.shape[0] // 2
+        cut = pairs // 3
+        lax.fori_loop(0, cut, tables, 0)
+        add_pair(2)
+        y_sum.start()
+        lax.fori_loop(cut, pairs, tables, 0)
+        y_sum.middle()
+
+        def put_freq(n, _):
+            for c in range(2):
+                for y in range(4):
+                    f_both[n, c, y] = freq[pl.ds(pl.multiple_of((n * 8 + c * 4 + y) * 8, 8), 8), :]
+            return 0
+
+        lax.fori_loop(0, count // 8, put_freq, 0)
+        f_got = send(f_both.at[:, 1 - core], f_pair, partner)
+        stores = []
+        for p in (0, 1):
+            add_pair(p)
             stores.append(pltpu.make_async_copy(part(p, core), outs[p], local_sems.at[1 + p]))
             stores[-1].start()
+        f_got.wait_recv()
+        f_both[:, core] = f_both[:, core] + f_pair[...]
+        f_sum.start()
+        y_sum.finish()
+        stores.append(pltpu.make_async_copy(y_at(me["y"], 0, rows), outs[2], local_sems.at[3]))
+        stores[-1].start()
+        f_sum.finish()
+        stores.append(pltpu.make_async_copy(f_both.at[:, core, me["y"]], freq_out, local_sems.at[4]))
+        stores[-1].start()
         for c in stores:
             c.wait()
         for c in sent:
@@ -307,40 +426,25 @@
 
 
 def reduce_kernel(*refs):
-    n_port = len(PORT)
     it = iter(refs)
-    loads = [next(it) for _ in PORT]
-    arrived, mine, freq_out, seg_out = next(it), next(it), next(it), next(it)
-    work = [next(it) for _ in PORT]
-    land = [[[next(it) for _ in range(4)] for _ in range(3)] for _ in PORT]
-    swork = next(it)
-    sland = [next(it) for _ in range(4)]
-    sgath = next(it)
-    gath = next(it)
-    ids, right, acc = next(it), next(it), next(it)
-    send_sems, recv_sems, local_sems = next(it), next(it), next(it)
+    take = lambda n: [next(it) for _ in range(n)]
+    loads, (load_f, arrived), (mine, freq_out, seg_out) = take(3), take(2), take(3)
+    work = take(3)
+    land = {p: {k: take(4) for k in range(1 if p == 2 else 0, 3)} for p in range(3)}
+    swork, sland, sgath = next(it), take(4), next(it)
+    f_work, fx_land, fz_land, gath = next(it), take(3), take(3), next(it)
+    arr, ids, right, acc = take(4)
+    send_sems, recv_sems, local_sems = take(3)
     me, core, partner = mesh_place()
-
-    def device(axis, to):
-        at = dict(me, **{axis: to})
-        return ((at["x"] * 4 + at["z"]) * 2 + core, at["y"])
-
-    up = {a: (me[a] + 1) % 4 for a in "xzy"}
-    down = {a: (me[a] + 3) % 4 for a in "xzy"}
-    far = {a: (me[a] + 2) % 4 for a in "xzy"}
-    peers = [partner] + [device(a, s[a]) for a in "xzy" for s in (up, down)]
-    barrier = pltpu.get_barrier_semaphore()
-    for peer in peers:
-        pl.semaphore_signal(barrier, inc=1, device_id=peer, device_id_type=pl.DeviceIdType.MESH)
-    pl.semaphore_wait(barrier, len(peers))
-
+    near = {a: neighbours(me, core, a) for a in "xzy"}
+    greet([partner] + [near[a][1][t] for a in "xzy" for t in near[a][0][1:]])
     sent = []
     send = sender(send_sems, recv_sems, sent)
 
-    def place(done, axis, t, rem=None):
+    def where(dims, done, axis, t, rem=None):
         rem = iter(rem) if rem is not None else None
         out = []
-        for a in "xzy":
+        for a in dims:
             if a in done:
                 out.append(me[a])
             elif a == axis:
@@ -349,103 +453,98 @@
                 out.append(slice(None) if rem is None else next(rem))
         return tuple(out)
 
-    def each(n_rem, fn):
-        if n_rem == 0:
-            fn(())
-        elif n_rem == 1:
-            lax.fori_loop(0, 4, lambda i, _: (fn((i,)), 0)[1], 0)
-        else:
-            lax.fori_loop(0, 16, lambda i, _: (fn((i // 4, i % 4)), 0)[1], 0)
-
-    class Reduce:
-        def __init__(self, ref, done, axis, rows, half, lands, free=2):
-            self.ref, self.done, self.axis, self.rows, self.half, self.lands = ref, done, axis, rows, half, lands
-            self.n = free
-
-        def at(self, t, lo, hi):
-            if self.done is None:
-                return self.ref.at[t, pl.ds(lo, hi - lo), :]
-            return self.ref.at[place(self.done, self.axis, t) + (pl.ds(lo, hi - lo), slice(None))]
-
-        def add(self, t, lo, hi, *refs):
+    def phase(p, k):
+        _, rows, half, order = PORT[p]
+        dims = "xz" if p == 2 else "xzy"
+        done, axis = order[:k].replace("y", "") if p == 2 else order[:k], order[k]
+        ref, left = work[p], 2 - k
+
+        def at(t, lo, hi):
+            return ref.at[where(dims, done, axis, t) + (pl.ds(lo, hi - lo), slice(None))]
+
+        def add(t, lo, hi, lands):
             def one(rem):
-                if self.done is None:
-                    step = 128
-                    for r in range(lo, hi, step):
-                        v = self.ref[t, r : r + step, :]
-                        for ref in refs:
-                            v = v + ref[r - lo : r - lo + step, :]
-                        self.ref[t, r : r + step, :] = v
-                    return
-                where = place(self.done, self.axis, t, rem)
-                v = self.ref[where + (slice(lo, hi), slice(None))]
-                for ref in refs:
-                    v = v + ref[rem + (slice(None), slice(None))]
-                self.ref[where + (slice(lo, hi), slice(None))] = v
-
-            each(self.n, one)
-
+                spot = where(dims, done, axis, t, rem) + (slice(lo, hi), slice(None))
+                v = ref[spot]
+                for x in lands:
+                    v = v + x[rem + (slice(None), slice(None))]
+                ref[spot] = v
+
+            if left == 0:
+                one(())
+            elif left == 1:
+                lax.fori_loop(0, 4, lambda i, _: (one((i,)), 0)[1], 0)
+            else:
+                lax.fori_loop(0, 16, lambda i, _: (one((i // 4, i % 4)), 0)[1], 0)
+
+        return Reduce(send, near[axis], at, add, rows, half, land[p][k])
+
+    sums = {(p, k): phase(p, k) for p in range(3) for k in range(1 if p == 2 else 0, 3)}
+
+    owned = swork.shape[1]
+
+    def s_add(t, lo, hi, lands):
+        for r in range(lo, hi, 128):
+            v = swork[t, r : r + 128, :]
+            for ref in lands:
+                v = v + ref[r - lo : r - lo + 128, :]
+            swork[t, r : r + 128, :] = v
+
+    s_red = Reduce(
+        send, near["y"], lambda t, lo, hi: swork.at[t, pl.ds(lo, hi - lo), :], s_add, owned, owned // 2, sland
+    )
+
+    def f_add(spot, lands):
+        v = f_work[spot]
+        for ref in lands:
+            v = v + ref[...]
+        f_work[spot] = v
+
+    f_x = Direct(send, near["x"], lambda t: f_work.at[t], lambda t, l: f_add((t,), l), fx_land)
+    f_z = Direct(
+        send, near["z"], lambda t: f_work.at[me["x"], t], lambda t, l: f_add((me["x"], t), l), fz_land
+    )
+    g_z = Spread(send, near["z"], lambda t: gath.at[me["x"], t, core, me["y"]])
+    g_x = Spread(send, near["x"], lambda t: gath.at[t, :, core, me["y"]])
+    g_y = Spread(send, near["y"], lambda t: gath.at[:, :, core, t])
+
+    class SegGather:
         def start(self):
-            a = self.axis
-            self.c0 = send(self.at(far[a], 0, self.half), self.lands[0], device(a, up[a]))
-            self.c1 = send(self.at(far[a], self.half, self.rows), self.lands[1], device(a, down[a]))
+            (here, up, far, down), to = near["y"]
+            src = sgath.at[here]
+            self.c0, self.c1 = send(src, src, to[up]), send(src, src, to[down])
 
         def middle(self):
-            a = self.axis
+            (here, up, far, down), to = near["y"]
             self.c0.wait_recv()
-            self.add(up[a], 0, self.half, self.lands[0])
-            self.c2 = send(self.at(up[a], 0, self.rows), self.lands[2], device(a, up[a]))
+            src = sgath.at[down, pl.ds(0, owned // 2), :]
+            self.c2 = send(src, src, to[up])
             self.c1.wait_recv()
-            self.add(down[a], self.half, self.rows, self.lands[1])
-            self.c3 = send(self.at(down[a], 0, self.rows), self.lands[3], device(a, down[a]))
+            src = sgath.at[up, pl.ds(owned // 2, owned // 2), :]
+            self.c3 = send(src, src, to[down])
 
         def finish(self):
             self.c2.wait_recv()
             self.c3.wait_recv()
-            self.add(me[self.axis], 0, self.rows, self.lands[2], self.lands[3])
-
-    class Gather:
-        def __init__(self, axis, at):
-            self.axis, self.at = axis, at
-
-        def start(self):
-            a = self.axis
-            src = self.at(me[a], None)
-            self.c0 = send(src, src, device(a, up[a]))
-            self.c1 = send(src, src, device(a, down[a]))
-
-        def middle(self):
-            a = self.axis
-            self.c0.wait_recv()
-            src = self.at(down[a], 0)
-            self.c2 = send(src, src, device(a, up[a]))
-            self.c1.wait_recv()
-            src = self.at(up[a], 1)
-            self.c3 = None
-            if src is not None:
-                self.c3 = send(src, src, device(a, down[a]))
-
-        def finish(self):
-            self.c2.wait_recv()
-            if self.c3 is not None:
-                self.c3.wait_recv()
-
-    copies = [pltpu.make_async_copy(loads[p], work[p], local_sems.at[p]) for p in range(n_port)]
-    for c in copies:
+
+    s_gat = SegGather()
+    copies = [pltpu.make_async_copy(loads[p], work[p], local_sems.at[p]) for p in range(3)]
+    copy_f = pltpu.make_async_copy(load_f, f_work, local_sems.at[3])
+    copy_a = pltpu.make_async_copy(arrived, arr, local_sems.at[4])
+    for c in [copy_f, copies[0], copies[1], copy_a, copies[2]]:
         c.start()
-    owned = swork.shape[1]
-    slots = arrived.shape[1] - 8
+    slots = arr.shape[1] - 8
     some = ids.shape[0]
-    each_of = arrived.shape[0] // some
+    each_of = arr.shape[0] // some
     chunk = each_of * slots
 
     def prepare(g, _):
         rows = []
         for b in range(each_of):
             n = g * each_of + b
-            rows.append(arrived[n, slots : slots + 1, :])
-            rows.append(arrived[n, slots + 1 : slots + 2, : slots - 128])
-            right[pl.ds(pl.multiple_of(n * slots, 16), slots), :] = hi_lo(arrived[n, :slots, :])
+            rows.append(arr[n, slots : slots + 1, :])
+            rows.append(arr[n, slots + 1 : slots + 2, : slots - 128])
+            right[pl.ds(pl.multiple_of(n * slots, 16), slots), :] = hi_lo(arr[n, :slots, :])
         ids[g] = jnp.concatenate(rows, axis=1).astype(i32)
         return 0
 
@@ -463,115 +562,91 @@
         lax.fori_loop(0, some, one, 0)
         swork[t] = acc[:, :128] + acc[:, 128:]
 
-    s_red = Reduce(swork, None, "y", owned, owned // 2, sland, 0)
-
-    reds = []
-    for p, (first, rows, half, order) in enumerate(PORT):
-        phases = []
-        for k in range(3):
-            phases.append(Reduce(work[p], order[:k], order[k], rows, half, land[p][k], 2 - k))
-        reds.append(phases)
-
-    def s_half(t, h):
-        if h is None:
-            return sgath.at[t]
-        return sgath.at[t, pl.ds(h * (owned // 2), owned // 2), :]
-
-    s_gat = Gather("y", s_half)
-
-    def y_at(t, h):
-        return None if h == 1 else gath.at[me["x"], me["z"], core, t]
-
-    def z_at(t, h):
-        return gath.at[me["x"], t, core] if h is None else gath.at[me["x"], t, core, pl.ds(2 * h, 2)]
-
-    def x_at(t, h):
-        return gath.at[t, :, core] if h is None else gath.at[t, pl.ds(2 * h, 2), core]
-
-    g_y, g_z, g_x = Gather("y", y_at), Gather("z", z_at), Gather("x", x_at)
-    here = (me["x"], me["z"], me["y"])
-
+    _, y_up, y_far, y_down = near["y"][0]
+    copy_f.wait()
+    f_x.start()
+    copies[0].wait()
+    sums[0, 0].start()
+    copies[1].wait()
+    sums[1, 0].start()
+    copy_a.wait()
     lax.fori_loop(0, some, prepare, 0)
-    for p in (2, 0, 1):
-        copies[p].wait()
-        reds[p][0].start()
-    seg_block(far["y"])
+    f_x.finish()
+    f_z.start()
+    seg_block(y_far)
     s_red.start()
-    reds[2][0].middle()
-    seg_block(up["y"])
-    reds[0][0].middle()
-    reds[1][0].middle()
-    seg_block(down["y"])
+    copies[2].wait()
+    seg_block(y_up)
+    sums[0, 0].middle()
+    sums[1, 0].middle()
+    sums[2, 1].start()
+    seg_block(y_down)
     s_red.middle()
+    f_z.finish()
+    gath[me["x"], me["z"], core, me["y"]] = f_work[me["x"], me["z"]]
+    g_z.start()
     seg_block(me["y"])
-    reds[2][0].finish()
-    reds[2][1].start()
     s_red.finish()
     sgath[me["y"]] = swork[me["y"]]
     s_gat.start()
-    reds[2][1].middle()
-    reds[2][1].finish()
-    reds[2][2].start()
-    reds[2][2].middle()
-    reds[2][2].finish()
-    last = n_port - 1
-    rows_last = PORT[last][1]
-    gath[me["x"], me["z"], core, me["y"]] = work[last][here + (slice(rows_last - 16, rows_last - 8), slice(None))]
-    g_y.start()
-    s_gat.middle()
-    g_y.middle()
-    reds[0][0].finish()
-    reds[0][1].start()
-    reds[1][0].finish()
-    reds[1][1].start()
-    g_y.finish()
-    g_z.start()
-    s_gat.finish()
-    reds[0][1].middle()
-    reds[1][1].middle()
-    g_z.middle()
-    reds[0][1].finish()
-    reds[0][2].start()
-    reds[1][1].finish()
-    reds[1][2].start()
+    sums[0, 0].finish()
+    sums[0, 1].start()
+    sums[1, 0].finish()
+    sums[1, 1].start()
+    sums[2, 1].middle()
     g_z.finish()
     g_x.start()
-    reds[0][2].middle()
-    reds[1][2].middle()
-    g_x.middle()
-    reds[0][2].finish()
-    reds[1][2].finish()
+    s_gat.middle()
+    sums[0, 1].middle()
+    sums[1, 1].middle()
+    sums[2, 1].finish()
+    sums[2, 2].start()
     g_x.finish()
+    g_y.start()
+    sums[0, 1].finish()
+    sums[0, 2].start()
+    sums[1, 1].finish()
+    sums[1, 2].start()
+    s_gat.finish()
+    seg_out[...] = sgath[...]
+    sums[2, 2].middle()
+    g_y.finish()
     g_c = send(gath.at[:, :, core], gath.at[:, :, core], partner)
-    for p, (first, rows, half, order) in enumerate(PORT):
-        mine[first : first + rows, :] = work[p][here]
-    seg_out[...] = sgath[...]
+    sums[0, 2].middle()
+    sums[1, 2].middle()
     g_c.wait_recv()
     freq_out[...] = gath[...]
+    sums[2, 2].finish()
+    sums[0, 2].finish()
+    sums[1, 2].finish()
+    here = (me["x"], me["z"], me["y"])
+    for p, (first, rows, _, _) in enumerate(PORT):
+        mine[first : first + rows, :] = work[p][here[:2] if p == 2 else here]
     for c in sent:
         c.wait_send()
 
 
 def reduce_scratch(owned, arrived):
     v = lambda *s: pltpu.VMEM(s, f32)
-    out = [v(4, 4, 4, r, 128) for _, r, _, _ in PORT]
-    for _, r, h, _ in PORT:
-        for k in range(3):
+    out = [v(*((4, 4) if p == 2 else (4, 4, 4)), PORT[p][1], 128) for p in range(3)]
+    for p, (_, r, h, _) in enumerate(PORT):
+        for k in range(1 if p == 2 else 0, 3):
             lead = (4,) * (2 - k)
             out += [v(*lead, h, 128), v(*lead, r - h, 128), v(*lead, r, 128), v(*lead, r, 128)]
-    out += [v(4, owned // 4, 128), v(owned // 8, 128), v(owned // 8, 128), v(owned // 4, 128), v(owned // 4, 128), v(4, owned // 4, 128)]
-    out += [v(4, 4, 2, 4, 8, 128)]
+    q = owned // 4
+    out += [v(4, q, 128), v(q // 2, 128), v(q // 2, 128), v(q, 128), v(q, 128), v(4, q, 128)]
+    out += [v(4, 4, 8, 128)] + [v(4, 8, 128)] * 3 + [v(8, 128)] * 3 + [v(4, 4, 2, 4, 8, 128)]
     n = arrived.shape[0] // 4
     flat = arrived.shape[0] * (arrived.shape[1] - 8)
-    out += [pltpu.VMEM((n, 1, flat // n), i32), pltpu.VMEM((flat, 256), bf16), v(owned // 4, 256)]
-    out += [pltpu.SemaphoreType.DMA((80,)), pltpu.SemaphoreType.DMA((80,)), pltpu.SemaphoreType.DMA((8,))]
+    out += [v(*arrived.shape), pltpu.VMEM((n, 1, flat // n), i32), pltpu.VMEM((flat, 256), bf16), v(q, 256)]
+    out += [pltpu.SemaphoreType.DMA((64,)), pltpu.SemaphoreType.DMA((64,)), pltpu.SemaphoreType.DMA((8,))]
     return out
 
 
 def reduce_all(parts, arrived, owned):
     vmem = pl.BlockSpec(memory_space=pltpu.VMEM)
     anyw = pl.BlockSpec(memory_space=pl.ANY)
-    total = PORT[-1][0] + PORT[-1][1]
+    total = max(a + r for a, r, _, _ in PORT)
     mine, freq, seg = pl.pallas_call(
         reduce_kernel,
         out_shape=(
@@ -579,12 +654,12 @@
             jax.ShapeDtypeStruct((4, 4, 2, 4, 8, 128), f32),
             jax.ShapeDtypeStruct((4, owned // 4, 128), f32),
         ),
-        in_specs=[anyw] * len(PORT) + [vmem],
+        in_specs=[anyw] * (len(PORT) + 2),
         out_specs=(vmem, vmem, vmem),
         scratch_shapes=reduce_scratch(owned, arrived),
         compiler_params=params(collective_id=0, has_side_effects=True),
         name="reduce_kernel",
-    )(*[w.reshape(4, 4, 4, w.shape[2], 128) for w in parts], arrived)
+    )(*[w.reshape(4, 4, *w.shape[1:]) for w in parts], arrived)
     return mine, freq.reshape(1024, 128), seg.reshape(owned, 128)
 
 
@@ -645,7 +720,10 @@
     parts = pl.pallas_call(
         functools.partial(weights_kernel, steps),
         grid=(steps,),
-        out_shape=tuple(jax.ShapeDtypeStruct((16, 4, r, 128), f32) for _, r, _, _ in PORT),
+        out_shape=tuple(
+            jax.ShapeDtypeStruct(shape, f32)
+            for shape in ((16, 4, PORT[0][1], 128), (16, 4, PORT[1][1], 128), (16, PORT[2][1], 128), (16, 8, 128))
+        ),
         in_specs=[
             pl.BlockSpec((samples, rank), lambda g: (0, 0)),
             pl.BlockSpec((samples, rank), lambda g: (0, 0)),
@@ -654,19 +732,22 @@
             anyw,
             pl.BlockSpec((tables, 1, samples), lambda g: (0, 0, 0)),
         ],
-        out_specs=(anyw,) * len(PORT),
+        out_specs=(anyw,) * (len(PORT) + 1),
         scratch_shapes=[pltpu.VMEM((16, 4, r, 128), f32) for _, r, _, _ in PORT]
+        + [pltpu.VMEM((16, r, 128), f32) for r in (PORT[2][2], PORT[2][1] - PORT[2][2], PORT[2][1], PORT[2][1])]
+        + [pltpu.VMEM((16, 2, 4, 8, 128), f32), pltpu.VMEM((16, 4, 8, 128), f32)]
+        + [pltpu.VMEM((16, 8, 128), f32)] * 3
         + [
-            pltpu.VMEM((16, 2, 4, PORT[-1][0] + PORT[-1][1], 128), f32),
+            pltpu.VMEM((16, 2, 4, max(a + r for a, r, _, _ in PORT), 128), f32),
             pltpu.VMEM((f_count, emb), f32),
             pltpu.VMEM((rank, samples), bf16),
             pltpu.VMEM((rank // 128 * width, 128), f32),
             pltpu.VMEM((per * rank, 128), f32),
             pltpu.VMEM((1, width), f32),
             pltpu.VMEM((blocks * samples, emb), f32),
-            pltpu.SemaphoreType.DMA((len(PORT),)),
-            pltpu.SemaphoreType.DMA((len(PORT),)),
-            pltpu.SemaphoreType.DMA((1 + len(PORT),)),
+            pltpu.SemaphoreType.DMA((16,)),
+            pltpu.SemaphoreType.DMA((16,)),
+            pltpu.SemaphoreType.DMA((8,)),
         ],
         compiler_params=params(collective_id=1, has_side_effects=True),
         name="weights_kernel",
@@ -676,7 +757,7 @@
     n = rank * width // count // 128
     grad_up = mine[:n].reshape(rank // count, width)
     grad_down = mine[n : 2 * n].reshape(width // count, rank)
-    grad_bias = mine[2 * n + f_count // count, : width // count]
+    grad_bias = mine[2 * n, : width // count]
     new_shard, new_shard_accum = row_adagrad(shard_table, shard_accum, shard_grad)
     new_frequent, new_frequent_accum = row_adagrad(frequent_table, frequent_accum, freq)
     return (new_frequent, new_frequent_accum, new_shard, new_shard_accum, grad_up, grad_down, grad_bias)

time: 171 us -> 153 us (0.89); the launches traced: 171 us -> 150 us
  waiting for transfers between devices: 16.3 us -> 0.01 us
  Pallas kernels: 129 us -> 125 us
    pallas_call x1, Pallas kernels: 75.3 us -> 50.4 us  [reduce_all(): pl.pallas_call(reduce_kernel, out_shape=(jax.ShapeDtypeStruct((total, 128...]
    pallas_call x1, Pallas kernels: 26.5 us -> 47.4 us  [body(): pl.pallas_call(functools.partial(weights_kernel, steps), grid=(steps,), o...]
    all_to_all x1, waiting for transfers between devices: 16.3 us -> 0.01 us  [body(): lax.all_to_all(bucket, 'dp', split_axis=0, concat_axis=0, tiled=True)]
  transfers between devices with their start and end apart: 1 -> 1, of which waited for: 1 -> 0; matrix products, arithmetic and copies ran while one was open for 1% -> 1% of each run, Pallas kernels for 16% -> 32%
where the time goes in v5:
time: 153 us; the launch traced here: 150 us
  Pallas kernels  125 us (82%)
  starting transfers between devices  9.45 us (6%)
  local copies, waits for them, and re-layouts  8.2 us (5%)
  other arithmetic  6.38 us (4%)
    pallas_call x1, Pallas kernels, reduce_all(): pl.pallas_call(reduce_kernel, out_shape=(jax.ShapeDtypeStruct((total, 128...  50.4 us
    pallas_call x1, Pallas kernels, body(): pl.pallas_call(functools.partial(weights_kernel, steps), grid=(steps,), o...  47.4 us
    pallas_call x1, Pallas kernels, body(): pl.pallas_call(functools.partial(front_kernel, f_count, owned), out_shape...  27.6 us
    all_to_all x1, starting transfers between devices, body(): lax.all_to_all(bucket, 'dp', split_axis=0, concat_axis=0, tiled=True)  9.45 us
  transfers between devices with their start and end apart: 1, of which 0 were waited for; matrix products, arithmetic and copies ran while one was open for 1% of the time, Pallas kernels for 32%

profile of v5, /device:TPU:1, one launch (start us, length us, event | category | flops | bytes accessed | tf_op | source)
XLA Modules:
  0.0 150.2 jit_solution(6405496456559663738)
XLA Ops:
  0.6 1.3 reshape.54.bias
  2.0 27.6 %front_kernel.1 = (bf16[512,512]{1,0:T(8,128)(2,1)}, bf16[512,512]{1,0:T(8,128)(2,1)}, f32[13824,128]{1,0:T(8,128)}, f32[32,216,128]{2,1,0:T(8,128)}) custom-call(s32[26,512]{1,0:T(8,128)} %bitcast.21, f32[1,3456]{1,0:T(1,128)} %reshape.54.bias, bf16[512,3456]{1,0:T(8,128)(2,1)} %cross.1, bf16[512,3456]{1,0:T(8,128)(2,1)} %cot.1, ...), custom_call_target="tpu_custom_call" | custom-call | tf_op jit(solution)/shard_map/front_kernel/pallas_call | solution.py:684
  29.6 9.4 %all-to-all-start = ((f32[32,216,128]{2,1,0:T(8,128)}), f32[32,216,128]{2,1,0:T(8,128)S(1)}, u32[]{:S(2)}, u32[]{:S(2)}) async-start(f32[32,216,128]{2,1,0:T(8,128)} %get-tuple-element.25), calls=%async_computation | async-start | bytes 7077888 | tf_op jit(solution)/shard_map/all_to_all | solution.py:718
  39.0 1.5 reshape.55.place
  40.5 47.4 %weights_kernel.1 = (f32[16,4,72,128]{3,2,1,0:T(8,128)}, f32[16,4,80,128]{3,2,1,0:T(8,128)}, f32[16,72,128]{2,1,0:T(8,128)}, f32[16,8,128]{2,1,0:T(8,128)}) custom-call(bf16[512,512]{1,0:T(8,128)(2,1)} %get-tuple-element.18.hidden, bf16[512,512]{1,0:T(8,128)(2,1)} %get-tuple-element.19.back_low, bf16[512,3456]{1,0:T(8,128)(2,1)} %cross.1, ...), custom_call_target="tpu_custom_call" | custom-call | tf_op jit(solution)/shard_map/weights_kernel/pallas_call | solution.py:720
  88.0 0.0 all-to-all-done.refs_4_
  88.0 1.7 %copy-done = f32[32,216,128]{2,1,0:T(8,128)} copy-done((f32[32,216,128]{2,1,0:T(8,128)}, f32[32,216,128]{2,1,0:T(8,128)S(1)}, u32[]{:S(2)}) %copy-start) | copy-done | bytes 3538968
  89.7 50.4 %reduce_kernel.1 = (f32[224,128]{1,0:T(8,128)}, f32[4,4,2,4,8,128]{5,4,3,2,1,0:T(8,128)}, f32[4,512,128]{2,1,0:T(8,128)}) custom-call(f32[4,4,4,72,128]{4,3,2,1,0:T(8,128)} %bitcast.19, f32[4,4,4,80,128]{4,3,2,1,0:T(8,128)} %bitcast.18, f32[4,4,72,128]{3,2,1,0:T(8,128)} %bitcast.20, f32[4,4,8,128]{3,2,1,0:T(8,128)} %bitcast.23, f32[32,216,128]{2,1,0:T(8,128)} %copy-done), custom_call_target="tpu_custom_call" | custom-call | tf_op jit(solution)/shard_map/reduce_kernel/pallas_call | solution.py:650
  140.1 0.0 copy-start.4
  140.1 0.0 copy-start.3
  140.1 0.0 copy-start.2
  140.1 0.0 copy-start.1
  140.2 1.3 slice_bitcast_fusion
  141.5 0.9 fusion.2
  142.4 0.6 reshape.61
  143.0 0.6 reshape.60
  143.7 1.3 multiply_reduce_fusion.1
  145.0 0.1 div.34
  145.1 1.6 %multiply_reduce_fusion = (f32[4,512]{1,0:T(4,128)S(1)}, f32[4,512,128]{2,1,0:T(8,128)S(1)}) fusion(f32[4,512,128]{2,1,0:T(8,128)} %get-tuple-element.27), kind=kLoop, calls=%fused_computation.2 | loop fusion | flops 784384 | bytes 2105344 | tf_op jit(solution)/shard_map/reduce_sum | solution.py:16
  146.7 0.0 copy-done.4
  146.7 0.6 sqrt_add_fusion.1
  147.3 0.6 sqrt_add_fusion
  147.9 1.0 fusion.1
  148.9 1.3 fusion
  (7 shorter events, 0.0 us)
Async XLA Ops:
  29.6 58.4 %all-to-all-start = ((f32[32,216,128]{2,1,0:T(8,128)}), f32[32,216,128]{2,1,0:T(8,128)S(1)}, u32[]{:S(2)}, u32[]{:S(2)}) async-start(f32[32,216,128]{2,1,0:T(8,128)} %get-tuple-element.25), calls=%async_computation | async-start | bytes 7077888 | tf_op jit(solution)/shard_map/all_to_all | solution.py:718
  88.0 1.7 %copy-start = (f32[32,216,128]{2,1,0:T(8,128)}, f32[32,216,128]{2,1,0:T(8,128)S(1)}, u32[]{:S(2)}) copy-start(f32[32,216,128]{2,1,0:T(8,128)S(1)} %all-to-all-done.refs_4_) | copy-start | bytes 10616836
  140.1 6.6 %copy-start.4 = (f32[1024]{0:T(1024)S(1)}, f32[1024]{0:T(1024)}, u32[]{:S(2)}) copy-start(f32[1024]{0:T(1024)} %param.17) | copy-start | bytes 12292
  140.1 7.2 %copy-start.3 = (f32[2048]{0:T(1024)S(1)}, f32[2048]{0:T(1024)}, u32[]{:S(2)}) copy-start(f32[2048]{0:T(1024)} %param.19) | copy-start | bytes 24580
  140.1 7.8 %copy-start.2 = (f32[1024,128]{1,0:T(8,128)S(1)}, f32[1024,128]{1,0:T(8,128)}, u32[]{:S(2)}) copy-start(f32[1024,128]{1,0:T(8,128)} %param.16) | copy-start | bytes 1572868
  140.1 8.7 %copy-start.1 = (f32[2048,128]{1,0:T(8,128)S(1)}, f32[2048,128]{1,0:T(8,128)}, u32[]{:S(2)}) copy-start(f32[2048,128]{1,0:T(8,128)} %param.18) | copy-start | bytes 3145732

commit v6 on v5

--- a/solution.py
+++ b/solution.py
@@ -9,12 +9,35 @@
 learn_rate = 0.05
 eps_ada = 1e-08
 f32, bf16, i32 = jnp.float32, jnp.bfloat16, jnp.int32
-VLIM = 60 * 1024 * 1024
-
-
-def row_adagrad(table, accum, grad):
-    accum_new = accum + jnp.mean(grad * grad, axis=1)
-    return (table - learn_rate * grad / (jnp.sqrt(accum_new)[:, None] + eps_ada), accum_new)
+VLIM = 66 * 1000 * 1000
+
+
+def row_adagrad(table, accum, grad, new, new_accum):
+    rows = table.shape[0]
+
+    def chunk(n, _):
+        at = pl.ds(pl.multiple_of(n * 128, 128), 128)
+        g = grad[at, :]
+        before = jnp.broadcast_to(accum[pl.ds(n, 1), :], (128, 128)).T
+        after = before + jnp.mean(g * g, axis=1, keepdims=True)
+        new[at, :] = table[at, :] - learn_rate * g / (jnp.sqrt(after) + eps_ada)
+        new_accum[pl.ds(n, 1), :] = after.T[0:1, :]
+        return 0
+
+    lax.fori_loop(0, rows // 128, chunk, 0)
+
+
+def finish_kernel(mine, freq, seg, f_table, f_accum, s_table, s_accum, new_f, new_fa, new_s, new_sa, g_up, g_down, g_bias):
+    row_adagrad(s_table, s_accum, seg, new_s, new_sa)
+    row_adagrad(f_table, f_accum, freq, new_f, new_fa)
+    up_rows, down_rows = g_up.shape[0], g_down.shape[0]
+    cols = g_up.shape[1] // 128
+    for c in range(cols):
+        g_up[:, c * 128 : (c + 1) * 128] = mine[pl.ds(c, up_rows, stride=cols), :]
+    first, cols = up_rows * cols, g_down.shape[1] // 128
+    for c in range(cols):
+        g_down[:, c * 128 : (c + 1) * 128] = mine[pl.ds(first + c, down_rows, stride=cols), :]
+    g_bias[...] = mine[first + down_rows * cols : first + down_rows * cols + 1, 0:down_rows]
 
 
 def dot_nt(a, b):
@@ -82,14 +105,16 @@
 ):
     samples = hidden.shape[0]
     emb = values.shape[1]
-    steps = in_sems.shape[0]
+    pieces = in_sems.shape[0]
+    steps = v_sems.shape[0]
     wide = cross.shape[1] // steps
+    thin = cross.shape[1] // pieces
     per = wide // emb
     owners = bucket.shape[0]
     slots = bucket.shape[1] - 8
 
     def loads(g):
-        cols = pl.ds(pl.multiple_of(g * wide, wide), wide)
+        cols = pl.ds(pl.multiple_of(g * thin, 128), thin)
         return [
             pltpu.make_async_copy(cross_hbm.at[:, cols], cross.at[:, cols], in_sems.at[g, 0]),
             pltpu.make_async_copy(cot_hbm.at[:, cols], cot.at[:, cols], in_sems.at[g, 1]),
@@ -97,7 +122,7 @@
             pltpu.make_async_copy(up_hbm.at[:, cols], up.at[:, cols], in_sems.at[g, 3]),
         ]
 
-    for g in range(steps):
+    for g in range(pieces):
         for c in loads(g):
             c.start()
     index_work(frequent, owned, place, idx_v, row_a, row_b, hot, cum)
@@ -107,8 +132,9 @@
     b_acc[...] = jnp.zeros_like(b_acc)
 
     def low(g, _):
-        for c in loads(g):
-            c.wait()
+        for n in range(pieces // steps):
+            for c in loads(g * (pieces // steps) + n):
+                c.wait()
         cols = pl.ds(pl.multiple_of(g * wide, wide), wide)
         x = cross[:, cols]
         inner = (cot[:, cols].astype(f32) * x.astype(f32)).astype(bf16)
@@ -126,7 +152,7 @@
 
     def high(g, _):
         cols = pl.ds(pl.multiple_of(g * wide, wide), wide)
-        scaled = jnp.dot(hidden[...], up[:, cols], preferred_element_type=f32) + bias[:, cols]
+        scaled = jnp.dot(hidden[...], up[:, cols], preferred_element_type=f32) + bias[cols].reshape(1, wide)
         v = cot[:, cols].astype(f32) * (scaled + 1.0) + dot_nt(back_low[...], down[cols, :])
         for k in range(per):
             values[pl.ds(pl.multiple_of((g * per + k) * samples, 128), samples), :] = v[:, k * emb : (k + 1) * emb]
@@ -256,13 +282,13 @@
     pl.semaphore_wait(barrier, len(peers))
 
 
-def weights_kernel(steps, hidden, back_low, cross, cot, values_hbm, place, *rest):
+def weights_kernel(steps, hidden, back_low, cross, cot, values_hbm, place_in, *rest):
     outs, rest = rest[: len(PORT)], rest[len(PORT) :]
     freq_out, rest = rest[0], rest[1:]
     pair, rest = rest[: len(PORT)], rest[len(PORT) :]
     y_land, rest = rest[:4], rest[4:]
     f_both, f_pair, f_land, rest = rest[0], rest[1], rest[2:5], rest[5:]
-    both, freq, hidden_t, down, up, bias, values, send_sems, recv_sems, local_sems = rest
+    both, freq, hidden_t, down, up, bias, values, place, send_sems, recv_sems, local_sems = rest
     g = pl.program_id(0)
     rank = hidden.shape[1]
     wide = cross.shape[1]
@@ -285,6 +311,8 @@
         greet([partner] + [near[1][t] for t in near[0][1:]])
         load.start()
         hidden_t[...] = hidden[...].T
+        for t in range(place.shape[0]):
+            place[t] = place_in[t : t + 1, :]
         freq[...] = jnp.zeros_like(freq)
 
     inner = cot[...].astype(f32) * cross[...].astype(f32)
@@ -707,13 +735,13 @@
             pltpu.VMEM((samples, rank), f32),
             pltpu.VMEM((samples, rank), f32),
             pltpu.SemaphoreType.DMA((steps, 4)),
-            pltpu.SemaphoreType.DMA((steps,)),
+            pltpu.SemaphoreType.DMA((3,)),
             pltpu.SemaphoreType.DMA((shards,)),
             pltpu.SemaphoreType.DMA,
         ],
         compiler_params=params(),
         name="front_kernel",
-    )(place_t, cross_bias.reshape(1, -1), cross_in, cotangent, weight_down, weight_up)
+    )(place_t, cross_bias, cross_in, cotangent, weight_down, weight_up)
 
     arrived = lax.all_to_all(bucket, "dp", split_axis=0, concat_axis=0, tiled=True)
 
@@ -730,7 +758,7 @@
             pl.BlockSpec((samples, wide), lambda g: (0, g)),
             pl.BlockSpec((samples, wide), lambda g: (0, g)),
             anyw,
-            pl.BlockSpec((tables, 1, samples), lambda g: (0, 0, 0)),
+            pl.BlockSpec((tables, samples), lambda g: (0, 0)),
         ],
         out_specs=(anyw,) * (len(PORT) + 1),
         scratch_shapes=[pltpu.VMEM((16, 4, r, 128), f32) for _, r, _, _ in PORT]
@@ -745,21 +773,38 @@
             pltpu.VMEM((per * rank, 128), f32),
             pltpu.VMEM((1, width), f32),
             pltpu.VMEM((blocks * samples, emb), f32),
+            pltpu.VMEM((tables, 1, samples), i32),
             pltpu.SemaphoreType.DMA((16,)),
             pltpu.SemaphoreType.DMA((16,)),
             pltpu.SemaphoreType.DMA((8,)),
         ],
         compiler_params=params(collective_id=1, has_side_effects=True),
         name="weights_kernel",
-    )(hidden, back_low, cross_in, cotangent, values, place_t.reshape(tables, 1, samples))
+    )(hidden, back_low, cross_in, cotangent, values, place_t)
 
     mine, freq, shard_grad = reduce_all(parts, arrived, owned)
-    n = rank * width // count // 128
-    grad_up = mine[:n].reshape(rank // count, width)
-    grad_down = mine[n : 2 * n].reshape(width // count, rank)
-    grad_bias = mine[2 * n, : width // count]
-    new_shard, new_shard_accum = row_adagrad(shard_table, shard_accum, shard_grad)
-    new_frequent, new_frequent_accum = row_adagrad(frequent_table, frequent_accum, freq)
+    n = width // count
+    new_frequent, new_frequent_accum, new_shard, new_shard_accum, grad_up, grad_down, grad_bias = pl.pallas_call(
+        finish_kernel,
+        out_shape=(
+            jax.ShapeDtypeStruct((f_count, emb), f32),
+            jax.ShapeDtypeStruct((f_count // 128, 128), f32),
+            jax.ShapeDtypeStruct((owned, emb), f32),
+            jax.ShapeDtypeStruct((owned // 128, 128), f32),
+            jax.ShapeDtypeStruct((rank // count, width), f32),
+            jax.ShapeDtypeStruct((n, rank), f32),
+            jax.ShapeDtypeStruct((1, n), f32),
+        ),
+        in_specs=[vmem] * 7,
+        out_specs=(vmem,) * 7,
+        compiler_params=pltpu.CompilerParams(vmem_limit_bytes=16 * 1024 * 1024),
+        name="finish_kernel",
+    )(
+        mine, freq, shard_grad, frequent_table, frequent_accum.reshape(-1, 128),
+        shard_table, shard_accum.reshape(-1, 128),
+    )
+    new_frequent_accum, new_shard_accum = new_frequent_accum.reshape(-1), new_shard_accum.reshape(-1)
+    grad_bias = grad_bias.reshape(-1)
     return (new_frequent, new_frequent_accum, new_shard, new_shard_accum, grad_up, grad_down, grad_bias)
 
 

time: 153 us -> 145 us (0.948)
  the two profiles are of different devices: /device:TPU:1 before, /device:TPU:0 now
where the time goes in v6:
time: 145 us
  Pallas kernels  131 us (90%)
  starting transfers between devices  8.54 us (6%)
  local copies, waits for them, and re-layouts  4.4 us (3%)
    pallas_call x1, Pallas kernels, reduce_all(): pl.pallas_call(reduce_kernel, out_shape=(jax.ShapeDtypeStruct((total, 128...  53.6 us
    pallas_call x1, Pallas kernels, body(): pl.pallas_call(functools.partial(weights_kernel, steps), grid=(steps,), o...  48.1 us
    pallas_call x1, Pallas kernels, body(): pl.pallas_call(functools.partial(front_kernel, f_count, owned), out_shape...  24 us
    all_to_all x1, starting transfers between devices, body(): lax.all_to_all(bucket, 'dp', split_axis=0, concat_axis=0, tiled=True)  8.54 us
    pallas_call x1, Pallas kernels, body(): pl.pallas_call(finish_kernel, out_shape=(jax.ShapeDtypeStruct((f_count, e...  5.42 us
    unnamed x14, local copies, waits for them, and re-layouts  4.4 us
  transfers between devices with their start and end apart: 1, of which 0 were waited for; matrix products, arithmetic and copies ran while one was open for 0% of the time, Pallas kernels for 33%

profile of v6, /device:TPU:0, one launch (start us, length us, event | category | flops | bytes accessed | tf_op | source)
XLA Modules:
  0.0 144.8 jit_solution(9182324917193170624)
XLA Ops:
  0.6 24.0 %front_kernel.1 = (bf16[512,512]{1,0:T(8,128)(2,1)}, bf16[512,512]{1,0:T(8,128)(2,1)}, f32[13824,128]{1,0:T(8,128)}, f32[32,216,128]{2,1,0:T(8,128)}) custom-call(s32[26,512]{1,0:T(8,128)} %bitcast.19, f32[3456]{0:T(1024)} %bias.1, bf16[512,3456]{1,0:T(8,128)(2,1)} %cross.1, bf16[512,3456]{1,0:T(8,128)(2,1)} %cot.1, bf16[3456,512]{1,0:T(8,128)(2,1)} %down_hbm.1, ...), custom_call_target="tpu_custom_call" | custom-call | tf_op jit(solution)/shard_map/front_kernel/pallas_call | solution.py:712
  24.6 8.5 %all-to-all-start = ((f32[32,216,128]{2,1,0:T(8,128)}), f32[32,216,128]{2,1,0:T(8,128)}, u32[]{:S(2)}, u32[]{:S(2)}) async-start(f32[32,216,128]{2,1,0:T(8,128)} %get-tuple-element.32), calls=%async_computation | async-start | bytes 7077888 | tf_op jit(solution)/shard_map/all_to_all | solution.py:746
  33.2 48.1 %weights_kernel.1 = (f32[16,4,72,128]{3,2,1,0:T(8,128)}, f32[16,4,80,128]{3,2,1,0:T(8,128)}, f32[16,72,128]{2,1,0:T(8,128)}, f32[16,8,128]{2,1,0:T(8,128)}) custom-call(bf16[512,512]{1,0:T(8,128)(2,1)} %get-tuple-element.25.hidden, bf16[512,512]{1,0:T(8,128)(2,1)} %get-tuple-element.26.back_low, bf16[512,3456]{1,0:T(8,128)(2,1)} %cross.1, ...), custom_call_target="tpu_custom_call" | custom-call | tf_op jit(solution)/shard_map/weights_kernel/pallas_call | solution.py:748
  81.3 0.0 all-to-all-done.refs_4_
  81.3 0.0 copy-start.2
  81.3 0.0 copy-start.5
  81.3 0.0 copy-start.6
  81.4 53.6 %reduce_kernel.1 = (f32[224,128]{1,0:T(8,128)}, f32[4,4,2,4,8,128]{5,4,3,2,1,0:T(8,128)}, f32[4,512,128]{2,1,0:T(8,128)}) custom-call(f32[4,4,4,72,128]{4,3,2,1,0:T(8,128)} %bitcast.17, f32[4,4,4,80,128]{4,3,2,1,0:T(8,128)} %bitcast.16, f32[4,4,72,128]{3,2,1,0:T(8,128)} %bitcast.18, f32[4,4,8,128]{3,2,1,0:T(8,128)} %bitcast.21, ...), custom_call_target="tpu_custom_call" | custom-call | tf_op jit(solution)/shard_map/reduce_kernel/pallas_call | solution.py:678
  135.0 0.0 copy-done.2
  135.0 0.0 copy-done.5
  135.0 0.0 copy-done.6
  135.0 0.0 copy-start
  135.0 1.2 copy-done
  136.3 0.0 copy-start.1
  136.3 1.2 copy-done.1
  137.5 0.0 copy-start.3
  137.5 1.0 copy-done.3
  138.5 0.0 copy-start.4
  138.5 0.9 copy-done.4
  139.4 5.4 %finish_kernel.1 = (f32[1024,128]{1,0:T(8,128)}, f32[8,128]{1,0:T(8,128)}, f32[2048,128]{1,0:T(8,128)}, f32[16,128]{1,0:T(8,128)}, f32[4,3456]{1,0:T(4,128)}, /*index=5*/f32[27,512]{1,0:T(8,128)}, f32[1,27]{1,0:T(1,128)}) custom-call(f32[224,128]{1,0:T(8,128)S(1)} %copy-done.4, f32[1024,128]{1,0:T(8,128)S(1)} %bitcast.13, f32[2048,128]{1,0:T(8,128)S(1)} %bitcast.12, ...), custom_call_target="tpu_custom_call" | custom-call | tf_op jit(solution)/shard_map/finish_kernel/pallas_call | solution.py:787
Async XLA Ops:
  24.6 56.7 %all-to-all-start = ((f32[32,216,128]{2,1,0:T(8,128)}), f32[32,216,128]{2,1,0:T(8,128)}, u32[]{:S(2)}, u32[]{:S(2)}) async-start(f32[32,216,128]{2,1,0:T(8,128)} %get-tuple-element.32), calls=%async_computation | async-start | bytes 7077888 | tf_op jit(solution)/shard_map/all_to_all | solution.py:746
  81.3 53.7 %copy-start.2 = (f32[1024,128]{1,0:T(8,128)S(1)}, f32[1024,128]{1,0:T(8,128)}, u32[]{:S(2)}) copy-start(f32[1024,128]{1,0:T(8,128)} %f_table.1) | copy-start | bytes 1572868
  81.3 53.7 %copy-start.5 = (f32[2048]{0:T(1024)S(1)}, f32[2048]{0:T(1024)}, u32[]{:S(2)}) copy-start(f32[2048]{0:T(1024)} %param.19) | copy-start | bytes 24580
  81.3 53.7 %copy-start.6 = (f32[1024]{0:T(1024)S(1)}, f32[1024]{0:T(1024)}, u32[]{:S(2)}) copy-start(f32[1024]{0:T(1024)} %param.17) | copy-start | bytes 12292
  135.0 1.2 copy-start
  136.3 1.2 copy-start.1
  137.5 1.0 copy-start.3
  138.5 0.9 copy-start.4

commit v7 on v6

--- a/solution.py
+++ b/solution.py
@@ -12,32 +12,31 @@
 VLIM = 66 * 1000 * 1000
 
 
-def row_adagrad(table, accum, grad, new, new_accum):
-    rows = table.shape[0]
-
+def row_adagrad(table, accum, grad_of, new, new_accum):
     def chunk(n, _):
         at = pl.ds(pl.multiple_of(n * 128, 128), 128)
-        g = grad[at, :]
+        g = grad_of(n)
         before = jnp.broadcast_to(accum[pl.ds(n, 1), :], (128, 128)).T
         after = before + jnp.mean(g * g, axis=1, keepdims=True)
         new[at, :] = table[at, :] - learn_rate * g / (jnp.sqrt(after) + eps_ada)
         new_accum[pl.ds(n, 1), :] = after.T[0:1, :]
         return 0
 
-    lax.fori_loop(0, rows // 128, chunk, 0)
-
-
-def finish_kernel(mine, freq, seg, f_table, f_accum, s_table, s_accum, new_f, new_fa, new_s, new_sa, g_up, g_down, g_bias):
-    row_adagrad(s_table, s_accum, seg, new_s, new_sa)
-    row_adagrad(f_table, f_accum, freq, new_f, new_fa)
-    up_rows, down_rows = g_up.shape[0], g_down.shape[0]
-    cols = g_up.shape[1] // 128
-    for c in range(cols):
-        g_up[:, c * 128 : (c + 1) * 128] = mine[pl.ds(c, up_rows, stride=cols), :]
-    first, cols = up_rows * cols, g_down.shape[1] // 128
-    for c in range(cols):
-        g_down[:, c * 128 : (c + 1) * 128] = mine[pl.ds(first + c, down_rows, stride=cols), :]
-    g_bias[...] = mine[first + down_rows * cols : first + down_rows * cols + 1, 0:down_rows]
+    lax.fori_loop(0, table.shape[0] // 128, chunk, 0)
+
+
+def move_kernel(*refs):
+    n = len(refs) // 3
+    src, dst, held, sems = refs[:n], refs[n : 2 * n], refs[2 * n : 3 * n], refs[3 * n]
+    takes = [pltpu.make_async_copy(a, b, sems.at[0, i]) for i, (a, b) in enumerate(zip(src, held))]
+    gives = [pltpu.make_async_copy(a, b, sems.at[1, i]) for i, (a, b) in enumerate(zip(held, dst))]
+    for c in takes:
+        c.start()
+    for c, d in zip(takes, gives):
+        c.wait()
+        d.start()
+    for d in gives:
+        d.wait()
 
 
 def dot_nt(a, b):
@@ -180,7 +179,15 @@
     lax.fori_loop(0, owners, lambda o, _: (ship(o).wait(), 0)[1], 0)
 
 
-PORT = ((72, 72, 40, "xzy"), (144, 80, 40, "zxy"), (0, 72, 40, "yxz"))
+PORT = (
+    (72, 40, 24, "xzy"),
+    (112, 32, 16, "xzy"),
+    (144, 40, 24, "zxy"),
+    (184, 40, 24, "zxy"),
+    (0, 40, 24, "yxz"),
+    (40, 32, 16, "yzx"),
+)
+N_BULK = 4
 
 
 def mesh_place():
@@ -286,7 +293,7 @@
     outs, rest = rest[: len(PORT)], rest[len(PORT) :]
     freq_out, rest = rest[0], rest[1:]
     pair, rest = rest[: len(PORT)], rest[len(PORT) :]
-    y_land, rest = rest[:4], rest[4:]
+    y_land, rest = [rest[:4], rest[4:8]], rest[8:]
     f_both, f_pair, f_land, rest = rest[0], rest[1], rest[2:5], rest[5:]
     both, freq, hidden_t, down, up, bias, values, place, send_sems, recv_sems, local_sems = rest
     g = pl.program_id(0)
@@ -345,7 +352,8 @@
             first, rows = PORT[p][0], PORT[p][1]
             return both.at[:, c, :, pl.ds(first, rows), :]
 
-        got = {2: send(part(2, 1 - core), pair[2], partner)}
+        firsts = range(N_BULK, len(PORT))
+        got = {p: send(part(p, 1 - core), pair[p], partner) for p in firsts}
 
         def put_down(n, _):
             for c in range(2):
@@ -363,7 +371,7 @@
             both[i // 8, (i // 4) % 2, i % 4, bias_at : bias_at + 1, 0:down_rows] = bias[
                 :, i * down_rows : (i + 1) * down_rows
             ]
-        for p in (0, 1):
+        for p in range(N_BULK):
             got[p] = send(part(p, 1 - core), pair[p], partner)
         load.wait()
         row_iota = lax.broadcasted_iota(i32, (frequent, samples), 0)
@@ -390,20 +398,23 @@
 
             lax.fori_loop(0, count // 8, add, 0)
 
-        first, rows, half, _ = PORT[2]
-
-        def y_at(t, lo, hi):
-            return both.at[:, core, t, pl.ds(first + lo, hi - lo), :]
-
-        def y_add(t, lo, hi, lands):
-            def add(n, _):
-                v = both[n, core, t, first + lo : first + hi, :]
-                for ref in lands:
-                    v = v + ref[n]
-                both[n, core, t, first + lo : first + hi, :] = v
-                return 0
-
-            lax.fori_loop(0, count // 8, add, 0)
+        def y_phase(p):
+            first, rows, half, _ = PORT[p]
+
+            def at(t, lo, hi):
+                return both.at[:, core, t, pl.ds(first + lo, hi - lo), :]
+
+            def y_add(t, lo, hi, lands):
+                def add(n, _):
+                    v = both[n, core, t, first + lo : first + hi, :]
+                    for ref in lands:
+                        v = v + ref[n]
+                    both[n, core, t, first + lo : first + hi, :] = v
+                    return 0
+
+                lax.fori_loop(0, count // 8, add, 0)
+
+            return Reduce(send, near, at, y_add, rows, half, y_land[p - N_BULK])
 
         def f_add(t, lands):
             v = f_both[:, core, t]
@@ -411,15 +422,17 @@
                 v = v + ref[...]
             f_both[:, core, t] = v
 
-        y_sum = Reduce(send, near, y_at, y_add, rows, half, y_land)
+        y_sums = {p: y_phase(p) for p in firsts}
         f_sum = Direct(send, near, lambda t: f_both.at[:, core, t], f_add, f_land)
         pairs = place.shape[0] // 2
-        cut = pairs // 3
-        lax.fori_loop(0, cut, tables, 0)
-        add_pair(2)
-        y_sum.start()
-        lax.fori_loop(cut, pairs, tables, 0)
-        y_sum.middle()
+        lax.fori_loop(0, 2, tables, 0)
+        for p in firsts:
+            add_pair(p)
+            y_sums[p].start()
+        lax.fori_loop(2, pairs // 2 + 2, tables, 0)
+        y_sums[N_BULK].middle()
+        lax.fori_loop(pairs // 2 + 2, pairs, tables, 0)
+        y_sums[N_BULK + 1].middle()
 
         def put_freq(n, _):
             for c in range(2):
@@ -430,18 +443,19 @@
         lax.fori_loop(0, count // 8, put_freq, 0)
         f_got = send(f_both.at[:, 1 - core], f_pair, partner)
         stores = []
-        for p in (0, 1):
+        for p in range(N_BULK):
             add_pair(p)
             stores.append(pltpu.make_async_copy(part(p, core), outs[p], local_sems.at[1 + p]))
             stores[-1].start()
         f_got.wait_recv()
         f_both[:, core] = f_both[:, core] + f_pair[...]
         f_sum.start()
-        y_sum.finish()
-        stores.append(pltpu.make_async_copy(y_at(me["y"], 0, rows), outs[2], local_sems.at[3]))
-        stores[-1].start()
+        for p in firsts:
+            y_sums[p].finish()
+            stores.append(pltpu.make_async_copy(y_sums[p].at(me["y"], 0, PORT[p][1]), outs[p], local_sems.at[1 + p]))
+            stores[-1].start()
         f_sum.finish()
-        stores.append(pltpu.make_async_copy(f_both.at[:, core, me["y"]], freq_out, local_sems.at[4]))
+        stores.append(pltpu.make_async_copy(f_both.at[:, core, me["y"]], freq_out, local_sems.at[1 + len(PORT)]))
         stores[-1].start()
         for c in stores:
             c.wait()
@@ -456,12 +470,16 @@
 def reduce_kernel(*refs):
     it = iter(refs)
     take = lambda n: [next(it) for _ in range(n)]
-    loads, (load_f, arrived), (mine, freq_out, seg_out) = take(3), take(2), take(3)
-    work = take(3)
-    land = {p: {k: take(4) for k in range(1 if p == 2 else 0, 3)} for p in range(3)}
-    swork, sland, sgath = next(it), take(4), next(it)
+    pieces = range(len(PORT))
+    begins = [1 if PORT[p][3][0] == "y" else 0 for p in pieces]
+    loads, (load_f, arrived), given = take(len(PORT)), take(2), take(4)
+    new_f, new_fa, new_s, new_sa, g_up, g_down, g_bias = take(7)
+    work = take(len(PORT))
+    land = {p: {k: take(4) for k in range(begins[p], 3)} for p in pieces}
+    swork, sland, sgath = next(it), [take(4), take(4)], next(it)
     f_work, fx_land, fz_land, gath = next(it), take(3), take(3), next(it)
-    arr, ids, right, acc = take(4)
+    mine, arr, ids, right, acc = take(5)
+    f_table, f_accum, s_table, s_accum = held = take(4)
     send_sems, recv_sems, local_sems = take(3)
     me, core, partner = mesh_place()
     near = {a: neighbours(me, core, a) for a in "xzy"}
@@ -483,8 +501,8 @@
 
     def phase(p, k):
         _, rows, half, order = PORT[p]
-        dims = "xz" if p == 2 else "xzy"
-        done, axis = order[:k].replace("y", "") if p == 2 else order[:k], order[k]
+        dims = "xz" if begins[p] else "xzy"
+        done, axis = order[begins[p] : k], order[k]
         ref, left = work[p], 2 - k
 
         def at(t, lo, hi):
@@ -507,20 +525,26 @@
 
         return Reduce(send, near[axis], at, add, rows, half, land[p][k])
 
-    sums = {(p, k): phase(p, k) for p in range(3) for k in range(1 if p == 2 else 0, 3)}
+    sums = {(p, k): phase(p, k) for p in pieces for k in range(begins[p], 3)}
 
     owned = swork.shape[1]
 
-    def s_add(t, lo, hi, lands):
-        for r in range(lo, hi, 128):
-            v = swork[t, r : r + 128, :]
-            for ref in lands:
-                v = v + ref[r - lo : r - lo + 128, :]
-            swork[t, r : r + 128, :] = v
-
-    s_red = Reduce(
-        send, near["y"], lambda t, lo, hi: swork.at[t, pl.ds(lo, hi - lo), :], s_add, owned, owned // 2, sland
-    )
+    part = owned // 2
+
+    def s_phase(h):
+        def at(t, lo, hi):
+            return swork.at[t, pl.ds(h * part + lo, hi - lo), :]
+
+        def add(t, lo, hi, lands):
+            for r in range(lo, hi, 128):
+                v = swork[t, h * part + r : h * part + r + 128, :]
+                for ref in lands:
+                    v = v + ref[r - lo : r - lo + 128, :]
+                swork[t, h * part + r : h * part + r + 128, :] = v
+
+        return Reduce(send, near["y"], at, add, part, part // 2, sland[h])
+
+    s_red = [s_phase(0), s_phase(1)]
 
     def f_add(spot, lands):
         v = f_work[spot]
@@ -537,29 +561,39 @@
     g_y = Spread(send, near["y"], lambda t: gath.at[:, :, core, t])
 
     class SegGather:
+        def __init__(self, h):
+            self.first = h * part
+
+        def at(self, t, lo, hi):
+            return sgath.at[t, pl.ds(self.first + lo, hi - lo), :]
+
         def start(self):
             (here, up, far, down), to = near["y"]
-            src = sgath.at[here]
+            spot = (here, slice(self.first, self.first + part), slice(None))
+            sgath[spot] = swork[spot]
+            src = self.at(here, 0, part)
             self.c0, self.c1 = send(src, src, to[up]), send(src, src, to[down])
 
         def middle(self):
             (here, up, far, down), to = near["y"]
             self.c0.wait_recv()
-            src = sgath.at[down, pl.ds(0, owned // 2), :]
+            src = self.at(down, 0, part // 2)
             self.c2 = send(src, src, to[up])
             self.c1.wait_recv()
-            src = sgath.at[up, pl.ds(owned // 2, owned // 2), :]
+            src = self.at(up, part // 2, part)
             self.c3 = send(src, src, to[down])
 
         def finish(self):
             self.c2.wait_recv()
             self.c3.wait_recv()
 
-    s_gat = SegGather()
-    copies = [pltpu.make_async_copy(loads[p], work[p], local_sems.at[p]) for p in range(3)]
-    copy_f = pltpu.make_async_copy(load_f, f_work, local_sems.at[3])
-    copy_a = pltpu.make_async_copy(arrived, arr, local_sems.at[4])
-    for c in [copy_f, copies[0], copies[1], copy_a, copies[2]]:
+    s_gat = [SegGather(0), SegGather(1)]
+    copies = [pltpu.make_async_copy(loads[p], work[p], local_sems.at[p]) for p in pieces]
+    more = [(load_f, f_work), (arrived, arr)] + list(zip(given, held))
+    copy_f, copy_a, *rest = [
+        pltpu.make_async_copy(a, b, local_sems.at[len(PORT) + i]) for i, (a, b) in enumerate(more)
+    ]
+    for c in [copy_f, copies[0], copies[2], copies[1], copies[3], copy_a, copies[4], copies[5]] + rest:
         c.start()
     slots = arr.shape[1] - 8
     some = ids.shape[0]
@@ -591,104 +625,139 @@
         swork[t] = acc[:, :128] + acc[:, 128:]
 
     _, y_up, y_far, y_down = near["y"][0]
+    def done(p, k):
+        sums[p, k].finish()
+        if k < 2:
+            sums[p, k + 1].start()
+
     copy_f.wait()
     f_x.start()
-    copies[0].wait()
-    sums[0, 0].start()
-    copies[1].wait()
-    sums[1, 0].start()
+    for p in (0, 2, 1, 3):
+        copies[p].wait()
+        sums[p, 0].start()
     copy_a.wait()
     lax.fori_loop(0, some, prepare, 0)
     f_x.finish()
     f_z.start()
     seg_block(y_far)
-    s_red.start()
-    copies[2].wait()
+    s_red[0].start()
+    s_red[1].start()
+    sums[0, 0].middle()
+    sums[2, 0].middle()
     seg_block(y_up)
-    sums[0, 0].middle()
     sums[1, 0].middle()
-    sums[2, 1].start()
+    sums[3, 0].middle()
+    for p in (4, 5):
+        copies[p].wait()
+        sums[p, 1].start()
     seg_block(y_down)
-    s_red.middle()
+    s_red[0].middle()
+    s_red[1].middle()
     f_z.finish()
     gath[me["x"], me["z"], core, me["y"]] = f_work[me["x"], me["z"]]
     g_z.start()
     seg_block(me["y"])
-    s_red.finish()
-    sgath[me["y"]] = swork[me["y"]]
-    s_gat.start()
-    sums[0, 0].finish()
-    sums[0, 1].start()
-    sums[1, 0].finish()
-    sums[1, 1].start()
-    sums[2, 1].middle()
+    done(0, 0)
+    done(2, 0)
+    s_red[0].finish()
+    s_gat[0].start()
+    s_red[1].finish()
+    s_gat[1].start()
+    done(1, 0)
+    done(3, 0)
+    sums[4, 1].middle()
+    sums[5, 1].middle()
     g_z.finish()
     g_x.start()
-    s_gat.middle()
     sums[0, 1].middle()
+    sums[2, 1].middle()
+    s_gat[0].middle()
+    s_gat[1].middle()
+    done(4, 1)
+    done(5, 1)
     sums[1, 1].middle()
-    sums[2, 1].finish()
-    sums[2, 2].start()
+    sums[3, 1].middle()
     g_x.finish()
     g_y.start()
-    sums[0, 1].finish()
-    sums[0, 2].start()
-    sums[1, 1].finish()
-    sums[1, 2].start()
-    s_gat.finish()
-    seg_out[...] = sgath[...]
-    sums[2, 2].middle()
+    done(0, 1)
+    done(2, 1)
+    done(1, 1)
+    done(3, 1)
+    for c in rest:
+        c.wait()
+    s_gat[0].finish()
+    s_gat[1].finish()
+    row_adagrad(s_table, s_accum, lambda n: sgath[n // 4, pl.ds(pl.multiple_of(n % 4 * 128, 128), 128), :], new_s, new_sa)
+    sums[4, 2].middle()
+    sums[5, 2].middle()
     g_y.finish()
     g_c = send(gath.at[:, :, core], gath.at[:, :, core], partner)
-    sums[0, 2].middle()
-    sums[1, 2].middle()
+    for p in (0, 2, 1, 3):
+        sums[p, 2].middle()
     g_c.wait_recv()
-    freq_out[...] = gath[...]
-    sums[2, 2].finish()
-    sums[0, 2].finish()
-    sums[1, 2].finish()
+    row_adagrad(f_table, f_accum, lambda n: gath[n // 2, pl.ds(n % 2 * 2, 2)].reshape(128, 128), new_f, new_fa)
     here = (me["x"], me["z"], me["y"])
-    for p, (first, rows, _, _) in enumerate(PORT):
-        mine[first : first + rows, :] = work[p][here[:2] if p == 2 else here]
+    for p in (4, 5, 0, 2, 1, 3):
+        sums[p, 2].finish()
+        first, rows = PORT[p][:2]
+        mine[first : first + rows, :] = work[p][here[:2] if begins[p] else here]
+    up_rows, down_rows = g_up.shape[0], g_down.shape[0]
+    cols = g_up.shape[1] // 128
+    for c in range(cols):
+        g_up[:, c * 128 : (c + 1) * 128] = mine[pl.ds(c, up_rows, stride=cols), :]
+    first, cols = up_rows * cols, g_down.shape[1] // 128
+    for c in range(cols):
+        g_down[:, c * 128 : (c + 1) * 128] = mine[pl.ds(first + c, down_rows, stride=cols), :]
+    g_bias[...] = mine[first + down_rows * cols : first + down_rows * cols + 1, 0:down_rows]
     for c in sent:
         c.wait_send()
 
 
-def reduce_scratch(owned, arrived):
+def reduce_scratch(owned, frequent, arrived):
     v = lambda *s: pltpu.VMEM(s, f32)
-    out = [v(*((4, 4) if p == 2 else (4, 4, 4)), PORT[p][1], 128) for p in range(3)]
-    for p, (_, r, h, _) in enumerate(PORT):
-        for k in range(1 if p == 2 else 0, 3):
+    begins = [1 if order[0] == "y" else 0 for _, _, _, order in PORT]
+    out = [v(*(4,) * (3 - b), r, 128) for b, (_, r, _, _) in zip(begins, PORT)]
+    for b, (_, r, h, _) in zip(begins, PORT):
+        for k in range(b, 3):
             lead = (4,) * (2 - k)
             out += [v(*lead, h, 128), v(*lead, r - h, 128), v(*lead, r, 128), v(*lead, r, 128)]
     q = owned // 4
-    out += [v(4, q, 128), v(q // 2, 128), v(q // 2, 128), v(q, 128), v(q, 128), v(4, q, 128)]
+    out += [v(4, q, 128)] + [v(q // 4, 128), v(q // 4, 128), v(q // 2, 128), v(q // 2, 128)] * 2 + [v(4, q, 128)]
     out += [v(4, 4, 8, 128)] + [v(4, 8, 128)] * 3 + [v(8, 128)] * 3 + [v(4, 4, 2, 4, 8, 128)]
     n = arrived.shape[0] // 4
     flat = arrived.shape[0] * (arrived.shape[1] - 8)
+    out += [v(max(a + r for a, r, _, _ in PORT), 128)]
     out += [v(*arrived.shape), pltpu.VMEM((n, 1, flat // n), i32), pltpu.VMEM((flat, 256), bf16), v(q, 256)]
-    out += [pltpu.SemaphoreType.DMA((64,)), pltpu.SemaphoreType.DMA((64,)), pltpu.SemaphoreType.DMA((8,))]
+    out += [v(frequent, 128), v(frequent // 128, 128), v(owned, 128), v(owned // 128, 128)]
+    out += [pltpu.SemaphoreType.DMA((112,)), pltpu.SemaphoreType.DMA((112,)), pltpu.SemaphoreType.DMA((16,))]
     return out
 
 
-def reduce_all(parts, arrived, owned):
+def reduce_all(parts, arrived, f_table, f_accum, s_table, s_accum, count, width, rank):
     vmem = pl.BlockSpec(memory_space=pltpu.VMEM)
     anyw = pl.BlockSpec(memory_space=pl.ANY)
-    total = max(a + r for a, r, _, _ in PORT)
-    mine, freq, seg = pl.pallas_call(
+    frequent, owned = f_table.shape[0], s_table.shape[0]
+    given = [f_table, f_accum.reshape(-1, 128), s_table, s_accum.reshape(-1, 128)]
+    shapes = [g.shape for g in given] + [(rank // count, width), (width // count, rank), (1, width // count)]
+    shapes = [jax.ShapeDtypeStruct(shape, f32) for shape in shapes]
+    outs = pl.pallas_call(
         reduce_kernel,
-        out_shape=(
-            jax.ShapeDtypeStruct((total, 128), f32),
-            jax.ShapeDtypeStruct((4, 4, 2, 4, 8, 128), f32),
-            jax.ShapeDtypeStruct((4, owned // 4, 128), f32),
-        ),
-        in_specs=[anyw] * (len(PORT) + 2),
-        out_specs=(vmem, vmem, vmem),
-        scratch_shapes=reduce_scratch(owned, arrived),
+        out_shape=tuple(shapes),
+        in_specs=[anyw] * (len(PORT) + 6),
+        out_specs=(vmem,) * 7,
+        scratch_shapes=reduce_scratch(owned, frequent, arrived),
         compiler_params=params(collective_id=0, has_side_effects=True),
         name="reduce_kernel",
-    )(*[w.reshape(4, 4, *w.shape[1:]) for w in parts], arrived)
-    return mine, freq.reshape(1024, 128), seg.reshape(owned, 128)
+    )(*[w.reshape(4, 4, *w.shape[1:]) for w in parts], arrived, *given)
+    return pl.pallas_call(
+        move_kernel,
+        out_shape=tuple(shapes),
+        in_specs=[anyw] * 7,
+        out_specs=(anyw,) * 7,
+        scratch_shapes=[pltpu.VMEM(x.shape, f32) for x in shapes] + [pltpu.SemaphoreType.DMA((2, 7))],
+        compiler_params=params(),
+        name="move_kernel",
+    )(*outs)
 
 
 def body(cross_in, cotangent, weight_down, weight_up, cross_bias, row_place, frequent_table, frequent_accum, shard_table, shard_accum):
@@ -750,7 +819,9 @@
         grid=(steps,),
         out_shape=tuple(
             jax.ShapeDtypeStruct(shape, f32)
-            for shape in ((16, 4, PORT[0][1], 128), (16, 4, PORT[1][1], 128), (16, PORT[2][1], 128), (16, 8, 128))
+            for shape in [(16, 4, r, 128) for _, r, _, _ in PORT[:N_BULK]]
+            + [(16, r, 128) for _, r, _, _ in PORT[N_BULK:]]
+            + [(16, 8, 128)]
         ),
         in_specs=[
             pl.BlockSpec((samples, rank), lambda g: (0, 0)),
@@ -762,7 +833,7 @@
         ],
         out_specs=(anyw,) * (len(PORT) + 1),
         scratch_shapes=[pltpu.VMEM((16, 4, r, 128), f32) for _, r, _, _ in PORT]
-        + [pltpu.VMEM((16, r, 128), f32) for r in (PORT[2][2], PORT[2][1] - PORT[2][2], PORT[2][1], PORT[2][1])]
+        + [pltpu.VMEM((16, n, 128), f32) for _, r, h, _ in PORT[N_BULK:] for n in (h, r - h, r, r)]
         + [pltpu.VMEM((16, 2, 4, 8, 128), f32), pltpu.VMEM((16, 4, 8, 128), f32)]
         + [pltpu.VMEM((16, 8, 128), f32)] * 3
         + [
@@ -774,34 +845,16 @@
             pltpu.VMEM((1, width), f32),
             pltpu.VMEM((blocks * samples, emb), f32),
             pltpu.VMEM((tables, 1, samples), i32),
+            pltpu.SemaphoreType.DMA((24,)),
+            pltpu.SemaphoreType.DMA((24,)),
             pltpu.SemaphoreType.DMA((16,)),
-            pltpu.SemaphoreType.DMA((16,)),
-            pltpu.SemaphoreType.DMA((8,)),
         ],
         compiler_params=params(collective_id=1, has_side_effects=True),
         name="weights_kernel",
     )(hidden, back_low, cross_in, cotangent, values, place_t)
 
-    mine, freq, shard_grad = reduce_all(parts, arrived, owned)
-    n = width // count
-    new_frequent, new_frequent_accum, new_shard, new_shard_accum, grad_up, grad_down, grad_bias = pl.pallas_call(
-        finish_kernel,
-        out_shape=(
-            jax.ShapeDtypeStruct((f_count, emb), f32),
-            jax.ShapeDtypeStruct((f_count // 128, 128), f32),
-            jax.ShapeDtypeStruct((owned, emb), f32),
-            jax.ShapeDtypeStruct((owned // 128, 128), f32),
-            jax.ShapeDtypeStruct((rank // count, width), f32),
-            jax.ShapeDtypeStruct((n, rank), f32),
-            jax.ShapeDtypeStruct((1, n), f32),
-        ),
-        in_specs=[vmem] * 7,
-        out_specs=(vmem,) * 7,
-        compiler_params=pltpu.CompilerParams(vmem_limit_bytes=16 * 1024 * 1024),
-        name="finish_kernel",
-    )(
-        mine, freq, shard_grad, frequent_table, frequent_accum.reshape(-1, 128),
-        shard_table, shard_accum.reshape(-1, 128),
+    new_frequent, new_frequent_accum, new_shard, new_shard_accum, grad_up, grad_down, grad_bias = reduce_all(
+        parts, arrived, frequent_table, frequent_accum, shard_table, shard_accum, count, width, rank
     )
     new_frequent_accum, new_shard_accum = new_frequent_accum.reshape(-1), new_shard_accum.reshape(-1)
     grad_bias = grad_bias.reshape(-1)

time: 145 us -> 132 us (0.910)
  the two profiles are of different devices: /device:TPU:0 before, /device:TPU:1 now
where the time goes in v7:
time: 132 us; the launch traced here: 131 us
  Pallas kernels  120 us (91%)
  starting transfers between devices  9.51 us (7%)
    pallas_call x1, Pallas kernels, reduce_all(): pl.pallas_call(reduce_kernel, out_shape=tuple(shapes), in_specs=[anyw] *...  50.1 us
    pallas_call x1, Pallas kernels, body(): pl.pallas_call(functools.partial(weights_kernel, steps), grid=(steps,), o...  43.8 us
    pallas_call x1, Pallas kernels, body(): pl.pallas_call(functools.partial(front_kernel, f_count, owned), out_shape...  23.9 us
    all_to_all x1, starting transfers between devices, body(): lax.all_to_all(bucket, 'dp', split_axis=0, concat_axis=0, tiled=True)  9.51 us
  transfers between devices with their start and end apart: 1, of which 1 were waited for; matrix products, arithmetic and copies ran while one was open for 0% of the time, Pallas kernels for 33%

profile of v7, /device:TPU:1, one launch (start us, length us, event | category | flops | bytes accessed | tf_op | source)
XLA Modules:
  0.0 131.2 jit_solution(54498659532745393)
XLA Ops:
  0.6 23.9 %front_kernel.1 = (bf16[512,512]{1,0:T(8,128)(2,1)}, bf16[512,512]{1,0:T(8,128)(2,1)}, f32[13824,128]{1,0:T(8,128)}, f32[32,216,128]{2,1,0:T(8,128)}) custom-call(s32[26,512]{1,0:T(8,128)} %bitcast.18, f32[3456]{0:T(1024)} %bias.1, bf16[512,3456]{1,0:T(8,128)(2,1)} %cross.1, bf16[512,3456]{1,0:T(8,128)(2,1)} %cot.1, bf16[3456,512]{1,0:T(8,128)(2,1)} %down_hbm.1, ...), custom_call_target="tpu_custom_call" | custom-call | tf_op jit(solution)/shard_map/front_kernel/pallas_call | solution.py:781
  24.5 9.5 %all-to-all-start = ((f32[32,216,128]{2,1,0:T(8,128)}), f32[32,216,128]{2,1,0:T(8,128)}, u32[]{:S(2)}, u32[]{:S(2)}) async-start(f32[32,216,128]{2,1,0:T(8,128)} %get-tuple-element.42), calls=%async_computation | async-start | bytes 7077888 | tf_op jit(solution)/shard_map/all_to_all | solution.py:815
  34.0 43.8 %weights_kernel.1 = (f32[16,4,40,128]{3,2,1,0:T(8,128)}, f32[16,4,32,128]{3,2,1,0:T(8,128)}, f32[16,4,40,128]{3,2,1,0:T(8,128)}, f32[16,4,40,128]{3,2,1,0:T(8,12...) custom-call(bf16[512,512]{1,0:T(8,128)(2,1)} %get-tuple-element.32.hidden, ...), custom_call_target="tpu_custom_call" | custom-call | tf_op jit(solution)/shard_map/weights_kernel/pallas_call | solution.py:817
  77.8 0.6 all-to-all-done.refs_7_
  78.4 50.1 %reduce_kernel.1 = (f32[1024,128]{1,0:T(8,128)}, f32[8,128]{1,0:T(8,128)}, f32[2048,128]{1,0:T(8,128)}, f32[16,128]{1,0:T(8,128)}, f32[4,3456]{1,0:T(4,128)}, /*index=5*/f32[27,512]{1,0:T(8,128)}, f32[1,27]{1,0:T(1,128)}) custom-call(f32[4,4,4,40,128]{4,3,2,1,0:T(8,128)} %bitcast.13, f32[4,4,4,32,128]{4,3,2,1,0:T(8,128)} %bitcast.16, ...), custom_call_target="tpu_custom_call" | custom-call | tf_op jit(solution)/shard_map/reduce_kernel/pallas_call | solution.py:743
  128.5 2.5 %move_kernel.1 = (f32[1024,128]{1,0:T(8,128)}, f32[8,128]{1,0:T(8,128)}, f32[2048,128]{1,0:T(8,128)}, f32[16,128]{1,0:T(8,128)}, f32[4,3456]{1,0:T(4,128)}, /*index=5*/f32[27,512]{1,0:T(8,128)}, f32[1,27]{1,0:T(1,128)}) custom-call(f32[1024,128]{1,0:T(8,128)} %get-tuple-element.43.refs_0_, f32[8,128]{1,0:T(8,128)} %get-tuple-element.44.refs_1_, ...), custom_call_target="tpu_custom_call" | custom-call | tf_op jit(solution)/shard_map/move_kernel/pallas_call | solution.py:752
Async XLA Ops:
  24.5 53.9 %all-to-all-start = ((f32[32,216,128]{2,1,0:T(8,128)}), f32[32,216,128]{2,1,0:T(8,128)}, u32[]{:S(2)}, u32[]{:S(2)}) async-start(f32[32,216,128]{2,1,0:T(8,128)} %get-tuple-element.42), calls=%async_computation | async-start | bytes 7077888 | tf_op jit(solution)/shard_map/all_to_all | solution.py:815

commit v8 on v7

--- a/solution.py
+++ b/solution.py
@@ -180,14 +180,16 @@
 
 
 PORT = (
-    (72, 40, 24, "xzy"),
-    (112, 32, 16, "xzy"),
-    (144, 40, 24, "zxy"),
-    (184, 40, 24, "zxy"),
-    (0, 40, 24, "yxz"),
-    (40, 32, 16, "yzx"),
+    (128, 24, 16, "xzy"),
+    (152, 24, 16, "xzy"),
+    (176, 24, 16, "zxy"),
+    (200, 24, 16, "zxy"),
+    (96, 32, 16, "yxz"),
+    (0, 48, 24, "yxz"),
+    (48, 48, 24, "yzx"),
 )
-N_BULK = 4
+N_BULK = 5
+BEGINS = [1 if p >= N_BULK else 0 for p in range(len(PORT))]
 
 
 def mesh_place():
@@ -196,46 +198,67 @@
     return {"x": dp // 8, "z": (dp // 2) % 4, "y": y}, core, (dp + 1 - 2 * core, y)
 
 
-def sender(send_sems, recv_sems, sent):
-    used = [0]
-
-    def send(src, dst, to):
-        k = used[0]
-        used[0] += 1
-        copy = pltpu.make_async_remote_copy(
-            src_ref=src, dst_ref=dst, send_sem=send_sems.at[k], recv_sem=recv_sems.at[k],
+class Links:
+    def __init__(self, send_sems, recv_sems):
+        self.sems, self.used, self.sent = (send_sems, recv_sems), 0, []
+
+    def base(self, n):
+        self.used += n
+        return self.used - n
+
+    def make(self, k, src, dst, to):
+        return pltpu.make_async_remote_copy(
+            src_ref=src, dst_ref=dst, send_sem=self.sems[0].at[k], recv_sem=self.sems[1].at[k],
             device_id=to, device_id_type=pl.DeviceIdType.MESH,
         )
+
+    def go(self, k, src, dst, to):
+        copy = self.make(k, src(), dst, to())
         copy.start()
-        sent.append(copy)
+        self.sent.append(lambda: self.make(k, src(), dst, to()))
         return copy
 
-    return send
+    def __call__(self, src, dst, to):
+        return self.go(self.base(1), lambda: src, dst, lambda: to)
 
 
 class Reduce:
-    def __init__(self, send, near, at, add, rows, half, lands):
-        self.send, self.near, self.at, self.add = send, near, at, add
-        self.rows, self.half, self.lands = rows, half, lands
+    def __init__(self, links, near, at, add, rows, half, lands):
+        (_, up, far, down), to = near
+        self.links, self.here, self.up, self.down = links, near[0][0], up, down
+        self.at, self.add, self.rows, self.half, self.lands = at, add, rows, half, lands
+        k = links.base(4)
+        self.args = [
+            (k, lambda: at(far, 0, half), lands[0], lambda: to[up]),
+            (k + 1, lambda: at(far, half, rows), lands[1], lambda: to[down]),
+            (k + 2, lambda: at(up, 0, rows), lands[2], lambda: to[up]),
+            (k + 3, lambda: at(down, 0, rows), lands[3], lambda: to[down]),
+        ]
+
+    def go(self, i):
+        k, src, dst, to = self.args[i]
+        self.links.go(k, src, dst, to)
+
+    def got(self, i):
+        k, src, dst, to = self.args[i]
+        self.links.make(k, src(), dst, to()).wait_recv()
 
     def start(self):
-        (_, up, far, down), to = self.near
-        self.c0 = self.send(self.at(far, 0, self.half), self.lands[0], to[up])
-        self.c1 = self.send(self.at(far, self.half, self.rows), self.lands[1], to[down])
+        self.go(0)
+        self.go(1)
 
     def middle(self):
-        (_, up, far, down), to = self.near
-        self.c0.wait_recv()
-        self.add(up, 0, self.half, self.lands[:1])
-        self.c2 = self.send(self.at(up, 0, self.rows), self.lands[2], to[up])
-        self.c1.wait_recv()
-        self.add(down, self.half, self.rows, self.lands[1:2])
-        self.c3 = self.send(self.at(down, 0, self.rows), self.lands[3], to[down])
+        self.got(0)
+        self.add(self.up, 0, self.half, self.lands[:1])
+        self.go(2)
+        self.got(1)
+        self.add(self.down, self.half, self.rows, self.lands[1:2])
+        self.go(3)
 
     def finish(self):
-        self.c2.wait_recv()
-        self.c3.wait_recv()
-        self.add(self.near[0][0], 0, self.rows, self.lands[2:4])
+        self.got(2)
+        self.got(3)
+        self.add(self.here, 0, self.rows, self.lands[2:4])
 
 
 class Direct:
@@ -313,6 +336,48 @@
     near = neighbours(me, core, "y")
     load = pltpu.make_async_copy(values_hbm, values, local_sems.at[0])
 
+    send = Links(send_sems, recv_sems)
+    firsts = range(N_BULK, len(PORT))
+
+    def part(p, c):
+        first, rows = PORT[p][0], PORT[p][1]
+        return both.at[:, c, :, pl.ds(first, rows), :]
+
+    pair_base = send.base(len(PORT))
+    pair_args = lambda p: (pair_base + p, lambda: part(p, 1 - core), pair[p], lambda: partner)
+
+    def add_pair(p):
+        first, rows = PORT[p][0], PORT[p][1]
+        k, src, dst, to = pair_args(p)
+        send.make(k, src(), dst, to()).wait_recv()
+
+        def add(n, _):
+            for y in range(4):
+                both[n, core, y, first : first + rows, :] = both[n, core, y, first : first + rows, :] + pair[p][n, y]
+            return 0
+
+        lax.fori_loop(0, count // 8, add, 0)
+
+    def y_phase(p):
+        first, rows, half, _ = PORT[p]
+
+        def at(t, lo, hi):
+            return both.at[:, core, t, pl.ds(first + lo, hi - lo), :]
+
+        def y_add(t, lo, hi, lands):
+            def add(n, _):
+                v = both[n, core, t, first + lo : first + hi, :]
+                for ref in lands:
+                    v = v + ref[n]
+                both[n, core, t, first + lo : first + hi, :] = v
+                return 0
+
+            lax.fori_loop(0, count // 8, add, 0)
+
+        return Reduce(send, near, at, y_add, rows, half, y_land[p - N_BULK])
+
+    y_sums = {p: y_phase(p) for p in firsts}
+
     @pl.when(g == 0)
     def _():
         greet([partner] + [near[1][t] for t in near[0][1:]])
@@ -322,39 +387,45 @@
             place[t] = place_in[t : t + 1, :]
         freq[...] = jnp.zeros_like(freq)
 
-    inner = cot[...].astype(f32) * cross[...].astype(f32)
-    bias[:, pl.ds(pl.multiple_of(g * wide, wide), wide)] = jnp.sum(inner, axis=0, keepdims=True)
-    u = jnp.dot(hidden_t[...], inner.astype(bf16), preferred_element_type=f32)
-    for k in range(per):
-        up[k * rank : (k + 1) * rank, :] = u[:, k * 128 : (k + 1) * 128]
-    d = dot_tn(cross[...], back_low[...])
-    for k in range(rank // 128):
-        down[pl.ds(pl.multiple_of(k * width + g * wide, 128), wide), :] = d[:, k * 128 : (k + 1) * 128]
-
-    def put_up(n, _):
-        for c in range(2):
-            for y in range(4):
-                i = n * 8 + c * 4 + y
-                for k in range(per):
-                    both[n, c, y, pl.ds(g * per + k, up_rows, stride=cols), :] = up[
-                        pl.ds(k * rank + i * up_rows, up_rows), :
-                    ]
-        return 0
-
-    lax.fori_loop(0, count // 8, put_up, 0)
-
-    @pl.when(g == steps - 1)
+    @pl.when(g < steps)
     def _():
-        sent = []
-        send = sender(send_sems, recv_sems, sent)
-
-        def part(p, c):
-            first, rows = PORT[p][0], PORT[p][1]
-            return both.at[:, c, :, pl.ds(first, rows), :]
-
-        firsts = range(N_BULK, len(PORT))
-        got = {p: send(part(p, 1 - core), pair[p], partner) for p in firsts}
-
+        inner = cot[...].astype(f32) * cross[...].astype(f32)
+        bias[:, pl.ds(pl.multiple_of(g * wide, wide), wide)] = jnp.sum(inner, axis=0, keepdims=True)
+        u = jnp.dot(hidden_t[...], inner.astype(bf16), preferred_element_type=f32)
+        for k in range(per):
+            up[k * rank : (k + 1) * rank, :] = u[:, k * 128 : (k + 1) * 128]
+
+        def put_up(n, _):
+            for c in range(2):
+                for y in range(4):
+                    i = n * 8 + c * 4 + y
+                    for k in range(per):
+                        both[n, c, y, pl.ds(g * per + k, up_rows, stride=cols), :] = up[
+                            pl.ds(k * rank + i * up_rows, up_rows), :
+                        ]
+            return 0
+
+        lax.fori_loop(0, count // 8, put_up, 0)
+
+    @pl.when(g == steps)
+    def _():
+        for p in firsts:
+            send.go(*pair_args(p))
+
+    @pl.when(g >= steps)
+    def _():
+        d = dot_tn(cross[...], back_low[...])
+        for k in range(rank // 128):
+            down[pl.ds(pl.multiple_of(k * width + (g - steps) * wide, 128), wide), :] = d[:, k * 128 : (k + 1) * 128]
+
+    @pl.when(g == 2 * steps - 2)
+    def _():
+        for p in firsts:
+            add_pair(p)
+            y_sums[p].start()
+
+    @pl.when(g == 2 * steps - 1)
+    def _():
         def put_down(n, _):
             for c in range(2):
                 for y in range(4):
@@ -372,7 +443,8 @@
                 :, i * down_rows : (i + 1) * down_rows
             ]
         for p in range(N_BULK):
-            got[p] = send(part(p, 1 - core), pair[p], partner)
+            send.go(*pair_args(p))
+        y_sums[N_BULK].middle()
         load.wait()
         row_iota = lax.broadcasted_iota(i32, (frequent, samples), 0)
 
@@ -385,54 +457,17 @@
             freq[...] += s[:, :128] + s[:, 128:]
             return 0
 
-        def add_pair(p):
-            first, rows = PORT[p][0], PORT[p][1]
-            got[p].wait_recv()
-
-            def add(n, _):
-                for y in range(4):
-                    both[n, core, y, first : first + rows, :] = (
-                        both[n, core, y, first : first + rows, :] + pair[p][n, y]
-                    )
-                return 0
-
-            lax.fori_loop(0, count // 8, add, 0)
-
-        def y_phase(p):
-            first, rows, half, _ = PORT[p]
-
-            def at(t, lo, hi):
-                return both.at[:, core, t, pl.ds(first + lo, hi - lo), :]
-
-            def y_add(t, lo, hi, lands):
-                def add(n, _):
-                    v = both[n, core, t, first + lo : first + hi, :]
-                    for ref in lands:
-                        v = v + ref[n]
-                    both[n, core, t, first + lo : first + hi, :] = v
-                    return 0
-
-                lax.fori_loop(0, count // 8, add, 0)
-
-            return Reduce(send, near, at, y_add, rows, half, y_land[p - N_BULK])
-
         def f_add(t, lands):
             v = f_both[:, core, t]
             for ref in lands:
                 v = v + ref[...]
             f_both[:, core, t] = v
 
-        y_sums = {p: y_phase(p) for p in firsts}
         f_sum = Direct(send, near, lambda t: f_both.at[:, core, t], f_add, f_land)
         pairs = place.shape[0] // 2
-        lax.fori_loop(0, 2, tables, 0)
-        for p in firsts:
-            add_pair(p)
-            y_sums[p].start()
-        lax.fori_loop(2, pairs // 2 + 2, tables, 0)
-        y_sums[N_BULK].middle()
-        lax.fori_loop(pairs // 2 + 2, pairs, tables, 0)
+        lax.fori_loop(0, pairs // 3, tables, 0)
         y_sums[N_BULK + 1].middle()
+        lax.fori_loop(pairs // 3, pairs, tables, 0)
 
         def put_freq(n, _):
             for c in range(2):
@@ -459,8 +494,8 @@
         stores[-1].start()
         for c in stores:
             c.wait()
-        for c in sent:
-            c.wait_send()
+        for c in send.sent:
+            c().wait_send()
 
 
 def params(**kw):
@@ -471,11 +506,11 @@
     it = iter(refs)
     take = lambda n: [next(it) for _ in range(n)]
     pieces = range(len(PORT))
-    begins = [1 if PORT[p][3][0] == "y" else 0 for p in pieces]
+    begins = BEGINS
     loads, (load_f, arrived), given = take(len(PORT)), take(2), take(4)
     new_f, new_fa, new_s, new_sa, g_up, g_down, g_bias = take(7)
     work = take(len(PORT))
-    land = {p: {k: take(4) for k in range(begins[p], 3)} for p in pieces}
+    land = {p: {k: take(3 if k == 2 else 4) for k in range(begins[p], 3)} for p in pieces}
     swork, sland, sgath = next(it), [take(4), take(4)], next(it)
     f_work, fx_land, fz_land, gath = next(it), take(3), take(3), next(it)
     mine, arr, ids, right, acc = take(5)
@@ -484,8 +519,7 @@
     me, core, partner = mesh_place()
     near = {a: neighbours(me, core, a) for a in "xzy"}
     greet([partner] + [near[a][1][t] for a in "xzy" for t in near[a][0][1:]])
-    sent = []
-    send = sender(send_sems, recv_sems, sent)
+    send = Links(send_sems, recv_sems)
 
     def where(dims, done, axis, t, rem=None):
         rem = iter(rem) if rem is not None else None
@@ -523,6 +557,9 @@
             else:
                 lax.fori_loop(0, 16, lambda i, _: (one((i // 4, i % 4)), 0)[1], 0)
 
+        if k == 2:
+            whole = lambda t: at(t, 0, rows)
+            return Direct(send, near[axis], whole, lambda t, lands: add(t, 0, rows, lands), land[p][k])
         return Reduce(send, near[axis], at, add, rows, half, land[p][k])
 
     sums = {(p, k): phase(p, k) for p in pieces for k in range(begins[p], 3)}
@@ -593,7 +630,7 @@
     copy_f, copy_a, *rest = [
         pltpu.make_async_copy(a, b, local_sems.at[len(PORT) + i]) for i, (a, b) in enumerate(more)
     ]
-    for c in [copy_f, copies[0], copies[2], copies[1], copies[3], copy_a, copies[4], copies[5]] + rest:
+    for c in [copy_f, copies[0], copies[2], copies[4], copies[1], copies[3], copy_a, copies[5], copies[6]] + rest:
         c.start()
     slots = arr.shape[1] - 8
     some = ids.shape[0]
@@ -632,75 +669,69 @@
 
     copy_f.wait()
     f_x.start()
-    for p in (0, 2, 1, 3):
+    for p in (0, 2, 4, 1, 3):
         copies[p].wait()
         sums[p, 0].start()
     copy_a.wait()
     lax.fori_loop(0, some, prepare, 0)
     f_x.finish()
     f_z.start()
+    sums[4, 0].middle()
     seg_block(y_far)
     s_red[0].start()
     s_red[1].start()
     sums[0, 0].middle()
     sums[2, 0].middle()
-    seg_block(y_up)
     sums[1, 0].middle()
     sums[3, 0].middle()
-    for p in (4, 5):
+    for p in (5, 6):
         copies[p].wait()
         sums[p, 1].start()
+    seg_block(y_up)
+    f_z.finish()
+    gath[me["x"], me["z"], core, me["y"]] = f_work[me["x"], me["z"]]
+    g_z.start()
     seg_block(y_down)
     s_red[0].middle()
     s_red[1].middle()
-    f_z.finish()
-    gath[me["x"], me["z"], core, me["y"]] = f_work[me["x"], me["z"]]
-    g_z.start()
+    done(4, 0)
     seg_block(me["y"])
     done(0, 0)
     done(2, 0)
+    done(1, 0)
+    done(3, 0)
+    sums[5, 1].middle()
+    sums[6, 1].middle()
     s_red[0].finish()
     s_gat[0].start()
     s_red[1].finish()
     s_gat[1].start()
-    done(1, 0)
-    done(3, 0)
-    sums[4, 1].middle()
-    sums[5, 1].middle()
     g_z.finish()
     g_x.start()
-    sums[0, 1].middle()
-    sums[2, 1].middle()
+    for p in (4, 0, 2, 1, 3):
+        sums[p, 1].middle()
     s_gat[0].middle()
     s_gat[1].middle()
-    done(4, 1)
     done(5, 1)
-    sums[1, 1].middle()
-    sums[3, 1].middle()
+    done(6, 1)
     g_x.finish()
     g_y.start()
-    done(0, 1)
-    done(2, 1)
-    done(1, 1)
-    done(3, 1)
+    for p in (4, 0, 2, 1, 3):
+        done(p, 1)
     for c in rest:
         c.wait()
     s_gat[0].finish()
     s_gat[1].finish()
     row_adagrad(s_table, s_accum, lambda n: sgath[n // 4, pl.ds(pl.multiple_of(n % 4 * 128, 128), 128), :], new_s, new_sa)
-    sums[4, 2].middle()
-    sums[5, 2].middle()
     g_y.finish()
     g_c = send(gath.at[:, :, core], gath.at[:, :, core], partner)
-    for p in (0, 2, 1, 3):
-        sums[p, 2].middle()
-    g_c.wait_recv()
-    row_adagrad(f_table, f_accum, lambda n: gath[n // 2, pl.ds(n % 2 * 2, 2)].reshape(128, 128), new_f, new_fa)
     here = (me["x"], me["z"], me["y"])
-    for p in (4, 5, 0, 2, 1, 3):
+    for p in (5, 6, 4, 0, 2, 1, 3):
         sums[p, 2].finish()
         first, rows = PORT[p][:2]
         mine[first : first + rows, :] = work[p][here[:2] if begins[p] else here]
+    g_c.wait_recv()
+    row_adagrad(f_table, f_accum, lambda n: gath[n // 2, pl.ds(n % 2 * 2, 2)].reshape(128, 128), new_f, new_fa)
     up_rows, down_rows = g_up.shape[0], g_down.shape[0]
     cols = g_up.shape[1] // 128
     for c in range(cols):
@@ -709,18 +740,18 @@
     for c in range(cols):
         g_down[:, c * 128 : (c + 1) * 128] = mine[pl.ds(first + c, down_rows, stride=cols), :]
     g_bias[...] = mine[first + down_rows * cols : first + down_rows * cols + 1, 0:down_rows]
-    for c in sent:
-        c.wait_send()
+    for c in send.sent:
+        c().wait_send()
 
 
 def reduce_scratch(owned, frequent, arrived):
     v = lambda *s: pltpu.VMEM(s, f32)
-    begins = [1 if order[0] == "y" else 0 for _, _, _, order in PORT]
+    begins = BEGINS
     out = [v(*(4,) * (3 - b), r, 128) for b, (_, r, _, _) in zip(begins, PORT)]
     for b, (_, r, h, _) in zip(begins, PORT):
         for k in range(b, 3):
             lead = (4,) * (2 - k)
-            out += [v(*lead, h, 128), v(*lead, r - h, 128), v(*lead, r, 128), v(*lead, r, 128)]
+            out += [v(*lead, n, 128) for n in ((r, r, r) if k == 2 else (h, r - h, r, r))]
     q = owned // 4
     out += [v(4, q, 128)] + [v(q // 4, 128), v(q // 4, 128), v(q // 2, 128), v(q // 2, 128)] * 2 + [v(4, q, 128)]
     out += [v(4, 4, 8, 128)] + [v(4, 8, 128)] * 3 + [v(8, 128)] * 3 + [v(4, 4, 2, 4, 8, 128)]
@@ -816,7 +847,7 @@
 
     parts = pl.pallas_call(
         functools.partial(weights_kernel, steps),
-        grid=(steps,),
+        grid=(2 * steps,),
         out_shape=tuple(
             jax.ShapeDtypeStruct(shape, f32)
             for shape in [(16, 4, r, 128) for _, r, _, _ in PORT[:N_BULK]]
@@ -826,8 +857,8 @@
         in_specs=[
             pl.BlockSpec((samples, rank), lambda g: (0, 0)),
             pl.BlockSpec((samples, rank), lambda g: (0, 0)),
-            pl.BlockSpec((samples, wide), lambda g: (0, g)),
-            pl.BlockSpec((samples, wide), lambda g: (0, g)),
+            pl.BlockSpec((samples, wide), lambda g: (0, lax.rem(g, steps))),
+            pl.BlockSpec((samples, wide), lambda g: (0, jnp.minimum(g, steps - 1))),
             anyw,
             pl.BlockSpec((tables, samples), lambda g: (0, 0)),
         ],

time: 132 us -> 138 us (1.045)
  Pallas kernels: 120 us -> 127 us
    pallas_call x1, Pallas kernels: 43.8 us -> 50.5 us  [body(): pl.pallas_call(functools.partial(weights_kernel, steps), grid=(2 * steps,...]
  transfers between devices with their start and end apart: 1 -> 1, of which waited for: 1 -> 0; matrix products, arithmetic and copies ran while one was open for 0% -> 0% of each run, Pallas kernels for 33% -> 37%
where the time goes in v8:
time: 138 us; the launch traced here: 137 us
  Pallas kernels  127 us (92%)
  starting transfers between devices  9.51 us (7%)
    pallas_call x1, Pallas kernels, body(): pl.pallas_call(functools.partial(weights_kernel, steps), grid=(2 * steps,...  50.5 us
    pallas_call x1, Pallas kernels, reduce_all(): pl.pallas_call(reduce_kernel, out_shape=tuple(shapes), in_specs=[anyw] *...  50 us
    pallas_call x1, Pallas kernels, body(): pl.pallas_call(functools.partial(front_kernel, f_count, owned), out_shape...  23.9 us
    all_to_all x1, starting transfers between devices, body(): lax.all_to_all(bucket, 'dp', split_axis=0, concat_axis=0, tiled=True)  9.51 us
  transfers between devices with their start and end apart: 1, of which 0 were waited for; matrix products, arithmetic and copies ran while one was open for 0% of the time, Pallas kernels for 37%

profile of v8, /device:TPU:1, one launch (start us, length us, event | category | flops | bytes accessed | tf_op | source)
XLA Modules:
  0.0 137.2 jit_solution(5495426343519292812)
XLA Ops:
  0.6 23.9 %front_kernel.1 = (bf16[512,512]{1,0:T(8,128)(2,1)}, bf16[512,512]{1,0:T(8,128)(2,1)}, f32[13824,128]{1,0:T(8,128)}, f32[32,216,128]{2,1,0:T(8,128)}) custom-call(s32[26,512]{1,0:T(8,128)} %bitcast.21, f32[3456]{0:T(1024)} %bias.1, bf16[512,3456]{1,0:T(8,128)(2,1)} %cross.1, bf16[512,3456]{1,0:T(8,128)(2,1)} %cot.1, bf16[3456,512]{1,0:T(8,128)(2,1)} %down_hbm.1, ...), custom_call_target="tpu_custom_call" | custom-call | tf_op jit(solution)/shard_map/front_kernel/pallas_call | solution.py:812
  24.5 9.5 %all-to-all-start = ((f32[32,216,128]{2,1,0:T(8,128)}), f32[32,216,128]{2,1,0:T(8,128)}, u32[]{:S(2)}, u32[]{:S(2)}) async-start(f32[32,216,128]{2,1,0:T(8,128)} %get-tuple-element.44), calls=%async_computation | async-start | bytes 7077888 | tf_op jit(solution)/shard_map/all_to_all | solution.py:846
  34.0 50.5 %weights_kernel.1 = (f32[16,4,24,128]{3,2,1,0:T(8,128)}, f32[16,4,24,128]{3,2,1,0:T(8,128)}, f32[16,4,24,128]{3,2,1,0:T(8,128)}, f32[16,4,24,128]{3,2,1,0:T(8,12...) custom-call(bf16[512,512]{1,0:T(8,128)(2,1)} %get-tuple-element.33.hid, ...), custom_call_target="tpu_custom_call" | custom-call | tf_op jit(solution)/shard_map/weights_kernel/pallas_call | solution.py:848
  84.6 0.0 all-to-all-done.refs_8_
  84.6 50.0 %reduce_kernel.1 = (f32[1024,128]{1,0:T(8,128)}, f32[8,128]{1,0:T(8,128)}, f32[2048,128]{1,0:T(8,128)}, f32[16,128]{1,0:T(8,128)}, f32[4,3456]{1,0:T(4,128)}, /*index=5*/f32[27,512]{1,0:T(8,128)}, f32[1,27]{1,0:T(1,128)}) custom-call(f32[4,4,4,24,128]{4,3,2,1,0:T(8,128)} %bitcast.15, f32[4,4,4,24,128]{4,3,2,1,0:T(8,128)} %bitcast.16, ...), custom_call_target="tpu_custom_call" | custom-call | tf_op jit(solution)/shard_map/reduce_kernel/pallas_call | solution.py:774
  134.6 2.5 %move_kernel.1 = (f32[1024,128]{1,0:T(8,128)}, f32[8,128]{1,0:T(8,128)}, f32[2048,128]{1,0:T(8,128)}, f32[16,128]{1,0:T(8,128)}, f32[4,3456]{1,0:T(4,128)}, /*index=5*/f32[27,512]{1,0:T(8,128)}, f32[1,27]{1,0:T(1,128)}) custom-call(f32[1024,128]{1,0:T(8,128)} %get-tuple-element.45.refs_0_, f32[8,128]{1,0:T(8,128)} %get-tuple-element.46.refs_1_, ...), custom_call_target="tpu_custom_call" | custom-call | tf_op jit(solution)/shard_map/move_kernel/pallas_call | solution.py:783
Async XLA Ops:
  24.5 60.0 %all-to-all-start = ((f32[32,216,128]{2,1,0:T(8,128)}), f32[32,216,128]{2,1,0:T(8,128)}, u32[]{:S(2)}, u32[]{:S(2)}) async-start(f32[32,216,128]{2,1,0:T(8,128)} %get-tuple-element.44), calls=%async_computation | async-start | bytes 7077888 | tf_op jit(solution)/shard_map/all_to_all | solution.py:846

commit v9 on v8

--- a/solution.py
+++ b/solution.py
@@ -180,13 +180,13 @@
 
 
 PORT = (
-    (128, 24, 16, "xzy"),
-    (152, 24, 16, "xzy"),
-    (176, 24, 16, "zxy"),
-    (200, 24, 16, "zxy"),
-    (96, 32, 16, "yxz"),
-    (0, 48, 24, "yxz"),
-    (48, 48, 24, "yzx"),
+    (104, 32, 16, "xzy"),
+    (136, 24, 16, "xzy"),
+    (160, 32, 16, "zxy"),
+    (192, 32, 16, "zxy"),
+    (72, 32, 16, "yxz"),
+    (0, 40, 24, "yxz"),
+    (40, 32, 16, "yzx"),
 )
 N_BULK = 5
 BEGINS = [1 if p >= N_BULK else 0 for p in range(len(PORT))]
@@ -305,10 +305,11 @@
     return [(me[axis] + d) % 4 for d in range(4)], Ids(device)
 
 
-def greet(peers):
+def greet(peers, meanwhile=lambda: None):
     barrier = pltpu.get_barrier_semaphore()
     for peer in peers:
         pl.semaphore_signal(barrier, inc=1, device_id=peer, device_id_type=pl.DeviceIdType.MESH)
+    meanwhile()
     pl.semaphore_wait(barrier, len(peers))
 
 
@@ -387,45 +388,32 @@
             place[t] = place_in[t : t + 1, :]
         freq[...] = jnp.zeros_like(freq)
 
-    @pl.when(g < steps)
-    def _():
-        inner = cot[...].astype(f32) * cross[...].astype(f32)
-        bias[:, pl.ds(pl.multiple_of(g * wide, wide), wide)] = jnp.sum(inner, axis=0, keepdims=True)
-        u = jnp.dot(hidden_t[...], inner.astype(bf16), preferred_element_type=f32)
-        for k in range(per):
-            up[k * rank : (k + 1) * rank, :] = u[:, k * 128 : (k + 1) * 128]
-
-        def put_up(n, _):
-            for c in range(2):
-                for y in range(4):
-                    i = n * 8 + c * 4 + y
-                    for k in range(per):
-                        both[n, c, y, pl.ds(g * per + k, up_rows, stride=cols), :] = up[
-                            pl.ds(k * rank + i * up_rows, up_rows), :
-                        ]
-            return 0
-
-        lax.fori_loop(0, count // 8, put_up, 0)
-
-    @pl.when(g == steps)
+    inner = cot[...].astype(f32) * cross[...].astype(f32)
+    bias[:, pl.ds(pl.multiple_of(g * wide, wide), wide)] = jnp.sum(inner, axis=0, keepdims=True)
+    u = jnp.dot(hidden_t[...], inner.astype(bf16), preferred_element_type=f32)
+    for k in range(per):
+        up[k * rank : (k + 1) * rank, :] = u[:, k * 128 : (k + 1) * 128]
+    d = dot_tn(cross[...], back_low[...])
+    for k in range(rank // 128):
+        down[pl.ds(pl.multiple_of(k * width + g * wide, 128), wide), :] = d[:, k * 128 : (k + 1) * 128]
+
+    def put_up(n, _):
+        for c in range(2):
+            for y in range(4):
+                i = n * 8 + c * 4 + y
+                for k in range(per):
+                    both[n, c, y, pl.ds(g * per + k, up_rows, stride=cols), :] = up[
+                        pl.ds(k * rank + i * up_rows, up_rows), :
+                    ]
+        return 0
+
+    lax.fori_loop(0, count // 8, put_up, 0)
+
+    @pl.when(g == steps - 1)
     def _():
         for p in firsts:
             send.go(*pair_args(p))
 
-    @pl.when(g >= steps)
-    def _():
-        d = dot_tn(cross[...], back_low[...])
-        for k in range(rank // 128):
-            down[pl.ds(pl.multiple_of(k * width + (g - steps) * wide, 128), wide), :] = d[:, k * 128 : (k + 1) * 128]
-
-    @pl.when(g == 2 * steps - 2)
-    def _():
-        for p in firsts:
-            add_pair(p)
-            y_sums[p].start()
-
-    @pl.when(g == 2 * steps - 1)
-    def _():
         def put_down(n, _):
             for c in range(2):
                 for y in range(4):
@@ -444,7 +432,6 @@
             ]
         for p in range(N_BULK):
             send.go(*pair_args(p))
-        y_sums[N_BULK].middle()
         load.wait()
         row_iota = lax.broadcasted_iota(i32, (frequent, samples), 0)
 
@@ -465,9 +452,14 @@
 
         f_sum = Direct(send, near, lambda t: f_both.at[:, core, t], f_add, f_land)
         pairs = place.shape[0] // 2
-        lax.fori_loop(0, pairs // 3, tables, 0)
+        lax.fori_loop(0, 2, tables, 0)
+        for p in firsts:
+            add_pair(p)
+            y_sums[p].start()
+        lax.fori_loop(2, pairs // 2 + 2, tables, 0)
+        y_sums[N_BULK].middle()
+        lax.fori_loop(pairs // 2 + 2, pairs, tables, 0)
         y_sums[N_BULK + 1].middle()
-        lax.fori_loop(pairs // 3, pairs, tables, 0)
 
         def put_freq(n, _):
             for c in range(2):
@@ -518,7 +510,17 @@
     send_sems, recv_sems, local_sems = take(3)
     me, core, partner = mesh_place()
     near = {a: neighbours(me, core, a) for a in "xzy"}
-    greet([partner] + [near[a][1][t] for a in "xzy" for t in near[a][0][1:]])
+    copies = [pltpu.make_async_copy(loads[p], work[p], local_sems.at[p]) for p in pieces]
+    more = [(load_f, f_work), (arrived, arr)] + list(zip(given, held))
+    copy_f, copy_a, *rest = [
+        pltpu.make_async_copy(a, b, local_sems.at[len(PORT) + i]) for i, (a, b) in enumerate(more)
+    ]
+
+    def load_all():
+        for c in [copy_f, copies[0], copies[2], copies[4], copy_a, copies[1], copies[3], copies[5], copies[6]] + rest:
+            c.start()
+
+    greet([partner] + [near[a][1][t] for a in "xzy" for t in near[a][0][1:]], load_all)
     send = Links(send_sems, recv_sems)
 
     def where(dims, done, axis, t, rem=None):
@@ -625,13 +627,6 @@
             self.c3.wait_recv()
 
     s_gat = [SegGather(0), SegGather(1)]
-    copies = [pltpu.make_async_copy(loads[p], work[p], local_sems.at[p]) for p in pieces]
-    more = [(load_f, f_work), (arrived, arr)] + list(zip(given, held))
-    copy_f, copy_a, *rest = [
-        pltpu.make_async_copy(a, b, local_sems.at[len(PORT) + i]) for i, (a, b) in enumerate(more)
-    ]
-    for c in [copy_f, copies[0], copies[2], copies[4], copies[1], copies[3], copy_a, copies[5], copies[6]] + rest:
-        c.start()
     slots = arr.shape[1] - 8
     some = ids.shape[0]
     each_of = arr.shape[0] // some
@@ -755,7 +750,7 @@
     q = owned // 4
     out += [v(4, q, 128)] + [v(q // 4, 128), v(q // 4, 128), v(q // 2, 128), v(q // 2, 128)] * 2 + [v(4, q, 128)]
     out += [v(4, 4, 8, 128)] + [v(4, 8, 128)] * 3 + [v(8, 128)] * 3 + [v(4, 4, 2, 4, 8, 128)]
-    n = arrived.shape[0] // 4
+    n = arrived.shape[0] // 16
     flat = arrived.shape[0] * (arrived.shape[1] - 8)
     out += [v(max(a + r for a, r, _, _ in PORT), 128)]
     out += [v(*arrived.shape), pltpu.VMEM((n, 1, flat // n), i32), pltpu.VMEM((flat, 256), bf16), v(q, 256)]
@@ -847,7 +842,7 @@
 
     parts = pl.pallas_call(
         functools.partial(weights_kernel, steps),
-        grid=(2 * steps,),
+        grid=(steps,),
         out_shape=tuple(
             jax.ShapeDtypeStruct(shape, f32)
             for shape in [(16, 4, r, 128) for _, r, _, _ in PORT[:N_BULK]]
@@ -857,8 +852,8 @@
         in_specs=[
             pl.BlockSpec((samples, rank), lambda g: (0, 0)),
             pl.BlockSpec((samples, rank), lambda g: (0, 0)),
-            pl.BlockSpec((samples, wide), lambda g: (0, lax.rem(g, steps))),
-            pl.BlockSpec((samples, wide), lambda g: (0, jnp.minimum(g, steps - 1))),
+            pl.BlockSpec((samples, wide), lambda g: (0, g)),
+            pl.BlockSpec((samples, wide), lambda g: (0, g)),
             anyw,
             pl.BlockSpec((tables, samples), lambda g: (0, 0)),
         ],

time: 138 us -> 129 us (0.935)
  Pallas kernels: 127 us -> 118 us
    pallas_call x1, Pallas kernels: 50.5 us -> 43.8 us  [body(): pl.pallas_call(functools.partial(weights_kernel, steps), grid=(steps,), o...]
    pallas_call x1, Pallas kernels: 50 us -> 47.9 us  [reduce_all(): pl.pallas_call(reduce_kernel, out_shape=tuple(shapes), in_specs=[anyw] *...]
  transfers between devices with their start and end apart: 1 -> 1, of which waited for: 0 -> 1; matrix products, arithmetic and copies ran while one was open for 0% -> 0% of each run, Pallas kernels for 37% -> 34%
where the time goes in v9:
time: 129 us
  Pallas kernels  118 us (91%)
  starting transfers between devices  9.51 us (7%)
    pallas_call x1, Pallas kernels, reduce_all(): pl.pallas_call(reduce_kernel, out_shape=tuple(shapes), in_specs=[anyw] *...  47.9 us
    pallas_call x1, Pallas kernels, body(): pl.pallas_call(functools.partial(weights_kernel, steps), grid=(steps,), o...  43.8 us
    pallas_call x1, Pallas kernels, body(): pl.pallas_call(functools.partial(front_kernel, f_count, owned), out_shape...  23.9 us
    all_to_all x1, starting transfers between devices, body(): lax.all_to_all(bucket, 'dp', split_axis=0, concat_axis=0, tiled=True)  9.51 us
  transfers between devices with their start and end apart: 1, of which 1 were waited for; matrix products, arithmetic and copies ran while one was open for 0% of the time, Pallas kernels for 34%

profile of v9, /device:TPU:1, one launch (start us, length us, event | category | flops | bytes accessed | tf_op | source)
XLA Modules:
  0.0 128.9 jit_solution(8445063921134547928)
XLA Ops:
  0.6 23.9 %front_kernel.1 = (bf16[512,512]{1,0:T(8,128)(2,1)}, bf16[512,512]{1,0:T(8,128)(2,1)}, f32[13824,128]{1,0:T(8,128)}, f32[32,216,128]{2,1,0:T(8,128)}) custom-call(s32[26,512]{1,0:T(8,128)} %bitcast.20, f32[3456]{0:T(1024)} %bias.1, bf16[512,3456]{1,0:T(8,128)(2,1)} %cross.1, bf16[512,3456]{1,0:T(8,128)(2,1)} %cot.1, bf16[3456,512]{1,0:T(8,128)(2,1)} %down_hbm.1, ...), custom_call_target="tpu_custom_call" | custom-call | tf_op jit(solution)/shard_map/front_kernel/pallas_call | solution.py:807
  24.5 9.5 %all-to-all-start = ((f32[32,216,128]{2,1,0:T(8,128)}), f32[32,216,128]{2,1,0:T(8,128)}, u32[]{:S(2)}, u32[]{:S(2)}) async-start(f32[32,216,128]{2,1,0:T(8,128)} %get-tuple-element.44), calls=%async_computation | async-start | bytes 7077888 | tf_op jit(solution)/shard_map/all_to_all | solution.py:841
  34.0 43.8 %weights_kernel.1 = (f32[16,4,32,128]{3,2,1,0:T(8,128)}, f32[16,4,24,128]{3,2,1,0:T(8,128)}, f32[16,4,32,128]{3,2,1,0:T(8,128)}, f32[16,4,32,128]{3,2,1,0:T(8,12...) custom-call(bf16[512,512]{1,0:T(8,128)(2,1)} %get-tuple-element.33.hid, ...), custom_call_target="tpu_custom_call" | custom-call | tf_op jit(solution)/shard_map/weights_kernel/pallas_call | solution.py:843
  77.8 0.6 all-to-all-done.refs_8_
  78.4 47.9 %reduce_kernel.1 = (f32[1024,128]{1,0:T(8,128)}, f32[8,128]{1,0:T(8,128)}, f32[2048,128]{1,0:T(8,128)}, f32[16,128]{1,0:T(8,128)}, f32[4,3456]{1,0:T(4,128)}, /*index=5*/f32[27,512]{1,0:T(8,128)}, f32[1,27]{1,0:T(1,128)}) custom-call(f32[4,4,4,32,128]{4,3,2,1,0:T(8,128)} %bitcast.14, f32[4,4,4,24,128]{4,3,2,1,0:T(8,128)} %bitcast.18, ...), custom_call_target="tpu_custom_call" | custom-call | tf_op jit(solution)/shard_map/reduce_kernel/pallas_call | solution.py:769
  126.3 2.5 %move_kernel.1 = (f32[1024,128]{1,0:T(8,128)}, f32[8,128]{1,0:T(8,128)}, f32[2048,128]{1,0:T(8,128)}, f32[16,128]{1,0:T(8,128)}, f32[4,3456]{1,0:T(4,128)}, /*index=5*/f32[27,512]{1,0:T(8,128)}, f32[1,27]{1,0:T(1,128)}) custom-call(f32[1024,128]{1,0:T(8,128)} %get-tuple-element.45.refs_0_, f32[8,128]{1,0:T(8,128)} %get-tuple-element.46.refs_1_, ...), custom_call_target="tpu_custom_call" | custom-call | tf_op jit(solution)/shard_map/move_kernel/pallas_call | solution.py:778
Async XLA Ops:
  24.5 53.9 %all-to-all-start = ((f32[32,216,128]{2,1,0:T(8,128)}), f32[32,216,128]{2,1,0:T(8,128)}, u32[]{:S(2)}, u32[]{:S(2)}) async-start(f32[32,216,128]{2,1,0:T(8,128)} %get-tuple-element.44), calls=%async_computation | async-start | bytes 7077888 | tf_op jit(solution)/shard_map/all_to_all | solution.py:841

commit v10 on v9

--- a/solution.py
+++ b/solution.py
@@ -59,7 +59,7 @@
 
 def index_work(frequent, owned, place, idx, row_a, row_b, hot, cum):
     tables, samples = place.shape
-    owners, slots = idx.shape
+    owners, slots = idx.shape[0], 256
     at = lax.broadcasted_iota(i32, (1, samples), 1)
     owner_iota = lax.broadcasted_iota(i32, (owners, samples), 0)
     tri = one_hot(
@@ -91,10 +91,16 @@
         ]
         left = jnp.concatenate(parts, axis=0).astype(bf16)
         total = total + dot_nt(left, one_hot(slot_iota == rank))
-    idx[...] = (total[:owners] * 128.0 + total[owners : 2 * owners]).astype(i32)
+    found = jnp.maximum((total[:owners] * 128.0 + total[owners : 2 * owners]).astype(i32), samples)
+    idx[:, 0, :] = found[:, :128]
+    idx[:, 1, :] = found[:, 128:]
     row = (total[2 * owners : 3 * owners] - 1.0) * 128.0 + total[3 * owners :]
     row_a[...] = row[:, :128]
     row_b[...] = row[:, 128:]
+
+
+def spans(first, end, most):
+    return [(at, min(most, end - at)) for at in range(first, end, most)]
 
 
 def front_kernel(
@@ -104,61 +110,53 @@
 ):
     samples = hidden.shape[0]
     emb = values.shape[1]
-    pieces = in_sems.shape[0]
-    steps = v_sems.shape[0]
-    wide = cross.shape[1] // steps
-    thin = cross.shape[1] // pieces
-    per = wide // emb
+    width = cross.shape[1]
+    lows = spans(0, width, 1280)
+    highs = spans(emb, width, 1280)
     owners = bucket.shape[0]
     slots = bucket.shape[1] - 8
 
-    def loads(g):
-        cols = pl.ds(pl.multiple_of(g * thin, 128), thin)
-        return [
+    loads = []
+    for g, (at, wide) in enumerate(lows):
+        cols = pl.ds(at, wide)
+        loads.append([
             pltpu.make_async_copy(cross_hbm.at[:, cols], cross.at[:, cols], in_sems.at[g, 0]),
             pltpu.make_async_copy(cot_hbm.at[:, cols], cot.at[:, cols], in_sems.at[g, 1]),
             pltpu.make_async_copy(down_hbm.at[cols, :], down.at[cols, :], in_sems.at[g, 2]),
             pltpu.make_async_copy(up_hbm.at[:, cols], up.at[:, cols], in_sems.at[g, 3]),
-        ]
-
-    for g in range(pieces):
-        for c in loads(g):
+        ])
+    for group in loads:
+        for c in group:
             c.start()
     index_work(frequent, owned, place, idx_v, row_a, row_b, hot, cum)
     to_scalar = pltpu.make_async_copy(idx_v, idx, i_sem)
     to_scalar.start()
-    h_acc[...] = jnp.zeros_like(h_acc)
-    b_acc[...] = jnp.zeros_like(b_acc)
-
-    def low(g, _):
-        for n in range(pieces // steps):
-            for c in loads(g * (pieces // steps) + n):
-                c.wait()
-        cols = pl.ds(pl.multiple_of(g * wide, wide), wide)
-        x = cross[:, cols]
-        inner = (cot[:, cols].astype(f32) * x.astype(f32)).astype(bf16)
-        h_acc[...] += jnp.dot(x, down[cols, :], preferred_element_type=f32)
-        b_acc[...] += dot_nt(inner, up[:, cols])
-        return 0
-
-    lax.fori_loop(0, steps, low, 0)
+    for g, (at, wide) in enumerate(lows):
+        for c in loads[g]:
+            c.wait()
+        x = cross[:, at : at + wide]
+        inner = (cot[:, at : at + wide].astype(f32) * x.astype(f32)).astype(bf16)
+        h = jnp.dot(x, down[at : at + wide, :], preferred_element_type=f32)
+        b = dot_nt(inner, up[:, at : at + wide])
+        if g == 0:
+            h_acc[...] = h
+            b_acc[...] = b
+        else:
+            h_acc[...] += h
+            b_acc[...] += b
     hidden[...] = h_acc[...].astype(bf16)
     back_low[...] = b_acc[...].astype(bf16)
-
-    def store(g):
-        part = pl.ds(pl.multiple_of(g * per * samples, 128), per * samples)
-        return pltpu.make_async_copy(values.at[part], values_hbm.at[part], v_sems.at[g])
-
-    def high(g, _):
-        cols = pl.ds(pl.multiple_of(g * wide, wide), wide)
-        scaled = jnp.dot(hidden[...], up[:, cols], preferred_element_type=f32) + bias[cols].reshape(1, wide)
-        v = cot[:, cols].astype(f32) * (scaled + 1.0) + dot_nt(back_low[...], down[cols, :])
-        for k in range(per):
-            values[pl.ds(pl.multiple_of((g * per + k) * samples, 128), samples), :] = v[:, k * emb : (k + 1) * emb]
-        store(g).start()
-        return 0
-
-    lax.fori_loop(0, steps, high, 0)
+    stores = []
+    for g, (at, wide) in enumerate(highs):
+        scaled = jnp.dot(hidden[...], up[:, at : at + wide], preferred_element_type=f32)
+        scaled = scaled + bias[pl.ds(at, wide)].reshape(1, wide)
+        v = cot[:, at : at + wide].astype(f32) * (scaled + 1.0) + dot_nt(back_low[...], down[at : at + wide, :])
+        for k in range(wide // emb):
+            first = (at // emb + k) * samples
+            values[first : first + samples, :] = v[:, k * emb : (k + 1) * emb]
+        part = pl.ds(at // emb * samples, wide // emb * samples)
+        stores.append(pltpu.make_async_copy(values.at[part], values_hbm.at[part], v_sems.at[g]))
+        stores[-1].start()
     to_scalar.wait()
 
     def ship(o):
@@ -166,7 +164,7 @@
 
     def pick(o, _):
         for k in range(slots):
-            src = idx[o, k]
+            src = idx[o, k // 128, k % 128]
             bucket[o, k : k + 1, :] = values[pl.ds(src, 1), :]
         bucket[o, slots : slots + 8, :] = jnp.zeros((8, emb), f32)
         bucket[o, slots : slots + 1, :] = row_a[pl.ds(o, 1), :]
@@ -175,7 +173,8 @@
         return 0
 
     lax.fori_loop(0, owners, pick, 0)
-    lax.fori_loop(0, steps, lambda g, _: (store(g).wait(), 0)[1], 0)
+    for c in stores:
+        c.wait()
     lax.fori_loop(0, owners, lambda o, _: (ship(o).wait(), 0)[1], 0)
 
 
@@ -823,10 +822,10 @@
             pltpu.VMEM((shards, capacity + 8, emb), f32),
             pltpu.VMEM((tables * shards, samples), bf16),
             pltpu.VMEM((tables * shards, samples), f32),
-            pltpu.VMEM((shards, 256), i32),
+            pltpu.VMEM((shards, 2, 128), i32),
             pltpu.VMEM((shards, 128), f32),
             pltpu.VMEM((shards, 128), f32),
-            pltpu.SMEM((shards, 256), i32),
+            pltpu.SMEM((shards, 2, 128), i32),
             pltpu.VMEM((samples, rank), f32),
             pltpu.VMEM((samples, rank), f32),
             pltpu.SemaphoreType.DMA((steps, 4)),

time: 129 us -> 131 us (1.016)
  Pallas kernels: 118 us -> 120 us
    pallas_call x1, Pallas kernels: 23.9 us -> 25.6 us  [body(): pl.pallas_call(functools.partial(front_kernel, f_count, owned), out_shape...]
  transfers between devices with their start and end apart: 1 -> 1, of which waited for: 1 -> 1; matrix products, arithmetic and copies ran while one was open for 0% -> 0% of each run, Pallas kernels for 34% -> 33%
where the time goes in v10:
time: 131 us
  Pallas kernels  120 us (92%)
  starting transfers between devices  9.49 us (7%)
    pallas_call x1, Pallas kernels, reduce_all(): pl.pallas_call(reduce_kernel, out_shape=tuple(shapes), in_specs=[anyw] *...  48 us
    pallas_call x1, Pallas kernels, body(): pl.pallas_call(functools.partial(weights_kernel, steps), grid=(steps,), o...  43.6 us
    pallas_call x1, Pallas kernels, body(): pl.pallas_call(functools.partial(front_kernel, f_count, owned), out_shape...  25.6 us
    all_to_all x1, starting transfers between devices, body(): lax.all_to_all(bucket, 'dp', split_axis=0, concat_axis=0, tiled=True)  9.49 us
  transfers between devices with their start and end apart: 1, of which 1 were waited for; matrix products, arithmetic and copies ran while one was open for 0% of the time, Pallas kernels for 33%

profile of v10, /device:TPU:1, one launch (start us, length us, event | category | flops | bytes accessed | tf_op | source)
XLA Modules:
  0.0 130.8 jit_solution(13176744996582190675)
XLA Ops:
  0.6 25.6 %front_kernel.1 = (bf16[512,512]{1,0:T(8,128)(2,1)}, bf16[512,512]{1,0:T(8,128)(2,1)}, f32[13824,128]{1,0:T(8,128)}, f32[32,216,128]{2,1,0:T(8,128)}) custom-call(s32[26,512]{1,0:T(8,128)} %bitcast.20, f32[3456]{0:T(1024)} %bias.1, bf16[512,3456]{1,0:T(8,128)(2,1)} %cross.1, bf16[512,3456]{1,0:T(8,128)(2,1)} %cot.1, bf16[3456,512]{1,0:T(8,128)(2,1)} %down_hbm.1, ...), custom_call_target="tpu_custom_call" | custom-call | tf_op jit(solution)/shard_map/front_kernel/pallas_call | solution.py:806
  26.2 9.5 %all-to-all-start = ((f32[32,216,128]{2,1,0:T(8,128)}), f32[32,216,128]{2,1,0:T(8,128)}, u32[]{:S(2)}, u32[]{:S(2)}) async-start(f32[32,216,128]{2,1,0:T(8,128)} %get-tuple-element.44), calls=%async_computation | async-start | bytes 7077888 | tf_op jit(solution)/shard_map/all_to_all | solution.py:840
  35.7 43.6 %weights_kernel.1 = (f32[16,4,32,128]{3,2,1,0:T(8,128)}, f32[16,4,24,128]{3,2,1,0:T(8,128)}, f32[16,4,32,128]{3,2,1,0:T(8,128)}, f32[16,4,32,128]{3,2,1,0:T(8,12...) custom-call(bf16[512,512]{1,0:T(8,128)(2,1)} %get-tuple-element.33.hid, ...), custom_call_target="tpu_custom_call" | custom-call | tf_op jit(solution)/shard_map/weights_kernel/pallas_call | solution.py:842
  79.3 0.8 all-to-all-done.refs_8_
  80.1 48.0 %reduce_kernel.1 = (f32[1024,128]{1,0:T(8,128)}, f32[8,128]{1,0:T(8,128)}, f32[2048,128]{1,0:T(8,128)}, f32[16,128]{1,0:T(8,128)}, f32[4,3456]{1,0:T(4,128)}, /*index=5*/f32[27,512]{1,0:T(8,128)}, f32[1,27]{1,0:T(1,128)}) custom-call(f32[4,4,4,32,128]{4,3,2,1,0:T(8,128)} %bitcast.14, f32[4,4,4,24,128]{4,3,2,1,0:T(8,128)} %bitcast.18, ...), custom_call_target="tpu_custom_call" | custom-call | tf_op jit(solution)/shard_map/reduce_kernel/pallas_call | solution.py:768
  128.1 2.5 %move_kernel.1 = (f32[1024,128]{1,0:T(8,128)}, f32[8,128]{1,0:T(8,128)}, f32[2048,128]{1,0:T(8,128)}, f32[16,128]{1,0:T(8,128)}, f32[4,3456]{1,0:T(4,128)}, /*index=5*/f32[27,512]{1,0:T(8,128)}, f32[1,27]{1,0:T(1,128)}) custom-call(f32[1024,128]{1,0:T(8,128)} %get-tuple-element.45.refs_0_, f32[8,128]{1,0:T(8,128)} %get-tuple-element.46.refs_1_, ...), custom_call_target="tpu_custom_call" | custom-call | tf_op jit(solution)/shard_map/move_kernel/pallas_call | solution.py:777
Async XLA Ops:
  26.2 53.9 %all-to-all-start = ((f32[32,216,128]{2,1,0:T(8,128)}), f32[32,216,128]{2,1,0:T(8,128)}, u32[]{:S(2)}, u32[]{:S(2)}) async-start(f32[32,216,128]{2,1,0:T(8,128)} %get-tuple-element.44), calls=%async_computation | async-start | bytes 7077888 | tf_op jit(solution)/shard_map/all_to_all | solution.py:840

commit v11 on v9

--- a/solution.py
+++ b/solution.py
@@ -59,7 +59,7 @@
 
 def index_work(frequent, owned, place, idx, row_a, row_b, hot, cum):
     tables, samples = place.shape
-    owners, slots = idx.shape
+    owners, slots = idx.shape[0], 256
     at = lax.broadcasted_iota(i32, (1, samples), 1)
     owner_iota = lax.broadcasted_iota(i32, (owners, samples), 0)
     tri = one_hot(
@@ -91,7 +91,9 @@
         ]
         left = jnp.concatenate(parts, axis=0).astype(bf16)
         total = total + dot_nt(left, one_hot(slot_iota == rank))
-    idx[...] = (total[:owners] * 128.0 + total[owners : 2 * owners]).astype(i32)
+    found = (total[:owners] * 128.0 + total[owners : 2 * owners]).astype(i32)
+    idx[:, 0, :] = found[:, :128]
+    idx[:, 1, :] = found[:, 128:]
     row = (total[2 * owners : 3 * owners] - 1.0) * 128.0 + total[3 * owners :]
     row_a[...] = row[:, :128]
     row_b[...] = row[:, 128:]
@@ -166,7 +168,7 @@
 
     def pick(o, _):
         for k in range(slots):
-            src = idx[o, k]
+            src = idx[o, k // 128, k % 128]
             bucket[o, k : k + 1, :] = values[pl.ds(src, 1), :]
         bucket[o, slots : slots + 8, :] = jnp.zeros((8, emb), f32)
         bucket[o, slots : slots + 1, :] = row_a[pl.ds(o, 1), :]
@@ -671,26 +673,26 @@
     lax.fori_loop(0, some, prepare, 0)
     f_x.finish()
     f_z.start()
-    sums[4, 0].middle()
     seg_block(y_far)
     s_red[0].start()
     s_red[1].start()
     sums[0, 0].middle()
     sums[2, 0].middle()
+    sums[4, 0].middle()
+    seg_block(y_up)
     sums[1, 0].middle()
     sums[3, 0].middle()
     for p in (5, 6):
         copies[p].wait()
         sums[p, 1].start()
-    seg_block(y_up)
     f_z.finish()
     gath[me["x"], me["z"], core, me["y"]] = f_work[me["x"], me["z"]]
     g_z.start()
     seg_block(y_down)
     s_red[0].middle()
     s_red[1].middle()
+    seg_block(me["y"])
     done(4, 0)
-    seg_block(me["y"])
     done(0, 0)
     done(2, 0)
     done(1, 0)
@@ -823,10 +825,10 @@
             pltpu.VMEM((shards, capacity + 8, emb), f32),
             pltpu.VMEM((tables * shards, samples), bf16),
             pltpu.VMEM((tables * shards, samples), f32),
-            pltpu.VMEM((shards, 256), i32),
+            pltpu.VMEM((shards, 2, 128), i32),
             pltpu.VMEM((shards, 128), f32),
             pltpu.VMEM((shards, 128), f32),
-            pltpu.SMEM((shards, 256), i32),
+            pltpu.SMEM((shards, 2, 128), i32),
             pltpu.VMEM((samples, rank), f32),
             pltpu.VMEM((samples, rank), f32),
             pltpu.SemaphoreType.DMA((steps, 4)),

time: 129 us -> 127 us (0.984)
  Pallas kernels: 118 us -> 115 us
    pallas_call x1, Pallas kernels: 23.9 us -> 22.2 us  [body(): pl.pallas_call(functools.partial(front_kernel, f_count, owned), out_shape...]
  transfers between devices with their start and end apart: 1 -> 1, of which waited for: 1 -> 1; matrix products, arithmetic and copies ran while one was open for 0% -> 0% of each run, Pallas kernels for 34% -> 35%
where the time goes in v11:
time: 127 us; the launch traced here: 126 us
  Pallas kernels  115 us (91%)
  starting transfers between devices  9.5 us (7%)
    pallas_call x1, Pallas kernels, reduce_all(): pl.pallas_call(reduce_kernel, out_shape=tuple(shapes), in_specs=[anyw] *...  47 us
    pallas_call x1, Pallas kernels, body(): pl.pallas_call(functools.partial(weights_kernel, steps), grid=(steps,), o...  43.8 us
    pallas_call x1, Pallas kernels, body(): pl.pallas_call(functools.partial(front_kernel, f_count, owned), out_shape...  22.2 us
    all_to_all x1, starting transfers between devices, body(): lax.all_to_all(bucket, 'dp', split_axis=0, concat_axis=0, tiled=True)  9.5 us
  transfers between devices with their start and end apart: 1, of which 1 were waited for; matrix products, arithmetic and copies ran while one was open for 0% of the time, Pallas kernels for 35%

profile of v11, /device:TPU:1, one launch (start us, length us, event | category | flops | bytes accessed | tf_op | source)
XLA Modules:
  0.0 126.3 jit_solution(10828163772677121822)
XLA Ops:
  0.6 22.2 %front_kernel.1 = (bf16[512,512]{1,0:T(8,128)(2,1)}, bf16[512,512]{1,0:T(8,128)(2,1)}, f32[13824,128]{1,0:T(8,128)}, f32[32,216,128]{2,1,0:T(8,128)}) custom-call(s32[26,512]{1,0:T(8,128)} %bitcast.20, f32[3456]{0:T(1024)} %bias.1, bf16[512,3456]{1,0:T(8,128)(2,1)} %cross.1, bf16[512,3456]{1,0:T(8,128)(2,1)} %cot.1, bf16[3456,512]{1,0:T(8,128)(2,1)} %down_hbm.1, ...), custom_call_target="tpu_custom_call" | custom-call | tf_op jit(solution)/shard_map/front_kernel/pallas_call | solution.py:809
  22.8 9.5 %all-to-all-start = ((f32[32,216,128]{2,1,0:T(8,128)}), f32[32,216,128]{2,1,0:T(8,128)}, u32[]{:S(2)}, u32[]{:S(2)}) async-start(f32[32,216,128]{2,1,0:T(8,128)} %get-tuple-element.44), calls=%async_computation | async-start | bytes 7077888 | tf_op jit(solution)/shard_map/all_to_all | solution.py:843
  32.3 43.8 %weights_kernel.1 = (f32[16,4,32,128]{3,2,1,0:T(8,128)}, f32[16,4,24,128]{3,2,1,0:T(8,128)}, f32[16,4,32,128]{3,2,1,0:T(8,128)}, f32[16,4,32,128]{3,2,1,0:T(8,12...) custom-call(bf16[512,512]{1,0:T(8,128)(2,1)} %get-tuple-element.33.hid, ...), custom_call_target="tpu_custom_call" | custom-call | tf_op jit(solution)/shard_map/weights_kernel/pallas_call | solution.py:845
  76.1 0.6 all-to-all-done.refs_8_
  76.7 47.0 %reduce_kernel.1 = (f32[1024,128]{1,0:T(8,128)}, f32[8,128]{1,0:T(8,128)}, f32[2048,128]{1,0:T(8,128)}, f32[16,128]{1,0:T(8,128)}, f32[4,3456]{1,0:T(4,128)}, /*index=5*/f32[27,512]{1,0:T(8,128)}, f32[1,27]{1,0:T(1,128)}) custom-call(f32[4,4,4,32,128]{4,3,2,1,0:T(8,128)} %bitcast.14, f32[4,4,4,24,128]{4,3,2,1,0:T(8,128)} %bitcast.18, ...), custom_call_target="tpu_custom_call" | custom-call | tf_op jit(solution)/shard_map/reduce_kernel/pallas_call | solution.py:771
  123.6 2.5 %move_kernel.1 = (f32[1024,128]{1,0:T(8,128)}, f32[8,128]{1,0:T(8,128)}, f32[2048,128]{1,0:T(8,128)}, f32[16,128]{1,0:T(8,128)}, f32[4,3456]{1,0:T(4,128)}, /*index=5*/f32[27,512]{1,0:T(8,128)}, f32[1,27]{1,0:T(1,128)}) custom-call(f32[1024,128]{1,0:T(8,128)} %get-tuple-element.45.refs_0_, f32[8,128]{1,0:T(8,128)} %get-tuple-element.46.refs_1_, ...), custom_call_target="tpu_custom_call" | custom-call | tf_op jit(solution)/shard_map/move_kernel/pallas_call | solution.py:780
Async XLA Ops:
  22.8 53.9 %all-to-all-start = ((f32[32,216,128]{2,1,0:T(8,128)}), f32[32,216,128]{2,1,0:T(8,128)}, u32[]{:S(2)}, u32[]{:S(2)}) async-start(f32[32,216,128]{2,1,0:T(8,128)} %get-tuple-element.44), calls=%async_computation | async-start | bytes 7077888 | tf_op jit(solution)/shard_map/all_to_all | solution.py:843

commit v12 on v11

--- a/solution.py
+++ b/solution.py
@@ -692,17 +692,17 @@
     s_red[0].middle()
     s_red[1].middle()
     seg_block(me["y"])
-    done(4, 0)
     done(0, 0)
     done(2, 0)
+    s_red[0].finish()
+    s_gat[0].start()
     done(1, 0)
     done(3, 0)
+    s_red[1].finish()
+    s_gat[1].start()
+    done(4, 0)
     sums[5, 1].middle()
     sums[6, 1].middle()
-    s_red[0].finish()
-    s_gat[0].start()
-    s_red[1].finish()
-    s_gat[1].start()
     g_z.finish()
     g_x.start()
     for p in (4, 0, 2, 1, 3):

time: 127 us -> 126 us (level)
  no operation moved by 1% of the time
where the time goes in v12:
time: 126 us
  Pallas kernels  115 us (91%)
  starting transfers between devices  9.5 us (8%)
    pallas_call x1, Pallas kernels, reduce_all(): pl.pallas_call(reduce_kernel, out_shape=tuple(shapes), in_specs=[anyw] *...  46.3 us
    pallas_call x1, Pallas kernels, body(): pl.pallas_call(functools.partial(weights_kernel, steps), grid=(steps,), o...  43.8 us
    pallas_call x1, Pallas kernels, body(): pl.pallas_call(functools.partial(front_kernel, f_count, owned), out_shape...  22.2 us
    all_to_all x1, starting transfers between devices, body(): lax.all_to_all(bucket, 'dp', split_axis=0, concat_axis=0, tiled=True)  9.5 us
  transfers between devices with their start and end apart: 1, of which 1 were waited for; matrix products, arithmetic and copies ran while one was open for 0% of the time, Pallas kernels for 35%

profile of v12, /device:TPU:1, one launch (start us, length us, event | category | flops | bytes accessed | tf_op | source)
XLA Modules:
  0.0 125.6 jit_solution(989321813211554671)
XLA Ops:
  0.6 22.2 %front_kernel.1 = (bf16[512,512]{1,0:T(8,128)(2,1)}, bf16[512,512]{1,0:T(8,128)(2,1)}, f32[13824,128]{1,0:T(8,128)}, f32[32,216,128]{2,1,0:T(8,128)}) custom-call(s32[26,512]{1,0:T(8,128)} %bitcast.20, f32[3456]{0:T(1024)} %bias.1, bf16[512,3456]{1,0:T(8,128)(2,1)} %cross.1, bf16[512,3456]{1,0:T(8,128)(2,1)} %cot.1, bf16[3456,512]{1,0:T(8,128)(2,1)} %down_hbm.1, ...), custom_call_target="tpu_custom_call" | custom-call | tf_op jit(solution)/shard_map/front_kernel/pallas_call | solution.py:809
  22.8 9.5 %all-to-all-start = ((f32[32,216,128]{2,1,0:T(8,128)}), f32[32,216,128]{2,1,0:T(8,128)}, u32[]{:S(2)}, u32[]{:S(2)}) async-start(f32[32,216,128]{2,1,0:T(8,128)} %get-tuple-element.44), calls=%async_computation | async-start | bytes 7077888 | tf_op jit(solution)/shard_map/all_to_all | solution.py:843
  32.3 43.8 %weights_kernel.1 = (f32[16,4,32,128]{3,2,1,0:T(8,128)}, f32[16,4,24,128]{3,2,1,0:T(8,128)}, f32[16,4,32,128]{3,2,1,0:T(8,128)}, f32[16,4,32,128]{3,2,1,0:T(8,12...) custom-call(bf16[512,512]{1,0:T(8,128)(2,1)} %get-tuple-element.33.hid, ...), custom_call_target="tpu_custom_call" | custom-call | tf_op jit(solution)/shard_map/weights_kernel/pallas_call | solution.py:845
  76.1 0.6 all-to-all-done.refs_8_
  76.7 46.3 %reduce_kernel.1 = (f32[1024,128]{1,0:T(8,128)}, f32[8,128]{1,0:T(8,128)}, f32[2048,128]{1,0:T(8,128)}, f32[16,128]{1,0:T(8,128)}, f32[4,3456]{1,0:T(4,128)}, /*index=5*/f32[27,512]{1,0:T(8,128)}, f32[1,27]{1,0:T(1,128)}) custom-call(f32[4,4,4,32,128]{4,3,2,1,0:T(8,128)} %bitcast.14, f32[4,4,4,24,128]{4,3,2,1,0:T(8,128)} %bitcast.18, ...), custom_call_target="tpu_custom_call" | custom-call | tf_op jit(solution)/shard_map/reduce_kernel/pallas_call | solution.py:771
  123.0 2.5 %move_kernel.1 = (f32[1024,128]{1,0:T(8,128)}, f32[8,128]{1,0:T(8,128)}, f32[2048,128]{1,0:T(8,128)}, f32[16,128]{1,0:T(8,128)}, f32[4,3456]{1,0:T(4,128)}, /*index=5*/f32[27,512]{1,0:T(8,128)}, f32[1,27]{1,0:T(1,128)}) custom-call(f32[1024,128]{1,0:T(8,128)} %get-tuple-element.45.refs_0_, f32[8,128]{1,0:T(8,128)} %get-tuple-element.46.refs_1_, ...), custom_call_target="tpu_custom_call" | custom-call | tf_op jit(solution)/shard_map/move_kernel/pallas_call | solution.py:780
Async XLA Ops:
  22.8 53.9 %all-to-all-start = ((f32[32,216,128]{2,1,0:T(8,128)}), f32[32,216,128]{2,1,0:T(8,128)}, u32[]{:S(2)}, u32[]{:S(2)}) async-start(f32[32,216,128]{2,1,0:T(8,128)} %get-tuple-element.44), calls=%async_computation | async-start | bytes 7077888 | tf_op jit(solution)/shard_map/all_to_all | solution.py:843
